TPU v7x, 32 devices: a whole 2x2x4 slice. The times are simulated.
32 devices in a mesh: dp: 8 (over y, x, core), tensor: 4 (over z).
Axes of the slice: x: 2, y: 2, z: 4, core: 2. Of those that a mesh axis runs over, the one named last changes fastest.
Arguments:
- tokens: bfloat16 [4096, 768], P('dp'), may hold values from -6 to 6
- lengths: int32 [8, 16], P('dp'), may hold values from 0 to 512, as said below
- w_query: bfloat16 [768, 768], P(None, 'tensor'), may hold values from -0.21875 to 0.21875
- w_key: bfloat16 [768, 768], P(None, 'tensor'), may hold values from -0.21875 to 0.21875
- w_value: bfloat16 [768, 768], P(None, 'tensor'), may hold values from -0.21875 to 0.21875
- b_query: float32 [768], P('tensor'), may hold values from -3 to 3
- b_value: float32 [768], P('tensor'), may hold values from -3 to 3
- w_out: bfloat16 [768, 768], P('tensor'), may hold values from -0.625 to 0.625
- b_out: float32 [768], replicated, may hold values from -3 to 3
- g_attn: float32 [768], replicated, may hold values from 0.5 to 1.5
- b_attn: float32 [768], replicated, may hold values from -3 to 3
- w_up: bfloat16 [768, 3072], P(None, 'tensor'), may hold values from -0.21875 to 0.21875
- b_up: float32 [3072], P('tensor'), may hold values from -3 to 3
- w_down: bfloat16 [3072, 768], P('tensor'), may hold values from -0.109375 to 0.109375
- b_down: float32 [768], replicated, may hold values from -3 to 3
- g_ffn: float32 [768], replicated, may hold values from 0.5 to 1.5
- b_ffn: float32 [768], replicated, may hold values from -3 to 3
- out_grad: bfloat16 [4096, 768], P('dp'), may hold values from -6 to 6
- pool_grad: float32 [128, 1728], P('dp'), may hold values from -6 to 6
Outputs:
- layer_out: bfloat16 [4096, 768], P('dp')
- pools: float32 [128, 1728], replicated
- d_tokens: float32 [4096, 768], P('dp')
- d_w_query: float32 [768, 768], P(None, 'tensor')
- d_w_key: float32 [768, 768], P(None, 'tensor')
- d_w_value: float32 [768, 768], P(None, 'tensor')
- d_b_query: float32 [768], P('tensor')
- d_b_value: float32 [768], P('tensor')
- d_w_out: float32 [768, 768], P('tensor')
- d_b_out: float32 [768], replicated
- d_g_attn: float32 [768], replicated
- d_b_attn: float32 [768], replicated
- d_w_up: float32 [768, 3072], P(None, 'tensor')
- d_b_up: float32 [3072], P('tensor')
- d_w_down: float32 [3072, 768], P('tensor')
- d_b_down: float32 [768], replicated
- d_g_ffn: float32 [768], replicated
- d_b_ffn: float32 [768], replicated
Inputs may be any that keep to these rules, and one draw needn't show every extreme that they name: In each bucket the nonzero lengths come first and add up to at most 512; the first is nonzero; in every draw some bucket holds one sentence of exactly 512 tokens.
All inputs are finite; a program needn't handle non-finite values.
Results may differ from a plain program's by a relative error of at most 0.013.
Values sent between devices are 32-bit elements; how exact they have to be, the bound alone decides.
No kernel may reach another device: no remote copies, remote signals or barrier semaphores. Data moves between devices by JAX's collectives and lax.ppermute only.
A program may use at most 128 MiB of HBM per device.

v0:
```python
import jax
import jax.numpy as jnp
from jax import lax
from jax.sharding import PartitionSpec as P

HDIM = 64
SENTS = 16


norm_eps = 1e-06
pool_eps = 1e-05
highest = lax.Precision.HIGHEST


def truncations(width):
    return [width, width * 2 // 3, width // 3, width // 6, width // 12]


def segment_ids(sizes, slot_count):
    ends = jnp.cumsum(sizes, dtype=jnp.int32)
    places = jnp.arange(slot_count, dtype=jnp.int32)
    return jnp.sum((places[:, None] >= ends[None, :]).astype(jnp.int32), axis=1)


def norm_stats(rows):
    centre = jnp.mean(rows, axis=-1, keepdims=True)
    shifted = rows - centre
    inverse = lax.rsqrt(jnp.mean(shifted * shifted, axis=-1, keepdims=True) + norm_eps)
    return (shifted * inverse, inverse)


def norm_back(grad_in, normal, inverse):
    centre = jnp.mean(grad_in, axis=-1, keepdims=True)
    along = jnp.mean(grad_in * normal, axis=-1, keepdims=True)
    return inverse * (grad_in - centre - normal * along)


def gelu_exact(upper):
    return jax.nn.gelu(upper, approximate=False)


def attention_scores(query_heads, key_heads, allowed, score_scale):
    scores = (
        jnp.einsum("qhd,khd->hqk", query_heads, key_heads, preferred_element_type=jnp.float32)
        * score_scale
    )
    return jnp.where(allowed[None], scores, -1000000000.0)


def shards(
    tokens,
    lengths,
    w_query,
    w_key,
    w_value,
    b_query,
    b_value,
    w_out,
    b_out,
    g_attn,
    b_attn,
    w_up,
    b_up,
    w_down,
    b_down,
    g_ffn,
    b_ffn,
    out_grad,
    pool_grad,
):
    slot_count = tokens.shape[0]
    model_width = tokens.shape[1]
    local_cols = w_query.shape[1]
    head_count = local_cols // HDIM
    score_scale = HDIM ** (-0.5)
    segment = segment_ids(lengths[0], slot_count)
    allowed = segment[:, None] == segment[None, :]
    inputs = tokens.astype(jnp.float32)
    query_rows = (jnp.dot(tokens, w_query, preferred_element_type=jnp.float32) + b_query).astype(
        jnp.bfloat16
    )
    key_rows = jnp.dot(tokens, w_key, preferred_element_type=jnp.float32).astype(jnp.bfloat16)
    value_rows = (jnp.dot(tokens, w_value, preferred_element_type=jnp.float32) + b_value).astype(
        jnp.bfloat16
    )
    query_heads = query_rows.reshape(slot_count, head_count, HDIM)
    key_heads = key_rows.reshape(slot_count, head_count, HDIM)
    value_heads = value_rows.reshape(slot_count, head_count, HDIM)
    scores = attention_scores(query_heads, key_heads, allowed, score_scale)
    top_score = jnp.max(scores, axis=-1, keepdims=True)
    log_total = top_score + jnp.log(jnp.sum(jnp.exp(scores - top_score), axis=-1, keepdims=True))
    probs_low = jnp.exp(scores - log_total).astype(jnp.bfloat16)
    mixed = jnp.einsum("hqk,khd->qhd", probs_low, value_heads, preferred_element_type=jnp.float32)
    mixed = mixed.reshape(slot_count, local_cols).astype(jnp.bfloat16)
    partial_value = jnp.dot(mixed, w_out, preferred_element_type=jnp.float32)
    attn_total = lax.psum(partial_value, "tensor")
    normal_attn, inverse_attn = norm_stats(inputs + attn_total + b_out)
    normed = normal_attn * g_attn + b_attn
    normed_low = normed.astype(jnp.bfloat16)
    upper = jnp.dot(normed_low, w_up, preferred_element_type=jnp.float32) + b_up
    act_rows = gelu_exact(upper).astype(jnp.bfloat16)
    down_total = lax.psum(jnp.dot(act_rows, w_down, preferred_element_type=jnp.float32), "tensor")
    normal_ffn, inverse_ffn = norm_stats(normed + down_total + b_down)
    final = normal_ffn * g_ffn + b_ffn
    layer_out = final.astype(jnp.bfloat16)
    sentence = jnp.arange(SENTS, dtype=jnp.int32)
    member = (segment[None, :] == sentence[:, None]).astype(jnp.float32)
    denom = jnp.maximum(lengths[0], 1).astype(jnp.float32)[:, None]
    pooled = jnp.dot(member, final, precision=highest, preferred_element_type=jnp.float32) / denom
    pieces = []
    factors = []
    for keep_width in truncations(model_width):
        leading = pooled[:, :keep_width]
        factor = lax.rsqrt(jnp.mean(leading * leading, axis=1, keepdims=True) + pool_eps)
        pieces.append(leading * factor)
        factors.append(factor)
    pools = lax.all_gather(jnp.concatenate(pieces, axis=1), "dp", axis=0, tiled=True)
    d_pooled = jnp.zeros_like(pooled)
    offset = 0
    for keep_width, factor in zip(truncations(model_width), factors):
        leading = pooled[:, :keep_width]
        upstream = pool_grad[:, offset : offset + keep_width]
        inner = jnp.mean(upstream * leading, axis=1, keepdims=True)
        d_pooled = d_pooled.at[:, :keep_width].add(factor * upstream - leading * factor**3 * inner)
        offset = offset + keep_width
    spread_back = jnp.einsum(
        "st,sd->td", member, d_pooled / denom, precision=highest, preferred_element_type=jnp.float32
    )
    d_final = out_grad.astype(jnp.float32) + spread_back
    g_ffn_part = jnp.sum(d_final * normal_ffn, axis=0)
    b_ffn_part = jnp.sum(d_final, axis=0)
    d_resid = norm_back(d_final * g_ffn, normal_ffn, inverse_ffn)
    b_down_part = jnp.sum(d_resid, axis=0)
    resid_low = d_resid.astype(jnp.bfloat16)
    w_down_part = jnp.einsum("tf,td->fd", act_rows, resid_low, preferred_element_type=jnp.float32)
    d_act = jnp.einsum("td,fd->tf", resid_low, w_down, preferred_element_type=jnp.float32)
    d_upper = jax.vjp(gelu_exact, upper)[1](d_act)[0]
    b_up_part = jnp.sum(d_upper, axis=0)
    upper_low = d_upper.astype(jnp.bfloat16)
    w_up_part = jnp.einsum("td,tf->df", normed_low, upper_low, preferred_element_type=jnp.float32)
    normed_term = jnp.einsum("tf,df->td", upper_low, w_up, preferred_element_type=jnp.float32)
    d_normed = d_resid + lax.psum(normed_term, "tensor")
    g_attn_part = jnp.sum(d_normed * normal_attn, axis=0)
    b_attn_part = jnp.sum(d_normed, axis=0)
    d_hidden = norm_back(d_normed * g_attn, normal_attn, inverse_attn)
    b_out_part = jnp.sum(d_hidden, axis=0)
    hidden_low = d_hidden.astype(jnp.bfloat16)
    w_out_part = jnp.einsum("tc,td->cd", mixed, hidden_low, preferred_element_type=jnp.float32)
    d_mixed = jnp.einsum("td,cd->tc", hidden_low, w_out, preferred_element_type=jnp.float32)
    d_mixed = d_mixed.astype(jnp.bfloat16).reshape(slot_count, head_count, HDIM)
    scores_again = attention_scores(query_heads, key_heads, allowed, score_scale)
    probs = jnp.exp(scores_again - log_total)
    probs_again = probs.astype(jnp.bfloat16)
    d_probs = jnp.einsum("qhd,khd->hqk", d_mixed, value_heads, preferred_element_type=jnp.float32)
    row_inner = jnp.sum(probs * d_probs, axis=-1, keepdims=True)
    d_scores = (probs * (d_probs - row_inner) * score_scale).astype(jnp.bfloat16)
    d_query = jnp.einsum(
        "hqk,khd->qhd", d_scores, key_heads, preferred_element_type=jnp.float32
    ).reshape(slot_count, local_cols)
    d_key = jnp.einsum(
        "hqk,qhd->khd", d_scores, query_heads, preferred_element_type=jnp.float32
    ).reshape(slot_count, local_cols)
    d_value = jnp.einsum(
        "hqk,qhd->khd", probs_again, d_mixed, preferred_element_type=jnp.float32
    ).reshape(slot_count, local_cols)
    b_query_part = jnp.sum(d_query, axis=0)
    b_value_part = jnp.sum(d_value, axis=0)
    query_low = d_query.astype(jnp.bfloat16)
    key_low = d_key.astype(jnp.bfloat16)
    value_low = d_value.astype(jnp.bfloat16)
    w_query_part = jnp.einsum("td,tc->dc", tokens, query_low, preferred_element_type=jnp.float32)
    w_key_part = jnp.einsum("td,tc->dc", tokens, key_low, preferred_element_type=jnp.float32)
    w_value_part = jnp.einsum("td,tc->dc", tokens, value_low, preferred_element_type=jnp.float32)
    input_term = jnp.einsum("tc,dc->td", query_low, w_query, preferred_element_type=jnp.float32)
    input_term = input_term + jnp.einsum(
        "tc,dc->td", key_low, w_key, preferred_element_type=jnp.float32
    )
    input_term = input_term + jnp.einsum(
        "tc,dc->td", value_low, w_value, preferred_element_type=jnp.float32
    )
    d_tokens = d_hidden + lax.psum(input_term, "tensor")
    grad_sums = lax.psum(
        (
            w_query_part,
            w_key_part,
            w_value_part,
            b_query_part,
            b_value_part,
            w_out_part,
            b_out_part,
            g_attn_part,
            b_attn_part,
            w_up_part,
            b_up_part,
            w_down_part,
            b_down_part,
            g_ffn_part,
            b_ffn_part,
        ),
        "dp",
    )
    (
        d_w_query,
        d_w_key,
        d_w_value,
        d_b_query,
        d_b_value,
        d_w_out,
        d_b_out,
        d_g_attn,
        d_b_attn,
        d_w_up,
        d_b_up,
        d_w_down,
        d_b_down,
        d_g_ffn,
        d_b_ffn,
    ) = grad_sums
    return (
        layer_out,
        pools,
        d_tokens,
        d_w_query,
        d_w_key,
        d_w_value,
        d_b_query,
        d_b_value,
        d_w_out,
        d_b_out,
        d_g_attn,
        d_b_attn,
        d_w_up,
        d_b_up,
        d_w_down,
        d_b_down,
        d_g_ffn,
        d_b_ffn,
    )


def solution(mesh):
    return jax.shard_map(
        shards,
        mesh=mesh,
        in_specs=(
            P("dp", None),
            P("dp", None),
            P(None, "tensor"),
            P(None, "tensor"),
            P(None, "tensor"),
            P("tensor"),
            P("tensor"),
            P("tensor", None),
            P(),
            P(),
            P(),
            P(None, "tensor"),
            P("tensor"),
            P("tensor", None),
            P(),
            P(),
            P(),
            P("dp", None),
            P("dp", None),
        ),
        out_specs=(
            P("dp", None),
            P(),
            P("dp", None),
            P(None, "tensor"),
            P(None, "tensor"),
            P(None, "tensor"),
            P("tensor"),
            P("tensor"),
            P("tensor", None),
            P(),
            P(),
            P(),
            P(None, "tensor"),
            P("tensor"),
            P("tensor", None),
            P(),
            P(),
            P(),
        ),
        check_vma=False,
    )
```

profile of v0, /device:TPU:0, one launch (start us, length us, event | category | flops | bytes accessed | tf_op | source)
XLA Modules:
  0.0 486.1 jit_solution(11460330406638272772)
XLA Ops:
  8.6 1.7 convolution_convert_fusion.2
  16.0 71.8 %all-reduce.8.cloned.1.call-done = f32[512,768]{1,0:T(8,128)} async-done(((f32[512,768]{1,0:T(8,128)}), f32[512,768]{1,0:T(8,128)}) %all-reduce.8.cloned.1.call-update) | async-done | bytes 1572880 | tf_op jit(solution)/shard_map/psum | solution.py:96
  87.7 1.7 fusion.64
  90.2 5.4 %multiply_convert_fusion.1 = (bf16[512,768]{1,0:T(8,128)(2,1)S(1)}, f32[512,768]{1,0:T(8,128)}, f32[512,768]{1,0:T(8,128)}) fusion(f32[768]{0:T(1024)S(1)} %copy-done.59, bf16[768,768]{1,0:T(8,128)(2,1)S(1)} %copy-done, f32[512,768]{1,0:T(8,128)S(1)} %get-tuple-element.189, f32[768]{0:T(1024)S(1)} %copy-done.53, f32[768]{0:T(1024)S(1)} %copy-done.35, ...), kind=kOutput, calls=%fused_computation.24 | convolution fusion | flops 631898112 | bytes 6697984 | tf_op jit(solution)/shard_map/dot_general | solution.py:100
  96.4 1.9 fusion.71
  101.0 65.6 %all-reduce.10.cloned.1.call-done = f32[512,768]{1,0:T(8,128)} async-done(((f32[512,768]{1,0:T(8,128)}), f32[512,768]{1,0:T(8,128)}) %all-reduce.10.cloned.1.call-update) | async-done | bytes 1572880 | tf_op jit(solution)/shard_map/psum | solution.py:102
  166.7 2.0 fusion.62
  177.0 3.9 multiply_reduce_fusion.1
  183.5 1.8 fusion.69
  186.2 2.0 fusion.42
  188.4 68.0 %all-reduce.12.cloned.1.call-done = f32[512,768]{1,0:T(8,128)} async-done(((f32[512,768]{1,0:T(8,128)}), f32[512,768]{1,0:T(8,128)}) %all-reduce.12.cloned.1.call-update) | async-done | bytes 1572880 | tf_op jit(solution)/shard_map/psum | solution.py:142
  256.4 3.3 multiply_reduce_fusion.2
  262.5 2.3 fusion.72
  264.8 7.5 %fusion.66 = (f32[3,64]{1,0:T(4,128)}, bf16[512,3,64]{0,2,1:T(8,128)(2,1)S(1)}) fusion(bf16[512,3,64]{0,2,1:T(8,128)(2,1)S(1)} %bitcast.68, f32[3,512,512]{1,2,0:T(8,128)} %fusion.72, f32[3,512]{1,0:T(4,128)S(1)} %copy-done.44, f32[3,512,512]{1,2,0:T(8,128)} %copy-done.8, pred[512,512]{0,1:T(8,128)(4,1)S(1)} %copy-done.12), kind=kOutput, calls=%fused_computation.151 | convolution fusion | flops 109512512 | bytes 6953728 | tf_op jit(solution)/shard_map/hqk,khd->qhd/dot_general | solution.py:157
  272.3 6.9 %fusion.27 = bf16[3,64,512]{2,1,0:T(8,128)(2,1)S(1)} fusion(bf16[512,3,64]{0,2,1:T(8,128)(2,1)} %bitcast.78, f32[3,512,512]{1,2,0:T(8,128)} %fusion.72, f32[3,512,512]{1,2,0:T(8,128)} %copy-done.8, f32[3,512]{1,0:T(4,128)S(1)} %copy-done.44, pred[512,512]{0,1:T(8,128)(4,1)S(1)} %copy-done.12), kind=kOutput, calls=%fused_computation.60 | convolution fusion | flops 109414400 | bytes 6952960 | tf_op jit(solution)/shard_map/hqk,qhd->khd/dot_general | solution.py:160
  279.3 3.6 fusion.65
  285.9 3.9 fusion.44
  289.8 2.4 fusion.40
  297.7 10.6 %all_gather.3 = f32[128,1728]{1,0:T(8,128)S(1)} all-gather(f32[16,1728]{1,0:T(8,128)S(1)} %copy-done.30), channel_id=1, replica_groups=mesh['dp'=8,'tensor'=4] {'dp'}, dimensions={0}, use_global_device_ids=true | all-gather | bytes 995328 | tf_op jit(solution)/shard_map/all_gather | solution.py:117
  309.7 25.0 %all-reduce = (f32[192]{0:T(256)}, f32[192]{0:T(256)}, f32[768]{0:T(1024)}, f32[768]{0:T(1024)}, f32[768]{0:T(1024)}, /*index=5*/f32[768]{0:T(1024)}, f32[768]{0:T(1024)}, f32[768]{0:T(1024)}, f32[768]{0:T(1024)}) all-reduce(f32[192]{0:T(256)S(1)} %reduce_sum.296, ...), channel_id=1, replica_groups=mesh['dp'=8,'tensor'=4] {'dp'}, use_global_device_ids=true, to_apply=%region_35.36 | all-reduce | flops 5760 | bytes 46080 | tf_op jit(solution)/shard_map/psum | solution.py:182
  334.7 19.3 %all-reduce.14.cloned.1.call-done = f32[512,768]{1,0:T(8,128)} async-done(((f32[512,768]{1,0:T(8,128)}), f32[512,768]{1,0:T(8,128)}) %all-reduce.14.cloned.1.call-update) | async-done | bytes 1572880 | tf_op jit(solution)/shard_map/psum | solution.py:181
  354.1 2.7 add.261
  356.8 114.3 %all-reduce.16.cloned.1.call-done = (f32[768,192]{0,1:T(8,128)}, f32[768,192]{0,1:T(8,128)}, f32[768,192]{0,1:T(8,128)}, f32[192,768]{1,0:T(8,128)}, f32[768,768]{1,0:T(8,128)}, /*index=5*/f32[768,768]{1,0:T(8,128)}) async-done(((f32[768,192]{0,1:T(8,128)}, f32[768,192]{0,1:T(8,128)}, f32[768,192]{0,1:T(8,128)}, f32[192,768]{1,0:T(8,128)}, f32[768,768]{1,0:T(8,128)}, /*index=5*/f32[768,768]{1,0:T(8,128)}), ...) | async-done | bytes 7077904 | tf_op jit(solution)/shard_map/psum | solution.py:182
  471.1 2.0 copy.77
  (203 shorter events, 41.8 us)
Async XLA Ops:
  7.2 82.6 %copy-start = (bf16[768,768]{1,0:T(8,128)(2,1)S(1)}, bf16[768,768]{1,0:T(8,128)(2,1)}, u32[]{:S(2)}) copy-start(bf16[768,768]{1,0:T(8,128)(2,1)} %param.42) | copy-start | bytes 3538948
  7.2 80.5 %all-reduce.8.cloned.1.call-start = ((), (), s32[]{:S(2)}) async-start(), calls=%async_computation | async-start | bytes 3145728 | tf_op jit(solution)/shard_map/psum | solution.py:96
  8.6 4.6 copy-start.11
  14.3 73.4 %copy-start.52 = (f32[768]{0:T(1024)S(1)}, f32[768]{0:T(1024)}, u32[]{:S(2)}) copy-start(f32[768]{0:T(1024)} %param.39) | copy-start | bytes 9220
  15.9 150.8 %all-reduce.10.cloned.1.call-start = ((), (), s32[]{:S(2)}) async-start(), calls=%async_computation.1 | async-start | bytes 3145728 | tf_op jit(solution)/shard_map/psum | solution.py:102
  90.1 6.3 %copy-start.57 = (bf16[768,768]{1,0:T(8,128)(2,1)S(1)}, bf16[768,768]{1,0:T(8,128)(2,1)}, u32[]{:S(2)}) copy-start(bf16[768,768]{1,0:T(8,128)(2,1)} %param.44) | copy-start | bytes 3538948
  98.4 158.1 %all-reduce.12.cloned.1.call-start = ((), (), s32[]{:S(2)}) async-start(), calls=%async_computation.2 | async-start | bytes 3145728 | tf_op jit(solution)/shard_map/psum | solution.py:142
  169.7 5.9 %copy-start.41 = (f32[512]{0:T(512)}, f32[512]{0:T(512)S(1)}, u32[]{:S(2)}) copy-start(f32[512]{0:T(512)S(1)} %add_rsqrt_fusion) | copy-start | bytes 6148
  176.9 4.0 copy-start.6
  176.9 4.0 copy-start.37
  176.9 4.0 copy-start.42
  176.9 4.0 copy-start.46
  176.9 4.0 copy-start.48
  188.2 165.9 %all-reduce.14.cloned.1.call-start = ((), (), s32[]{:S(2)}) async-start(), calls=%async_computation.3 | async-start | bytes 3145728 | tf_op jit(solution)/shard_map/psum | solution.py:181
  285.8 4.0 copy-start.54
  285.8 185.3 %all-reduce.16.cloned.1.call-start = ((), (), s32[]{:S(2)}) async-start(), calls=%async_computation.4 | async-start | bytes 14155776 | tf_op jit(solution)/shard_map/psum | solution.py:182
  296.8 12.7 %copy-start.55 = (f32[3,64]{1,0:T(4,128)S(1)}, f32[3,64]{1,0:T(4,128)}, u32[]{:S(2)}) copy-start(f32[3,64]{1,0:T(4,128)} %get-tuple-element.193) | copy-start | bytes 2308
  296.8 12.8 %copy-start.56 = (f32[3,64]{1,0:T(4,128)S(1)}, f32[3,64]{1,0:T(4,128)}, u32[]{:S(2)}) copy-start(f32[3,64]{1,0:T(4,128)} %get-tuple-element.191) | copy-start | bytes 2308
  296.9 12.9 %copy-start.38 = (f32[768]{0:T(1024)S(1)}, f32[768]{0:T(1024)}, u32[]{:S(2)}) copy-start(f32[768]{0:T(1024)} %get-tuple-element.175) | copy-start | bytes 9220
  296.9 12.8 %copy-start.39 = (f32[768]{0:T(1024)S(1)}, f32[768]{0:T(1024)}, u32[]{:S(2)}) copy-start(f32[768]{0:T(1024)} %get-tuple-element.142) | copy-start | bytes 9220
  296.9 12.8 %copy-start.40 = (f32[768]{0:T(1024)S(1)}, f32[768]{0:T(1024)}, u32[]{:S(2)}) copy-start(f32[768]{0:T(1024)} %get-tuple-element.147) | copy-start | bytes 9220
  296.9 12.8 %copy-start.49 = (f32[768]{0:T(1024)S(1)}, f32[768]{0:T(1024)}, u32[]{:S(2)}) copy-start(f32[768]{0:T(1024)} %get-tuple-element.140) | copy-start | bytes 9220
  296.9 12.8 %copy-start.50 = (f32[768]{0:T(1024)S(1)}, f32[768]{0:T(1024)}, u32[]{:S(2)}) copy-start(f32[768]{0:T(1024)} %get-tuple-element.146) | copy-start | bytes 9220
  296.9 12.8 %copy-start.51 = (f32[768]{0:T(1024)S(1)}, f32[768]{0:T(1024)}, u32[]{:S(2)}) copy-start(f32[768]{0:T(1024)} %get-tuple-element.219) | copy-start | bytes 9220
  (48 other events, 89.0 us)
Sparse Core Ops, SparseCore 0:
  16.0 71.6 all-reduce.7
  98.5 68.1 all-reduce.9
  188.3 68.1 all-reduce.11
  285.9 68.0 all-reduce.13
  359.1 111.9 all-reduce.15
where the time goes:
time: 487 us; the launch traced here: 486 us
  waiting for transfers between devices  339 us (70%)
  matrix products  55.8 us (11%)
  blocking collectives  35.6 us (7%)
  other arithmetic  20.7 us (4%)
  local copies, waits for them, and re-layouts  19.7 us (4%)
  between operations  14.5 us (3%)
    psum x1, waiting for transfers between devices, shards(): lax.psum((w_query_part, w_key_part, w_value_part, b_query_part, b_value_p...  114 us
    psum x1, waiting for transfers between devices, shards(): attn_total = lax.psum(partial_value, 'tensor')  71.8 us
    psum x1, waiting for transfers between devices, shards(): d_normed = d_resid + lax.psum(normed_term, 'tensor')  68 us
    psum x1, waiting for transfers between devices, shards(): lax.psum(jnp.dot(act_rows, w_down, preferred_element_type=jnp.float32), '...  65.6 us
    psum x1, blocking collectives, shards(): lax.psum((w_query_part, w_key_part, w_value_part, b_query_part, b_value_p...  25 us
    psum x1, waiting for transfers between devices, shards(): d_tokens = d_hidden + lax.psum(input_term, 'tensor')  19.3 us
    unnamed x141, local copies, waits for them, and re-layouts  17.3 us
    all_gather x1, blocking collectives, shards(): lax.all_gather(jnp.concatenate(pieces, axis=1), 'dp', axis=0, tiled=True)  10.6 us
  transfers between devices with their start and end apart: 5, of which 5 were waited for; matrix products, arithmetic and copies ran while one was open for 4% of the time, Pallas kernels for 0%

commit v1 on v0

v1 whole, which is shorter than its diff:
```python
import functools

import jax
import jax.numpy as jnp
from jax import lax
from jax.experimental import pallas as pl
from jax.experimental.pallas import tpu as pltpu
from jax.sharding import PartitionSpec as P

HDIM = 64
SENTS = 16
norm_eps = 1e-06
pool_eps = 1e-05
highest = lax.Precision.HIGHEST
f32 = jnp.float32
bf16 = jnp.bfloat16
swaps = {k: [(i, i ^ k) for i in range(4)] for k in (1, 2, 3)}


def truncations(width):
    return [width, width * 2 // 3, width // 3, width // 6, width // 12]


def nn(left, right, precision=None):
    return lax.dot_general(
        left, right, (((1,), (0,)), ((), ())), precision=precision, preferred_element_type=f32
    )


def nt(left, right):
    return lax.dot_general(left, right, (((1,), (1,)), ((), ())), preferred_element_type=f32)


def tn(left, right):
    return lax.dot_general(left, right, (((0,), (0,)), ((), ())), preferred_element_type=f32)


def norm_stats(rows):
    centre = jnp.mean(rows, axis=-1, keepdims=True)
    shifted = rows - centre
    inverse = lax.rsqrt(jnp.mean(shifted * shifted, axis=-1, keepdims=True) + norm_eps)
    return shifted * inverse, inverse


def norm_back(grad_in, normal, inverse):
    centre = jnp.mean(grad_in, axis=-1, keepdims=True)
    along = jnp.mean(grad_in * normal, axis=-1, keepdims=True)
    return inverse * (grad_in - centre - normal * along)


def col_sum(rows):
    return jnp.sum(rows, axis=0, keepdims=True)


def shape(*extent, kind=f32):
    return jax.ShapeDtypeStruct(extent, kind)


def call(body, outs, ins, flops=0, moved=0, scratch=(), limit=32):
    specs = [
        pl.BlockSpec(memory_space=pltpu.SMEM if item.dtype == jnp.int32 else pltpu.VMEM)
        for item in ins
    ]
    return pl.pallas_call(
        body,
        out_shape=outs,
        in_specs=specs,
        out_specs=jax.tree.map(lambda _: pl.BlockSpec(memory_space=pltpu.VMEM), outs),
        scratch_shapes=list(scratch),
        cost_estimate=pl.CostEstimate(flops=flops, bytes_accessed=moved, transcendentals=0),
        compiler_params=pltpu.CompilerParams(vmem_limit_bytes=limit << 20),
    )(*ins)


def chunk(me, j, rows):
    return pl.ds(pl.multiple_of((me ^ j) * rows, rows), rows)


def segment_of(lengths, places):
    end = jnp.int32(0)
    found = jnp.zeros(places.shape, jnp.int32)
    for s in range(SENTS):
        end = end + lengths[0, s]
        found = found + jnp.where(places >= end, 1, 0)
    return found


def row_places(me, extent, dim, rows):
    at = lax.broadcasted_iota(jnp.int32, extent, dim)
    return ((at // rows) ^ me) * rows + at % rows


def attend(ids, lens, tok, wq, wk, wv, bq, bv, tok_x, q_out, k_out, v_out, probs_out, low_out, wide_out):
    me = ids[0]
    slots, cols = q_out.shape
    rows = slots // 4
    for j in range(4):
        tok_x[j * rows : (j + 1) * rows, :] = tok[chunk(me, j, rows), :]
    t = tok_x[...]
    q_out[...] = (nt(t, wq[...]) + bq[...]).astype(bf16)
    k_out[...] = nt(t, wk[...]).astype(bf16)
    v_out[...] = (nt(t, wv[...]) + bv[...]).astype(bf16)
    seg_row = segment_of(lens, row_places(me, (1, slots), 1, rows))
    seg_col = segment_of(lens, row_places(me, (slots, 1), 0, rows))
    scale = HDIM**-0.5
    for j in range(4):
        at = slice(j * rows, (j + 1) * rows)
        allowed = seg_col[at] == seg_row
        for h in range(cols // HDIM):
            lane = slice(h * HDIM, (h + 1) * HDIM)
            s = jnp.where(allowed, nt(q_out[at, lane], k_out[:, lane]) * scale, -1000000000.0)
            e = jnp.exp(s - jnp.max(s, axis=-1, keepdims=True))
            p = (e * (1.0 / jnp.sum(e, axis=-1, keepdims=True))).astype(bf16)
            probs_out[h, at, :] = p
            low_out[at, lane] = nn(p, v_out[:, lane]).astype(bf16)
        wide_out[at, :] = low_out[at, :].astype(f32)


def join_w_out(ids, *refs):
    pieces, out, held = refs[:-2], refs[-2], refs[-1]
    step = pieces[0].shape[1]
    for d in range(len(pieces)):
        at = pl.ds(pl.multiple_of((ids[1] ^ d) * step, 8), step)
        for k in range(4):
            held[k, at, :] = pieces[d][k]
    out[...] = held[...].astype(bf16)


def gelu_grad(upper, out):
    rows = 64
    for r in range(0, upper.shape[0], rows):
        u = upper[r : r + rows, :]
        cdf = 0.5 * (1.0 + lax.erf(u * 0.7071067811865476))
        out[r : r + rows, :] = cdf + u * (0.3989422804014327 * jnp.exp(-0.5 * u * u))


def feed(tok_x, m0, m1, m2, m3, w_all, b_out, g_attn, b_attn, w_up, b_up, w_down, b_down, *outs):
    p0, p1, p2, p3, low, upper, act, normal_own, inverse_own, resid_own = outs
    parts = (p0, p1, p2, p3)
    mixed = (m0, m1, m2, m3)
    rows = p0.shape[0]
    for j in (3, 2, 1, 0):
        at = slice(j * rows, (j + 1) * rows)
        total = tok_x[at, :].astype(f32) + b_out[...]
        for k in range(4):
            i = j ^ k
            total = total + nn(mixed[k][i * rows : (i + 1) * rows, :].astype(bf16), w_all[k])
        normal, inverse = norm_stats(total)
        normed = normal * g_attn[...] + b_attn[...]
        low[at, :] = normed.astype(bf16)
        up = nn(low[at, :], w_up[...]) + b_up[...]
        upper[at, :] = up
        half = rows // 2
        for r in (0, half):
            u = upper[j * rows + r : j * rows + r + half, :]
            cdf = 0.5 * (1.0 + lax.erf(u * 0.7071067811865476))
            act[j * rows + r : j * rows + r + half, :] = (u * cdf).astype(bf16)
        parts[j][...] = nn(act[at, :], w_down[...])
        if j == 0:
            normal_own[...] = normal
            inverse_own[...] = jnp.broadcast_to(inverse, inverse_own.shape)
            resid_own[...] = normed + b_down[...]


def finish(ids, lens, r0, r1, r2, r3, g_ffn, b_ffn, out_grad, pool_grad, grad_of, w_down, w_up, *refs):
    outs, (normal_ref, inverse_ref, pooled_grad) = refs[:-3], refs[-3:]
    p0, p1, p2, p3, layer_out, pools, d_own, low_out, up_out, side = outs
    me = ids[0]
    parts = (p0, p1, p2, p3)
    rows, width = r0.shape
    gain, shift = g_ffn[...], b_ffn[...]
    seg_row = segment_of(lens, row_places(me, (1, 4 * rows), 1, rows))
    seg_col = segment_of(lens, row_places(me, (4 * rows, 1), 0, rows))
    slot_col = lax.broadcasted_iota(jnp.int32, (SENTS, 1), 0)
    slot_row = lax.broadcasted_iota(jnp.int32, (1, SENTS), 1)
    pooled = jnp.zeros((SENTS, width), f32)
    for j, block in enumerate((r0, r1, r2, r3)):
        at = slice(j * rows, (j + 1) * rows)
        normal, inverse = norm_stats(block[...])
        normal_ref[at, :] = normal
        inverse_ref[at, :] = jnp.broadcast_to(inverse, (rows, 128))
        final = normal * gain + shift
        layer_out[chunk(me, j, rows), :] = final.astype(bf16)
        member = jnp.where(slot_col == seg_row[:, at], 1.0, 0.0)
        pooled = pooled + nn(member, final, highest)
    denom = jnp.zeros((SENTS, 1), f32)
    for s in range(SENTS):
        size = jnp.maximum(lens[0, s], 1).astype(f32)
        denom = denom + jnp.where(slot_col == s, size, 0.0)
    pooled = pooled / denom
    pooled_grad[...] = jnp.zeros((SENTS, width), f32)
    offset = 0
    for m in truncations(width):
        leading = pooled[:, :m]
        factor = lax.rsqrt(jnp.mean(leading * leading, axis=1, keepdims=True) + pool_eps)
        third, lane = offset // width, offset % width
        pools[third * SENTS : (third + 1) * SENTS, lane : lane + m] = leading * factor
        upstream = pool_grad[:, offset : offset + m]
        inner = jnp.mean(upstream * leading, axis=1, keepdims=True)
        pooled_grad[:, :m] += factor * upstream - leading * (factor * factor * factor * inner)
        offset += m
    rest = offset % width
    pools[2 * SENTS :, rest:] = jnp.zeros((SENTS, width - rest), f32)
    spread = pooled_grad[...] / denom
    sums = [jnp.zeros((1, width), f32) for _ in range(4)]
    for j in (3, 2, 1, 0):
        at = slice(j * rows, (j + 1) * rows)
        belongs = jnp.where(seg_col[at] == slot_row, 1.0, 0.0)
        d_final = out_grad[chunk(me, j, rows), :].astype(f32) + nn(belongs, spread, highest)
        normal = normal_ref[at, :]
        sums[0] = sums[0] + col_sum(d_final)
        sums[1] = sums[1] + col_sum(d_final * normal)
        d_resid = norm_back(d_final * gain, normal, inverse_ref[at, :1])
        sums[2] = sums[2] + col_sum(d_resid)
        low_out[at, :] = d_resid.astype(bf16)
        d_upper = nt(low_out[at, :], w_down[...]) * grad_of[at, :]
        sums[3] = sums[3] + col_sum(d_upper)
        up_out[at, :] = d_upper.astype(bf16)
        parts[j][...] = nt(up_out[at, :], w_up[...])
        if j == 0:
            d_own[...] = d_resid
    for n in range(4):
        side[n : n + 1, :] = sums[n]
    side[4:, :] = jnp.zeros((4, width), f32)


def ffn_grads(ids, low, up_low, act, resid_low, even, odd, held):
    width = low.shape[1]
    held[:width, :] = tn(low[...], up_low[...])
    held[width:, :] = tn(act[...], resid_low[...])
    step = even.shape[1]
    for d in range(8):
        at = pl.ds(pl.multiple_of((ids[1] ^ d) * step, 8), step)
        (odd if d & 1 else even)[d // 2] = held[at, :]


def back_hidden(own, near, across, d_resid, normal, inverse, g_attn, w_all, *outs):
    e0, e1, e2, e3, d_hidden_out, low_out = outs
    d_normed = d_resid[...] + (own[...] + near[...] + across[...])
    rows, width = d_normed.shape
    cols = e0.shape[1]
    side = [None, col_sum(d_normed * normal[...]), col_sum(d_normed)]
    d_hidden = norm_back(d_normed * g_attn[...], normal[...], inverse[:, :1])
    side[0] = col_sum(d_hidden)
    d_hidden_out[...] = d_hidden
    low_out[...] = d_hidden.astype(bf16)
    for k, out in enumerate((e0, e1, e2, e3)):
        out[:rows, :] = nt(low_out[...], w_all[k]).astype(bf16).astype(f32)
        for v in range(3):
            for s in range(width // cols):
                r = rows + 4 * v + s
                out[r : r + 1, :] = side[v][:, s * cols : (s + 1) * cols]
        out[rows + 12 :, :] = jnp.zeros((4, cols), f32)


def out_grads(ids, m0, m1, m2, m3, hidden_low, even, odd, held):
    rows = hidden_low.shape[0]
    for k, block in enumerate((m0, m1, m2, m3)):
        held[k] = tn(block[k * rows : (k + 1) * rows, :].astype(bf16), hidden_low[...])
    step = even.shape[2]
    for d in range(8):
        at = pl.ds(pl.multiple_of((ids[1] ^ d) * step, 8), step)
        for k in range(4):
            (odd if d & 1 else even)[d // 2, k] = held[k, at, :]


def attend_back(e0, e1, e2, e3, probs, q, k, v, wq, wk, wv, *refs):
    outs, (d_mixed, turned, d_scores) = refs[:-3], refs[-3:]
    p0, p1, p2, p3, grads, bias, shared = outs
    slots, cols = q.shape
    rows = slots // 4
    scale = HDIM**-0.5
    for j, block in enumerate((e0, e1, e2, e3)):
        d_mixed[j * rows : (j + 1) * rows, :] = block[:rows, :].astype(bf16)
    shared[...] = (e0[rows:, :] + e1[rows:, :]) + (e2[rows:, :] + e3[rows:, :])
    for h in range(cols // HDIM):
        lane = slice(h * HDIM, (h + 1) * HDIM)
        for j in range(4):
            at = slice(j * rows, (j + 1) * rows)
            p = probs[h, at, :].astype(f32)
            dp = nt(d_mixed[at, lane], v[:, lane])
            t = p * dp
            ds = (t - p * jnp.sum(t, axis=-1, keepdims=True)) * scale
            d_scores[at, :] = ds.astype(bf16)
        d_query = nn(d_scores[...], k[:, lane])
        bias[0:1, lane] = col_sum(d_query)
        grads[:, lane] = d_query.astype(bf16)
        d_key = tn(d_scores[...], q[:, lane])
        grads[:, cols + h * HDIM : cols + (h + 1) * HDIM] = d_key.astype(bf16)
        d_value = tn(probs[h], d_mixed[:, lane])
        bias[1:2, lane] = col_sum(d_value)
        grads[:, 2 * cols + h * HDIM : 2 * cols + (h + 1) * HDIM] = d_value.astype(bf16)
    bias[2:, :] = jnp.zeros((6, cols), f32)
    turned[:cols, :] = wq[...]
    turned[cols : 2 * cols, :] = wk[...]
    turned[2 * cols :, :] = wv[...]
    for j, out in ((3, p3), (2, p2), (1, p1), (0, p0)):
        out[...] = nn(grads[j * rows : (j + 1) * rows, :], turned[...])


def qkv_grads(ids, grads, tok_x, side, shared, bias, even, odd, held):
    width = tok_x.shape[1]
    cols = bias.shape[1]
    part = width // cols
    total = grads.shape[1]
    step = total // 8
    held[:total, :] = tn(grads[...], tok_x[...])
    held[total:, :] = jnp.zeros((64, width), f32)
    held[total : total + 4, :] = side[:4, :]

    @pl.when(ids[0] >= 0)
    def _():
        for n in range(2):
            held[total + 4 : total + 5, n * cols : (n + 1) * cols] = bias[n : n + 1, :]
        for n in range(3):
            for s in range(part):
                row = shared[4 * n + s : 4 * n + s + 1, :]
                held[total + 8 + n : total + 9 + n, s * cols : (s + 1) * cols] = row

    for d in range(8):
        c = ids[1] ^ d
        out = odd if d & 1 else even
        out[d // 2, :step, :] = held[pl.ds(pl.multiple_of(c * step, 8), step), :]
        out[d // 2, step:, :] = held[pl.ds(pl.multiple_of(total + c * 8, 8), 8), :]


def fold(mine, theirs, a0, a1, a2, a3):
    for n, out in enumerate((a0, a1, a2, a3)):
        out[...] = mine[n] + theirs[n]


def place(me, r0, r1, r2, r3, out):
    rows = r0.shape[0]
    for j, block in enumerate((r0, r1, r2, r3)):
        out[chunk(me[0], j, rows), :] = block[...]


def unpack_ffn(ids, *refs):
    blocks, (up_out, down_out, pools_out, held) = refs[:8], refs[8:]
    half = up_out.shape[0]
    step = 2 * half // 8
    wide = pools_out.shape[0]
    width = up_out.shape[1]
    for d, block in enumerate(blocks):
        c = ids[1] ^ d
        at = pl.ds(pl.multiple_of((c % 4) * step, 8), step)

        @pl.when(c < 4)
        def _(block=block, at=at):
            up_out[at, :] = block[:step, :]

        @pl.when(c >= 4)
        def _(block=block, at=at):
            down_out[at, :] = block[:step, :]

        to = pl.ds(pl.multiple_of(c * SENTS, 8), SENTS)
        for n in range(3):
            held[n, to, :] = block[step + n * SENTS : step + (n + 1) * SENTS, :]
    for n in range(3):
        m = min(width, wide - n * width)
        pools_out[n * width : n * width + m, :] = held[n].T[:m, :]


def unpack_attn(ids, *refs):
    blocks, (q_out, k_out, v_out, o_out, side, held) = refs[:8], refs[8:]
    cols = o_out.shape[0]
    step = 3 * cols // 8
    small = cols // 8
    for d, block in enumerate(blocks):
        c = ids[1] ^ d
        held[pl.ds(pl.multiple_of(c * step, 8), step), :] = block[:step, :]
        side[pl.ds(pl.multiple_of(c * 8, 8), 8), :] = block[step : step + 8, :]
        o_out[pl.ds(pl.multiple_of(c * small, 8), small), :] = block[step + 8 :, :]
    q_out[...] = held[:cols, :]
    k_out[...] = held[cols : 2 * cols, :]
    v_out[...] = held[2 * cols :, :]


def swap(block, k):
    return lax.ppermute(block, "tensor", swaps[k])


def swap_dp(block, k, n_dp):
    return lax.ppermute(block, "dp", [(i, i ^ k) for i in range(n_dp)])


def scatter_sum(parts):
    far = swap(parts[3], 1)
    across = swap(parts[2] + far, 2)
    near = swap(parts[1], 1)
    return parts[0], near, across


def gather(block):
    across = swap(block, 2)
    near = swap(block, 1)
    return block, near, across, swap(across, 1)


def rest_of_dp(block, n_dp):
    if n_dp == 8:
        return block
    groups = [[i + 8 * j for j in range(n_dp // 8)] for i in range(8)]
    return lax.psum(block, "dp", axis_index_groups=groups)


def dp_scatter(even, odd, n_dp):
    other = swap_dp(odd, 1, n_dp)
    flat = even.shape[-2] if even.ndim == 3 else even.shape[1] * even.shape[2]
    even = even.reshape(4, flat, even.shape[-1])
    other = other.reshape(even.shape)
    block = shape(*even.shape[1:])
    parts = call(fold, [block] * 4, [even, other], moved=3 * even.size * 4)
    total = parts[0]
    for n in (1, 2, 3):
        total = total + swap_dp(parts[n], 2 * n, n_dp)
    return rest_of_dp(total, n_dp)


def dp_gather(block, n_dp):
    blocks = [block] + [swap_dp(block, 2 * n, n_dp) for n in (1, 2, 3)]
    others = [swap_dp(item, 1, n_dp) for item in blocks]
    return [item for pair in zip(blocks, others) for item in pair]


def make_shards(n_dp):
    def shards(
        tokens,
        lengths,
        w_query,
        w_key,
        w_value,
        b_query,
        b_value,
        w_out,
        b_out,
        g_attn,
        b_attn,
        w_up,
        b_up,
        w_down,
        b_down,
        g_ffn,
        b_ffn,
        out_grad,
        pool_grad,
    ):
        me = lax.axis_index("tensor").astype(jnp.int32)
        group = (lax.axis_index("dp") % 8).astype(jnp.int32)
        ids = jnp.stack([me, group])
        slots, width = tokens.shape
        cols = w_query.shape[1]
        units = w_up.shape[1]
        heads = cols // HDIM
        rows = slots // 4
        row = lambda vector: vector.reshape(1, -1)
        wq, wk, wv = w_query.T, w_key.T, w_value.T

        piece = cols // 8
        slice_own = lax.dynamic_slice_in_dim(w_out, group * piece, piece, 0).astype(f32)
        slices = jnp.stack(gather(slice_own))
        w_all = call(
            join_w_out,
            shape(4, cols, width, kind=bf16),
            [ids] + dp_gather(slices, n_dp),
            moved=4 * cols * width * 6,
            scratch=[pltpu.VMEM((4, cols, width), f32)],
        )

        tok_x, q, k, v, probs, mixed_low, mixed = call(
            attend,
            [
                shape(slots, width, kind=bf16),
                shape(slots, cols, kind=bf16),
                shape(slots, cols, kind=bf16),
                shape(slots, cols, kind=bf16),
                shape(heads, slots, slots, kind=bf16),
                shape(slots, cols, kind=bf16),
                shape(slots, cols),
            ],
            [ids, lengths, tokens, wq, wk, wv, row(b_query), row(b_value)],
            flops=2 * slots * width * 3 * cols + 4 * slots * slots * cols,
            moved=slots * width * 4 + 3 * cols * width * 2 + heads * slots * slots * 2,
        )
        mixed_all = gather(mixed)
        *parts, normed_low, upper, act, normal_own, inverse_own, resid_own = call(
            feed,
            [shape(rows, width)] * 4
            + [
                shape(slots, width, kind=bf16),
                shape(slots, units),
                shape(slots, units, kind=bf16),
                shape(rows, width),
                shape(rows, 128),
                shape(rows, width),
            ],
            [tok_x, *mixed_all, w_all, row(b_out), row(g_attn), row(b_attn)]
            + [w_up, row(b_up), w_down, row(b_down)],
            flops=2 * slots * width * (width + 2 * units),
            moved=4 * slots * width * 4 + 3 * width * units * 2,
        )
        slope = call(
            gelu_grad, shape(slots, units), [upper], moved=8 * slots * units, flops=slots * units
        )
        own, near, across = scatter_sum(parts)
        resid = gather(resid_own + own + near + across)
        *parts, layer_out, own_pools, d_resid, resid_low, upper_low, side = call(
            finish,
            [shape(rows, width)] * 4
            + [
                shape(slots, width, kind=bf16),
                shape(3 * SENTS, width),
                shape(rows, width),
                shape(slots, width, kind=bf16),
                shape(slots, units, kind=bf16),
                shape(8, width),
            ],
            [ids, lengths, *resid, row(g_ffn), row(b_ffn), out_grad, pool_grad, slope]
            + [w_down, w_up],
            flops=4 * slots * width * units,
            moved=6 * slots * width * 4,
            scratch=[
                pltpu.VMEM((slots, width), f32),
                pltpu.VMEM((slots, 128), f32),
                pltpu.VMEM((SENTS, width), f32),
            ],
        )
        own, near, across = scatter_sum(parts)
        step = 2 * width // 8
        even, odd = call(
            ffn_grads,
            [shape(4, step, width)] * 2,
            [ids, normed_low, upper_low, act, resid_low],
            flops=4 * slots * width * units,
            moved=4 * slots * width * 2 + 8 * width * units,
            scratch=[pltpu.VMEM((2 * width, width), f32)],
        )
        ffn_sum = dp_scatter(even, odd, n_dp)
        *sent, d_hidden, hidden_low = call(
            back_hidden,
            [shape(rows + 16, cols)] * 4 + [shape(rows, width), shape(rows, width, kind=bf16)],
            [own, near, across, d_resid, normal_own, inverse_own, row(g_attn), w_all],
            flops=2 * rows * width * 4 * cols,
            moved=6 * rows * width * 4,
        )
        d_mixed = [sent[0]] + [swap(sent[n], n) for n in (1, 2, 3)]
        even, odd = call(
            out_grads,
            [shape(4, 4, piece, width)] * 2,
            [ids, *mixed_all, hidden_low],
            flops=2 * rows * width * 4 * cols,
            moved=8 * 4 * cols * width,
            scratch=[pltpu.VMEM((4, cols, width), f32)],
        )
        out_sum = dp_scatter(even, odd, n_dp)
        *parts, grads, bias, shared = call(
            attend_back,
            [shape(rows, width)] * 4
            + [shape(slots, 3 * cols, kind=bf16), shape(8, cols), shape(16, cols)],
            [*d_mixed, probs, q, k, v, wq, wk, wv],
            flops=8 * slots * slots * cols + 6 * slots * width * cols,
            moved=heads * slots * slots * 2 + 2 * slots * width * 4,
            scratch=[
                pltpu.VMEM((slots, cols), bf16),
                pltpu.VMEM((3 * cols, width), bf16),
                pltpu.VMEM((slots, slots), bf16),
            ],
        )
        even, odd = call(
            qkv_grads,
            [shape(4, 3 * piece + 8, width)] * 2,
            [ids, grads, tok_x, side, shared, bias],
            flops=6 * slots * width * cols,
            moved=8 * 3 * cols * width,
            scratch=[pltpu.VMEM((3 * cols + 64, width), f32)],
        )
        own, near, across = scatter_sum(parts)
        qkv_sum = dp_scatter(even, odd, n_dp)
        out_parts = out_sum.reshape(4, piece, width)
        out_terms = scatter_sum([out_parts[n] for n in range(4)])
        attn_own = jnp.concatenate([qkv_sum, sum(out_terms)])
        attn_blocks = dp_gather(attn_own, n_dp)
        own_rows = [own + near + across + d_hidden]
        d_tokens = call(
            place, shape(slots, width), [ids, *gather(own_rows[0])], moved=8 * slots * width
        )
        ffn_blocks = dp_gather(jnp.concatenate([ffn_sum, own_pools]), n_dp)
        wide = pool_grad.shape[1]
        d_w_up, d_w_down, pools = call(
            unpack_ffn,
            [shape(width, units), shape(units, width), shape(wide, 8 * SENTS)],
            [ids, *ffn_blocks],
            moved=16 * width * units,
            scratch=[pltpu.VMEM((3, 8 * SENTS, width), f32)],
        )
        pools = pools.T
        if n_dp > 8:
            third = [own_pools[n * SENTS : (n + 1) * SENTS] for n in range(3)]
            third = jnp.concatenate(third, axis=1)[:, :wide]
            pools = lax.all_gather(third, "dp", axis=0, tiled=True)
        d_w_query, d_w_key, d_w_value, d_w_out, vectors = call(
            unpack_attn,
            [shape(cols, width)] * 4 + [shape(64, width)],
            [ids, *attn_blocks],
            moved=8 * 4 * cols * width,
            scratch=[pltpu.VMEM((3 * cols, width), f32)],
        )
        return (
            layer_out,
            pools,
            d_tokens,
            d_w_query.T,
            d_w_key.T,
            d_w_value.T,
            vectors[4, :cols],
            vectors[4, cols : 2 * cols],
            d_w_out,
            vectors[8],
            vectors[9],
            vectors[10],
            d_w_up,
            vectors[3],
            d_w_down,
            vectors[2],
            vectors[1],
            vectors[0],
        )

    return shards


def solution(mesh):
    return jax.shard_map(
        make_shards(mesh.shape["dp"]),
        mesh=mesh,
        in_specs=(
            P("dp", None),
            P("dp", None),
            P(None, "tensor"),
            P(None, "tensor"),
            P(None, "tensor"),
            P("tensor"),
            P("tensor"),
            P("tensor", None),
            P(),
            P(),
            P(),
            P(None, "tensor"),
            P("tensor"),
            P("tensor", None),
            P(),
            P(),
            P(),
            P("dp", None),
            P("dp", None),
        ),
        out_specs=(
            P("dp", None),
            P(),
            P("dp", None),
            P(None, "tensor"),
            P(None, "tensor"),
            P(None, "tensor"),
            P("tensor"),
            P("tensor"),
            P("tensor", None),
            P(),
            P(),
            P(),
            P(None, "tensor"),
            P("tensor"),
            P("tensor", None),
            P(),
            P(),
            P(),
        ),
        check_vma=False,
    )
```

time: 487 us -> 343 us (0.70)
  waiting for transfers between devices: 339 us -> 208 us
  starting transfers between devices: 0.61 us -> 85.3 us
  matrix products: 55.8 us -> 0 us
  Pallas kernels: 0 us -> 38.5 us
  blocking collectives: 35.6 us -> 0 us
  other arithmetic: 20.7 us -> 1.59 us
  between operations: 14.5 us -> 1.22 us
  local copies, waits for them, and re-layouts: 19.7 us -> 7.44 us
    psum x5 -> x0, waiting for transfers between devices: 339 us -> none  [the longest x1 114 us: shards(): lax.psum((w_query_part, w_key_part, w_value_part, b_query_part, b_value_p...]
    ppermute x0 -> x60, waiting for transfers between devices: none -> 208 us  [the longest x27 130 us: swap(): return lax.ppermute(block, 'tensor', swaps[k])]
    ppermute x0 -> x60, starting transfers between devices: none -> 85.3 us  [the longest x27 59.8 us: swap(): return lax.ppermute(block, 'tensor', swaps[k])]
    dot_general x26 -> x0, matrix products: 55.8 us -> none  [the longest x1 7.53 us: shards(): jnp.einsum('hqk,khd->qhd', d_scores, key_heads, preferred_element_type=jn...]
    pallas_call x0 -> x16, Pallas kernels: none -> 38.5 us  [call(): pl.pallas_call(body, out_shape=outs, in_specs=specs, out_specs=jax.tree.m...]
    psum x1 -> x0, blocking collectives: 25 us -> none  [shards(): lax.psum((w_query_part, w_key_part, w_value_part, b_query_part, b_value_p...]
    reduce_sum x13 -> x0, other arithmetic: 11.5 us -> none  [the longest x2 3.66 us: norm_stats(): centre = jnp.mean(rows, axis=-1, keepdims=True)]
    unnamed x141 -> x44, local copies, waits for them, and re-layouts: 17.3 us -> 6.11 us
  transfers between devices with their start and end apart: 5 -> 60, of which waited for: 5 -> 27; matrix products, arithmetic and copies ran while one was open for 4% -> 1% of each run, Pallas kernels for 0% -> 6%
where the time goes in v1:
time: 343 us; the launch traced here: 342 us
  waiting for transfers between devices  208 us (61%)
  starting transfers between devices  85.3 us (25%)
  Pallas kernels  38.5 us (11%)
  local copies, waits for them, and re-layouts  7.44 us (2%)
    ppermute x27, waiting for transfers between devices, swap(): return lax.ppermute(block, 'tensor', swaps[k])  130 us
    ppermute x33, waiting for transfers between devices, swap_dp(): return lax.ppermute(block, 'dp', [(i, i ^ k) for i in range(n_dp)])  78.2 us
    ppermute x27, starting transfers between devices, swap(): return lax.ppermute(block, 'tensor', swaps[k])  59.8 us
    pallas_call x16, Pallas kernels, call(): pl.pallas_call(body, out_shape=outs, in_specs=specs, out_specs=jax.tree.m...  38.5 us
    ppermute x33, starting transfers between devices, swap_dp(): return lax.ppermute(block, 'dp', [(i, i ^ k) for i in range(n_dp)])  25.5 us
  transfers between devices with their start and end apart: 60, of which 27 were waited for; matrix products, arithmetic and copies ran while one was open for 1% of the time, Pallas kernels for 6%

profile of v1, /device:TPU:0, one launch (start us, length us, event | category | flops | bytes accessed | tf_op | source)
XLA Modules:
  0.0 342.2 jit_solution(11927552740702189284)
XLA Ops:
  16.4 6.7 %shard_map.322 = (bf16[512,768]{1,0:T(8,128)(2,1)S(1)}, bf16[512,192]{1,0:T(8,128)(2,1)S(1)}, bf16[512,192]{1,0:T(8,128)(2,1)S(1)}, bf16[512,192]{1,0:T(8,128)(2...) custom-call(s32[2]{0:T(128)S(1)} %pad_add_fusion.ids.me, ...), custom_call_target="tpu_custom_call" | custom-call | flops 654311424 | bytes 4030464 | tf_op jit(solution)/shard_map/pallas_call | solution.py:64
  30.0 18.9 %collective-permute-done.1.m2 = f32[512,192]{1,0:T(8,128)S(1)} collective-permute-done((f32[512,192]{1,0:T(8,128)S(1)}, f32[512,192]{1,0:T(8,128)S(1)}, u32[]{:S(2)}, u32[]{:S(2)}) %collective-permute-start.1) | collective-permute-done | bytes 393248 | tf_op jit(solution)/shard_map/ppermute | solution.py:380
  54.2 9.5 %collective-permute-done.m1 = f32[512,192]{1,0:T(8,128)S(1)} collective-permute-done((f32[512,192]{1,0:T(8,128)S(1)}, f32[512,192]{1,0:T(8,128)S(1)}, u32[]{:S(2)}, u32[]{:S(2)}) %collective-permute-start) | collective-permute-done | bytes 393248 | tf_op jit(solution)/shard_map/ppermute | solution.py:380
  63.8 10.3 %collective-permute-done.2.m3 = f32[512,192]{1,0:T(8,128)S(1)} collective-permute-done((f32[512,192]{1,0:T(8,128)S(1)}, f32[512,192]{1,0:T(8,128)S(1)}, u32[]{:S(2)}, u32[]{:S(2)}) %collective-permute-start.2) | collective-permute-done | bytes 393248 | tf_op jit(solution)/shard_map/ppermute | solution.py:380
  74.0 4.7 %shard_map.324 = (f32[128,768]{1,0:T(8,128)S(1)}, f32[128,768]{1,0:T(8,128)S(1)}, f32[128,768]{1,0:T(8,128)S(1)}, f32[128,768]{1,0:T(8,128)S(1)}, bf16[512,768]{...) custom-call(bf16[512,768]{1,0:T(8,128)(2,1)S(1)} %get-tuple-element., ...), custom_call_target="tpu_custom_call" | custom-call | flops 1811939328 | bytes 9830400 | tf_op jit(solution)/shard_map/pallas_call | solution.py:64
  80.9 10.0 %collective-permute-done.14 = f32[128,768]{1,0:T(8,128)S(1)} collective-permute-done((f32[128,768]{1,0:T(8,128)S(1)}, f32[128,768]{1,0:T(8,128)S(1)}, u32[]{:S(2)}, u32[]{:S(2)}) %collective-permute-start.14) | collective-permute-done | bytes 393248 | tf_op jit(solution)/shard_map/ppermute | solution.py:380
  94.8 8.2 %collective-permute-done.13 = f32[128,768]{1,0:T(8,128)S(1)} collective-permute-done((f32[128,768]{1,0:T(8,128)S(1)}, f32[128,768]{1,0:T(8,128)S(1)}, u32[]{:S(2)}, u32[]{:S(2)}) %collective-permute-start.13) | collective-permute-done | bytes 393248 | tf_op jit(solution)/shard_map/ppermute | solution.py:380
  103.0 10.8 %collective-permute-done.15 = f32[128,768]{1,0:T(8,128)S(1)} collective-permute-done((f32[128,768]{1,0:T(8,128)S(1)}, f32[128,768]{1,0:T(8,128)S(1)}, u32[]{:S(2)}, u32[]{:S(2)}) %collective-permute-start.15) | collective-permute-done | bytes 393248 | tf_op jit(solution)/shard_map/ppermute | solution.py:380
  113.9 11.6 %collective-permute-start.16 = (f32[128,768]{1,0:T(8,128)S(1)}, f32[128,768]{1,0:T(8,128)S(1)}, u32[]{:S(2)}, u32[]{:S(2)}) collective-permute-start(f32[128,768]{1,0:T(8,128)S(1)} %add_add_fusion.2.r0), channel_id=1, source_target_pairs={{0,1},{1,0},{2,3},{3,2},{4,5},{5,4},{6,7},{7,6},{8,9},{9,8},{10,11... | collective-permute-start | bytes 1179656 | tf_op jit(solution)/shard_map/ppermute | solution.py:380
  125.6 9.2 %collective-permute-start.18 = (f32[128,768]{1,0:T(8,128)S(1)}, f32[128,768]{1,0:T(8,128)S(1)}, u32[]{:S(2)}, u32[]{:S(2)}) collective-permute-start(f32[128,768]{1,0:T(8,128)S(1)} %collective-permute-done.17.r2), channel_id=1, source_target_pairs={{0,1},{1,0},{2,3},{3,2},{4,5},{5,4},{6,7},{7,6},{8,9},{9,8},{10,11... | collective-permute-start | bytes 1179656 | tf_op jit(solution)/shard_map/ppermute | solution.py:380
  135.5 6.7 %collective-permute-done.18.r3 = f32[128,768]{1,0:T(8,128)S(1)} collective-permute-done((f32[128,768]{1,0:T(8,128)S(1)}, f32[128,768]{1,0:T(8,128)S(1)}, u32[]{:S(2)}, u32[]{:S(2)}) %collective-permute-start.18) | collective-permute-done | bytes 393248 | tf_op jit(solution)/shard_map/ppermute | solution.py:380
  142.2 8.6 %shard_map.326 = (f32[128,768]{1,0:T(8,128)S(1)}, f32[128,768]{1,0:T(8,128)S(1)}, f32[128,768]{1,0:T(8,128)S(1)}, f32[128,768]{1,0:T(8,128)S(1)}, bf16[512,768]{...) custom-call(s32[2]{0:T(128)S(1)} %pad_add_fusion.ids.me, ...), custom_call_target="tpu_custom_call" | custom-call | flops 1207959552 | bytes 9437184 | tf_op jit(solution)/shard_map/pallas_call | solution.py:64
  153.3 9.4 %collective-permute-done.31 = f32[128,768]{1,0:T(8,128)S(1)} collective-permute-done((f32[128,768]{1,0:T(8,128)S(1)}, f32[128,768]{1,0:T(8,128)S(1)}, u32[]{:S(2)}, u32[]{:S(2)}) %collective-permute-start.31) | collective-permute-done | bytes 393248 | tf_op jit(solution)/shard_map/ppermute | solution.py:380
  167.8 8.1 %collective-permute-done.32.across = f32[128,768]{1,0:T(8,128)S(1)} collective-permute-done((f32[128,768]{1,0:T(8,128)S(1)}, f32[128,768]{1,0:T(8,128)S(1)}, u32[]{:S(2)}, u32[]{:S(2)}) %collective-permute-start.32) | collective-permute-done | bytes 393248 | tf_op jit(solution)/shard_map/ppermute | solution.py:380
  182.5 4.6 %collective-permute-done.33.e1 = f32[144,192]{1,0:T(8,128)S(1)} collective-permute-done((f32[144,192]{1,0:T(8,128)S(1)}, f32[144,192]{1,0:T(8,128)S(1)}, u32[]{:S(2)}, u32[]{:S(2)}) %collective-permute-start.33) | collective-permute-done | bytes 110624 | tf_op jit(solution)/shard_map/ppermute | solution.py:380
  187.0 6.0 %collective-permute-done.34.e2 = f32[144,192]{1,0:T(8,128)S(1)} collective-permute-done((f32[144,192]{1,0:T(8,128)S(1)}, f32[144,192]{1,0:T(8,128)S(1)}, u32[]{:S(2)}, u32[]{:S(2)}) %collective-permute-start.34) | collective-permute-done | bytes 110624 | tf_op jit(solution)/shard_map/ppermute | solution.py:380
  199.8 9.9 %collective-permute-done.37 = f32[128,768]{1,0:T(8,128)S(1)} collective-permute-done((f32[128,768]{1,0:T(8,128)S(1)}, f32[128,768]{1,0:T(8,128)S(1)}, u32[]{:S(2)}, u32[]{:S(2)}) %collective-permute-start.37) | collective-permute-done | bytes 393248 | tf_op jit(solution)/shard_map/ppermute | solution.py:380
  216.1 8.8 %collective-permute-done.36 = f32[128,768]{1,0:T(8,128)S(1)} collective-permute-done((f32[128,768]{1,0:T(8,128)S(1)}, f32[128,768]{1,0:T(8,128)S(1)}, u32[]{:S(2)}, u32[]{:S(2)}) %collective-permute-start.36) | collective-permute-done | bytes 393248 | tf_op jit(solution)/shard_map/ppermute | solution.py:380
  230.8 8.4 %collective-permute-done.48 = f32[96,768]{1,0:T(8,128)S(1)} collective-permute-done((f32[96,768]{1,0:T(8,128)S(1)}, f32[96,768]{1,0:T(8,128)S(1)}, u32[]{:S(2)}, u32[]{:S(2)}) %collective-permute-start.48) | collective-permute-done | bytes 294944 | tf_op jit(solution)/shard_map/ppermute | solution.py:384
  242.5 5.4 %collective-permute-done.51 = f32[24,768]{1,0:T(8,128)S(1)} collective-permute-done((f32[24,768]{1,0:T(8,128)S(1)}, f32[24,768]{1,0:T(8,128)S(1)}, u32[]{:S(2)}, u32[]{:S(2)}) %collective-permute-start.51) | collective-permute-done | bytes 73760 | tf_op jit(solution)/shard_map/ppermute | solution.py:380
  261.8 9.0 %collective-permute-done.20 = f32[192,768]{1,0:T(8,128)S(1)} collective-permute-done((f32[192,768]{1,0:T(8,128)S(1)}, f32[192,768]{1,0:T(8,128)S(1)}, u32[]{:S(2)}, u32[]{:S(2)}) %collective-permute-start.20) | collective-permute-done | bytes 589856 | tf_op jit(solution)/shard_map/ppermute | solution.py:384
  271.4 25.2 %collective-permute-done.21 = f32[192,768]{1,0:T(8,128)S(1)} collective-permute-done((f32[192,768]{1,0:T(8,128)S(1)}, f32[192,768]{1,0:T(8,128)S(1)}, u32[]{:S(2)}, u32[]{:S(2)}) %collective-permute-start.21) | collective-permute-done | bytes 589856 | tf_op jit(solution)/shard_map/ppermute | solution.py:384
  301.0 11.6 %collective-permute-done.56.refs_4_ = f32[104,768]{1,0:T(8,128)S(1)} collective-permute-done((f32[104,768]{1,0:T(8,128)S(1)}, f32[104,768]{1,0:T(8,128)S(1)}, u32[]{:S(2)}, u32[]{:S(2)}) %collective-permute-start.56) | collective-permute-done | bytes 319520 | tf_op jit(solution)/shard_map/ppermute | solution.py:384
  312.7 15.3 %collective-permute-done.54.refs_2_ = f32[104,768]{1,0:T(8,128)S(1)} collective-permute-done((f32[104,768]{1,0:T(8,128)S(1)}, f32[104,768]{1,0:T(8,128)S(1)}, u32[]{:S(2)}, u32[]{:S(2)}) %collective-permute-start.54) | collective-permute-done | bytes 319520 | tf_op jit(solution)/shard_map/ppermute | solution.py:384
  (181 shorter events, 104.1 us)
Async XLA Ops:
  5.7 20.8 %collective-permute-start.3 = (f32[24,768]{1,0:T(8,128)S(1)}, f32[24,768]{1,0:T(8,128)S(1)}, u32[]{:S(2)}, u32[]{:S(2)}) collective-permute-start(f32[24,768]{1,0:T(8,128)S(1)} %get-tuple-element.158), channel_id=1, source_target_pairs={{0,1},{1,0},{2,3},{3,2},{4,5},{5,4},{6,7},{7,6},{8,9},{9,8},{10,11... | collective-permute-start | bytes 221192 | tf_op jit(solution)/shard_map/ppermute | solution.py:380
  23.2 25.8 %collective-permute-start.1 = (f32[512,192]{1,0:T(8,128)S(1)}, f32[512,192]{1,0:T(8,128)S(1)}, u32[]{:S(2)}, u32[]{:S(2)}) collective-permute-start(f32[512,192]{1,0:T(8,128)S(1)} %get-tuple-element.84.m0), channel_id=1, source_target_pairs={{0,2},{1,3},{2,0},{3,1},{4,6},{5,7},{6,4},{7,5},{8,10},{9,11},{10,... | collective-permute-start | bytes 1179656 | tf_op jit(solution)/shard_map/ppermute | solution.py:380
  26.5 22.5 %collective-permute-start.11 = (f32[4,24,768]{2,1,0:T(8,128)S(1)}, f32[4,24,768]{2,1,0:T(8,128)S(1)}, u32[]{:S(2)}, u32[]{:S(2)}) collective-permute-start(f32[4,24,768]{2,1,0:T(8,128)S(1)} %pad_maximum_fusion.2.refs_0_), channel_id=1, source_target_pairs={{0,24},{4,28},{8,16},{12,20},{16,8},{20,12},{24,0},{28,4},{1,25},{... | collective-permute-start | bytes 884744 | tf_op jit(solution)/shard_map/ppermute | solution.py:384
  29.0 22.0 %collective-permute-start.9 = (f32[4,24,768]{2,1,0:T(8,128)S(1)}, f32[4,24,768]{2,1,0:T(8,128)S(1)}, u32[]{:S(2)}, u32[]{:S(2)}) collective-permute-start(f32[4,24,768]{2,1,0:T(8,128)S(1)} %pad_maximum_fusion.2.refs_0_), channel_id=1, source_target_pairs={{0,16},{4,20},{8,24},{12,28},{16,0},{20,4},{24,8},{28,12},{1,17},{... | collective-permute-start | bytes 884744 | tf_op jit(solution)/shard_map/ppermute | solution.py:384
  29.5 21.5 %collective-permute-start.7 = (f32[4,24,768]{2,1,0:T(8,128)S(1)}, f32[4,24,768]{2,1,0:T(8,128)S(1)}, u32[]{:S(2)}, u32[]{:S(2)}) collective-permute-start(f32[4,24,768]{2,1,0:T(8,128)S(1)} %pad_maximum_fusion.2.refs_0_), channel_id=1, source_target_pairs={{0,8},{4,12},{8,0},{12,4},{16,24},{20,28},{24,16},{28,20},{1,9},{5... | collective-permute-start | bytes 884744 | tf_op jit(solution)/shard_map/ppermute | solution.py:384
  30.0 21.5 %collective-permute-start.6 = (f32[4,24,768]{2,1,0:T(8,128)S(1)}, f32[4,24,768]{2,1,0:T(8,128)S(1)}, u32[]{:S(2)}, u32[]{:S(2)}) collective-permute-start(f32[4,24,768]{2,1,0:T(8,128)S(1)} %pad_maximum_fusion.2.refs_0_), channel_id=1, source_target_pairs={{0,4},{4,0},{8,12},{12,8},{16,20},{20,16},{24,28},{28,24},{1,5},{5... | collective-permute-start | bytes 884744 | tf_op jit(solution)/shard_map/ppermute | solution.py:384
  49.0 25.1 %collective-permute-start.2 = (f32[512,192]{1,0:T(8,128)S(1)}, f32[512,192]{1,0:T(8,128)S(1)}, u32[]{:S(2)}, u32[]{:S(2)}) collective-permute-start(f32[512,192]{1,0:T(8,128)S(1)} %collective-permute-done.1.m2), channel_id=1, source_target_pairs={{0,1},{1,0},{2,3},{3,2},{4,5},{5,4},{6,7},{7,6},{8,9},{9,8},{10,11... | collective-permute-start | bytes 1179656 | tf_op jit(solution)/shard_map/ppermute | solution.py:380
  79.1 23.9 %collective-permute-start.13 = (f32[128,768]{1,0:T(8,128)S(1)}, f32[128,768]{1,0:T(8,128)S(1)}, u32[]{:S(2)}, u32[]{:S(2)}) collective-permute-start(f32[128,768]{1,0:T(8,128)S(1)} %get-tuple-element.87), channel_id=1, source_target_pairs={{0,1},{1,0},{2,3},{3,2},{4,5},{5,4},{6,7},{7,6},{8,9},{9,8},{10,11... | collective-permute-start | bytes 1179656 | tf_op jit(solution)/shard_map/ppermute | solution.py:380
  90.9 22.9 %collective-permute-start.15 = (f32[128,768]{1,0:T(8,128)S(1)}, f32[128,768]{1,0:T(8,128)S(1)}, u32[]{:S(2)}, u32[]{:S(2)}) collective-permute-start(f32[128,768]{1,0:T(8,128)S(1)} %add.74), channel_id=1, source_target_pairs={{0,2},{1,3},{2,0},{3,1},{4,6},{5,7},{6,4},{7,5},{8,10},{9,11},{10,... | collective-permute-start | bytes 1179656 | tf_op jit(solution)/shard_map/ppermute | solution.py:380
  113.9 21.5 %collective-permute-start.16 = (f32[128,768]{1,0:T(8,128)S(1)}, f32[128,768]{1,0:T(8,128)S(1)}, u32[]{:S(2)}, u32[]{:S(2)}) collective-permute-start(f32[128,768]{1,0:T(8,128)S(1)} %add_add_fusion.2.r0), channel_id=1, source_target_pairs={{0,1},{1,0},{2,3},{3,2},{4,5},{5,4},{6,7},{7,6},{8,9},{9,8},{10,11... | collective-permute-start | bytes 1179656 | tf_op jit(solution)/shard_map/ppermute | solution.py:380
  167.8 82.1 %collective-permute-start.19 = (f32[4,192,768]{2,1,0:T(8,128)S(1)}, f32[4,192,768]{2,1,0:T(8,128)S(1)}, u32[]{:S(2)}, u32[]{:S(2)}) collective-permute-start(f32[4,192,768]{2,1,0:T(8,128)S(1)} %get-tuple-element.97), channel_id=1, source_target_pairs={{0,4},{4,0},{8,12},{12,8},{16,20},{20,16},{24,28},{28,24},{1,5},{5... | collective-permute-start | bytes 7077896 | tf_op jit(solution)/shard_map/ppermute | solution.py:384
  177.9 36.5 %collective-permute-start.46 = (f32[4,4,24,768]{3,2,1,0:T(8,128)S(1)}, f32[4,4,24,768]{3,2,1,0:T(8,128)S(1)}, u32[]{:S(2)}, u32[]{:S(2)}) collective-permute-start(f32[4,4,24,768]{3,2,1,0:T(8,128)S(1)} %get-tuple-element.136), channel_id=1, source_target_pairs={{0,4},{4,0},{8,12},{12,8},{16,20},{20,16},{24,28},{28,24},{1,5},{5... | collective-permute-start | bytes 3538952 | tf_op jit(solution)/shard_map/ppermute | solution.py:384
  199.8 25.2 %collective-permute-start.36 = (f32[128,768]{1,0:T(8,128)S(1)}, f32[128,768]{1,0:T(8,128)S(1)}, u32[]{:S(2)}, u32[]{:S(2)}) collective-permute-start(f32[128,768]{1,0:T(8,128)S(1)} %get-tuple-element.120), channel_id=1, source_target_pairs={{0,1},{1,0},{2,3},{3,2},{4,5},{5,4},{6,7},{7,6},{8,9},{9,8},{10,11... | collective-permute-start | bytes 1179656 | tf_op jit(solution)/shard_map/ppermute | solution.py:380
  214.4 25.0 %collective-permute-start.42 = (f32[4,80,768]{2,1,0:T(8,128)S(1)}, f32[4,80,768]{2,1,0:T(8,128)S(1)}, u32[]{:S(2)}, u32[]{:S(2)}) collective-permute-start(f32[4,80,768]{2,1,0:T(8,128)S(1)} %get-tuple-element.129), channel_id=1, source_target_pairs={{0,4},{4,0},{8,12},{12,8},{16,20},{20,16},{24,28},{28,24},{1,5},{5... | collective-permute-start | bytes 2949128 | tf_op jit(solution)/shard_map/ppermute | solution.py:384
  230.6 19.6 %collective-permute-start.40 = (f32[128,768]{1,0:T(8,128)S(1)}, f32[128,768]{1,0:T(8,128)S(1)}, u32[]{:S(2)}, u32[]{:S(2)}) collective-permute-start(f32[128,768]{1,0:T(8,128)S(1)} %add_add_fusion.1.r0), channel_id=1, source_target_pairs={{0,2},{1,3},{2,0},{3,1},{4,6},{5,7},{6,4},{7,5},{8,10},{9,11},{10,... | collective-permute-start | bytes 1179656 | tf_op jit(solution)/shard_map/ppermute | solution.py:380
  253.9 42.7 %collective-permute-start.21 = (f32[192,768]{1,0:T(8,128)S(1)}, f32[192,768]{1,0:T(8,128)S(1)}, u32[]{:S(2)}, u32[]{:S(2)}) collective-permute-start(f32[192,768]{1,0:T(8,128)S(1)} %get-tuple-element.100), channel_id=1, source_target_pairs={{0,16},{4,20},{8,24},{12,28},{16,0},{20,4},{24,8},{28,12},{1,17},{... | collective-permute-start | bytes 1769480 | tf_op jit(solution)/shard_map/ppermute | solution.py:384
  257.5 39.1 %collective-permute-start.22 = (f32[192,768]{1,0:T(8,128)S(1)}, f32[192,768]{1,0:T(8,128)S(1)}, u32[]{:S(2)}, u32[]{:S(2)}) collective-permute-start(f32[192,768]{1,0:T(8,128)S(1)} %get-tuple-element.101), channel_id=1, source_target_pairs={{0,24},{4,28},{8,16},{12,20},{16,8},{20,12},{24,0},{28,4},{1,25},{... | collective-permute-start | bytes 1769480 | tf_op jit(solution)/shard_map/ppermute | solution.py:384
  259.7 37.2 %collective-permute-start.39 = (f32[128,768]{1,0:T(8,128)S(1)}, f32[128,768]{1,0:T(8,128)S(1)}, u32[]{:S(2)}, u32[]{:S(2)}) collective-permute-start(f32[128,768]{1,0:T(8,128)S(1)} %add_add_fusion.1.r0), channel_id=1, source_target_pairs={{0,1},{1,0},{2,3},{3,2},{4,5},{5,4},{6,7},{7,6},{8,9},{9,8},{10,11... | collective-permute-start | bytes 1179656 | tf_op jit(solution)/shard_map/ppermute | solution.py:380
  259.8 39.2 %collective-permute-start.41 = (f32[128,768]{1,0:T(8,128)S(1)}, f32[128,768]{1,0:T(8,128)S(1)}, u32[]{:S(2)}, u32[]{:S(2)}) collective-permute-start(f32[128,768]{1,0:T(8,128)S(1)} %collective-permute-done.40.r2), channel_id=1, source_target_pairs={{0,1},{1,0},{2,3},{3,2},{4,5},{5,4},{6,7},{7,6},{8,9},{9,8},{10,11... | collective-permute-start | bytes 1179656 | tf_op jit(solution)/shard_map/ppermute | solution.py:380
  270.8 29.6 %collective-permute-start.58 = (f32[104,768]{1,0:T(8,128)S(1)}, f32[104,768]{1,0:T(8,128)S(1)}, u32[]{:S(2)}, u32[]{:S(2)}) collective-permute-start(f32[104,768]{1,0:T(8,128)S(1)} %pad_maximum_fusion.1.refs_0_), channel_id=1, source_target_pairs={{0,24},{4,28},{8,16},{12,20},{16,8},{20,12},{24,0},{28,4},{1,25},{... | collective-permute-start | bytes 958472 | tf_op jit(solution)/shard_map/ppermute | solution.py:384
  296.8 32.9 %collective-permute-start.28 = (f32[240,768]{1,0:T(8,128)S(1)}, f32[240,768]{1,0:T(8,128)S(1)}, u32[]{:S(2)}, u32[]{:S(2)}) collective-permute-start(f32[240,768]{1,0:T(8,128)S(1)} %pad_maximum_fusion.refs_0_), channel_id=1, source_target_pairs={{0,24},{4,28},{8,16},{12,20},{16,8},{20,12},{24,0},{28,4},{1,25},{... | collective-permute-start | bytes 2211848 | tf_op jit(solution)/shard_map/ppermute | solution.py:384
  296.9 33.1 %collective-permute-start.26 = (f32[240,768]{1,0:T(8,128)S(1)}, f32[240,768]{1,0:T(8,128)S(1)}, u32[]{:S(2)}, u32[]{:S(2)}) collective-permute-start(f32[240,768]{1,0:T(8,128)S(1)} %pad_maximum_fusion.refs_0_), channel_id=1, source_target_pairs={{0,16},{4,20},{8,24},{12,28},{16,0},{20,4},{24,8},{28,12},{1,17},{... | collective-permute-start | bytes 2211848 | tf_op jit(solution)/shard_map/ppermute | solution.py:384
  299.0 31.2 %collective-permute-start.24 = (f32[240,768]{1,0:T(8,128)S(1)}, f32[240,768]{1,0:T(8,128)S(1)}, u32[]{:S(2)}, u32[]{:S(2)}) collective-permute-start(f32[240,768]{1,0:T(8,128)S(1)} %pad_maximum_fusion.refs_0_), channel_id=1, source_target_pairs={{0,8},{4,12},{8,0},{12,4},{16,24},{20,28},{24,16},{28,20},{1,9},{5... | collective-permute-start | bytes 2211848 | tf_op jit(solution)/shard_map/ppermute | solution.py:384
  300.5 27.5 %collective-permute-start.54 = (f32[104,768]{1,0:T(8,128)S(1)}, f32[104,768]{1,0:T(8,128)S(1)}, u32[]{:S(2)}, u32[]{:S(2)}) collective-permute-start(f32[104,768]{1,0:T(8,128)S(1)} %pad_maximum_fusion.1.refs_0_), channel_id=1, source_target_pairs={{0,8},{4,12},{8,0},{12,4},{16,24},{20,28},{24,16},{28,20},{1,9},{5... | collective-permute-start | bytes 958472 | tf_op jit(solution)/shard_map/ppermute | solution.py:384
  (58 other events, 852.3 us)

commit v2 on v1

--- a/solution.py
+++ b/solution.py
@@ -384,17 +384,8 @@
     return lax.ppermute(block, "dp", [(i, i ^ k) for i in range(n_dp)])
 
 
-def scatter_sum(parts):
-    far = swap(parts[3], 1)
-    across = swap(parts[2] + far, 2)
-    near = swap(parts[1], 1)
-    return parts[0], near, across
-
-
-def gather(block):
-    across = swap(block, 2)
-    near = swap(block, 1)
-    return block, near, across, swap(across, 1)
+def together(*items):
+    return lax.optimization_barrier(items)
 
 
 def rest_of_dp(block, n_dp):
@@ -404,21 +395,15 @@
     return lax.psum(block, "dp", axis_index_groups=groups)
 
 
-def dp_scatter(even, odd, n_dp):
+def dp_fold(even, odd, n_dp):
     other = swap_dp(odd, 1, n_dp)
     flat = even.shape[-2] if even.ndim == 3 else even.shape[1] * even.shape[2]
     even = even.reshape(4, flat, even.shape[-1])
     other = other.reshape(even.shape)
-    block = shape(*even.shape[1:])
-    parts = call(fold, [block] * 4, [even, other], moved=3 * even.size * 4)
-    total = parts[0]
-    for n in (1, 2, 3):
-        total = total + swap_dp(parts[n], 2 * n, n_dp)
-    return rest_of_dp(total, n_dp)
-
-
-def dp_gather(block, n_dp):
-    blocks = [block] + [swap_dp(block, 2 * n, n_dp) for n in (1, 2, 3)]
+    return call(fold, [shape(*even.shape[1:])] * 4, [even, other], moved=3 * even.size * 4)
+
+
+def with_other_core(blocks, n_dp):
     others = [swap_dp(item, 1, n_dp) for item in blocks]
     return [item for pair in zip(blocks, others) for item in pair]
 
@@ -458,14 +443,7 @@
 
         piece = cols // 8
         slice_own = lax.dynamic_slice_in_dim(w_out, group * piece, piece, 0).astype(f32)
-        slices = jnp.stack(gather(slice_own))
-        w_all = call(
-            join_w_out,
-            shape(4, cols, width, kind=bf16),
-            [ids] + dp_gather(slices, n_dp),
-            moved=4 * cols * width * 6,
-            scratch=[pltpu.VMEM((4, cols, width), f32)],
-        )
+        slices = [slice_own] + [swap(slice_own, n) for n in (1, 2, 3)]
 
         tok_x, q, k, v, probs, mixed_low, mixed = call(
             attend,
@@ -482,7 +460,19 @@
             flops=2 * slots * width * 3 * cols + 4 * slots * slots * cols,
             moved=slots * width * 4 + 3 * cols * width * 2 + heads * slots * slots * 2,
         )
-        mixed_all = gather(mixed)
+        mixed, *slices = together(mixed, *slices)
+        slices = jnp.stack(slices)
+        across, near = swap(mixed, 2), swap(mixed, 1)
+        w_blocks = [swap_dp(slices, 2 * n, n_dp) for n in (1, 2, 3)]
+        across, near, slices, *w_blocks = together(across, near, slices, *w_blocks)
+        mixed_all = [mixed, near, across, swap(across, 1)]
+        w_all = call(
+            join_w_out,
+            shape(4, cols, width, kind=bf16),
+            [ids] + with_other_core([slices] + w_blocks, n_dp),
+            moved=4 * cols * width * 6,
+            scratch=[pltpu.VMEM((4, cols, width), f32)],
+        )
         *parts, normed_low, upper, act, normal_own, inverse_own, resid_own = call(
             feed,
             [shape(rows, width)] * 4
@@ -499,11 +489,16 @@
             flops=2 * slots * width * (width + 2 * units),
             moved=4 * slots * width * 4 + 3 * width * units * 2,
         )
+        far = swap(parts[3], 1)
         slope = call(
             gelu_grad, shape(slots, units), [upper], moved=8 * slots * units, flops=slots * units
         )
-        own, near, across = scatter_sum(parts)
-        resid = gather(resid_own + own + near + across)
+        far, slope, part2, part1 = together(far, slope, parts[2], parts[1])
+        across, near = swap(part2 + far, 2), swap(part1, 1)
+        own = resid_own + parts[0] + near + across
+        across, near = swap(own, 2), swap(own, 1)
+        across, near = together(across, near)
+        resid = [own, near, across, swap(across, 1)]
         *parts, layer_out, own_pools, d_resid, resid_low, upper_low, side = call(
             finish,
             [shape(rows, width)] * 4
@@ -525,7 +520,7 @@
                 pltpu.VMEM((SENTS, width), f32),
             ],
         )
-        own, near, across = scatter_sum(parts)
+        far = swap(parts[3], 1)
         step = 2 * width // 8
         even, odd = call(
             ffn_grads,
@@ -535,15 +530,20 @@
             moved=4 * slots * width * 2 + 8 * width * units,
             scratch=[pltpu.VMEM((2 * width, width), f32)],
         )
-        ffn_sum = dp_scatter(even, odd, n_dp)
+        ffn = dp_fold(even, odd, n_dp)
+        far, part2, part1, *ffn = together(far, parts[2], parts[1], *ffn)
+        across, near = swap(part2 + far, 2), swap(part1, 1)
+        ffn[1], ffn[2] = swap_dp(ffn[1], 2, n_dp), swap_dp(ffn[2], 4, n_dp)
+        across, near, *ffn = together(across, near, *ffn)
         *sent, d_hidden, hidden_low = call(
             back_hidden,
             [shape(rows + 16, cols)] * 4 + [shape(rows, width), shape(rows, width, kind=bf16)],
-            [own, near, across, d_resid, normal_own, inverse_own, row(g_attn), w_all],
+            [parts[0], near, across, d_resid, normal_own, inverse_own, row(g_attn), w_all],
             flops=2 * rows * width * 4 * cols,
             moved=6 * rows * width * 4,
         )
         d_mixed = [sent[0]] + [swap(sent[n], n) for n in (1, 2, 3)]
+        ffn[3] = swap_dp(ffn[3], 6, n_dp)
         even, odd = call(
             out_grads,
             [shape(4, 4, piece, width)] * 2,
@@ -552,7 +552,10 @@
             moved=8 * 4 * cols * width,
             scratch=[pltpu.VMEM((4, cols, width), f32)],
         )
-        out_sum = dp_scatter(even, odd, n_dp)
+        out = dp_fold(even, odd, n_dp)
+        *joined, ffn_last = together(*d_mixed, *out, ffn[3])
+        d_mixed, out = joined[:4], joined[4:]
+        ffn_sum = rest_of_dp(ffn[0] + ffn[1] + ffn[2] + ffn_last, n_dp)
         *parts, grads, bias, shared = call(
             attend_back,
             [shape(rows, width)] * 4
@@ -566,6 +569,8 @@
                 pltpu.VMEM((slots, slots), bf16),
             ],
         )
+        far = swap(parts[3], 1)
+        out[1:] = [swap_dp(out[n], 2 * n, n_dp) for n in (1, 2, 3)]
         even, odd = call(
             qkv_grads,
             [shape(4, 3 * piece + 8, width)] * 2,
@@ -574,17 +579,34 @@
             moved=8 * 3 * cols * width,
             scratch=[pltpu.VMEM((3 * cols + 64, width), f32)],
         )
-        own, near, across = scatter_sum(parts)
-        qkv_sum = dp_scatter(even, odd, n_dp)
-        out_parts = out_sum.reshape(4, piece, width)
-        out_terms = scatter_sum([out_parts[n] for n in range(4)])
-        attn_own = jnp.concatenate([qkv_sum, sum(out_terms)])
-        attn_blocks = dp_gather(attn_own, n_dp)
-        own_rows = [own + near + across + d_hidden]
+        qkv = dp_fold(even, odd, n_dp)
+        ffn_own = jnp.concatenate([ffn_sum, own_pools])
+        far, part2, part1, ffn_own, *joined = together(
+            far, parts[2], parts[1], ffn_own, *qkv, *out
+        )
+        qkv, out = joined[:4], joined[4:]
+        across, near = swap(part2 + far, 2), swap(part1, 1)
+        ffn_x, ffn_y = swap_dp(ffn_own, 2, n_dp), swap_dp(ffn_own, 4, n_dp)
+        qkv[1], qkv[2] = swap_dp(qkv[1], 2, n_dp), swap_dp(qkv[2], 4, n_dp)
+        out_sum = rest_of_dp(sum(out), n_dp).reshape(4, piece, width)
+        across, near, ffn_x, ffn_y, out_sum, *qkv = together(
+            across, near, ffn_x, ffn_y, out_sum, *qkv
+        )
+        own = parts[0] + near + across + d_hidden
+        across, near = swap(own, 2), swap(own, 1)
+        ffn_d = swap_dp(ffn_own, 6, n_dp)
+        qkv[3] = swap_dp(qkv[3], 6, n_dp)
+        out_terms = [out_sum[0]] + [swap(out_sum[n], n) for n in (1, 2, 3)]
+        across, near, ffn_d, *joined = together(across, near, ffn_d, *qkv, *out_terms)
+        qkv, out_terms = joined[:4], joined[4:]
+        far = swap(across, 1)
+        attn_own = jnp.concatenate([rest_of_dp(sum(qkv), n_dp), sum(out_terms)])
+        attn_blocks = [attn_own] + [swap_dp(attn_own, 2 * n, n_dp) for n in (1, 2, 3)]
+        ffn_blocks = with_other_core([ffn_own, ffn_x, ffn_y, ffn_d], n_dp)
         d_tokens = call(
-            place, shape(slots, width), [ids, *gather(own_rows[0])], moved=8 * slots * width
-        )
-        ffn_blocks = dp_gather(jnp.concatenate([ffn_sum, own_pools]), n_dp)
+            place, shape(slots, width), [ids, own, near, across, far], moved=8 * slots * width
+        )
+        attn_blocks = with_other_core(attn_blocks, n_dp)
         wide = pool_grad.shape[1]
         d_w_up, d_w_down, pools = call(
             unpack_ffn,

time: 343 us -> 287 us (0.84)
  waiting for transfers between devices: 208 us -> 173 us
  starting transfers between devices: 85.3 us -> 64.7 us
    ppermute x27, waiting for transfers between devices: 130 us -> 110 us  [swap(): return lax.ppermute(block, 'tensor', swaps[k])]
    ppermute x27, starting transfers between devices: 59.8 us -> 40.9 us  [swap(): return lax.ppermute(block, 'tensor', swaps[k])]
    ppermute x33, waiting for transfers between devices: 78.2 us -> 63.1 us  [swap_dp(): return lax.ppermute(block, 'dp', [(i, i ^ k) for i in range(n_dp)])]
  transfers between devices with their start and end apart: 60 -> 60, of which waited for: 27 -> 33; matrix products, arithmetic and copies ran while one was open for 1% -> 1% of each run, Pallas kernels for 6% -> 4%
where the time goes in v2:
time: 287 us; the launch traced here: 286 us
  waiting for transfers between devices  173 us (60%)
  starting transfers between devices  64.7 us (23%)
  Pallas kernels  38.5 us (13%)
  local copies, waits for them, and re-layouts  7.44 us (3%)
    ppermute x27, waiting for transfers between devices, swap(): return lax.ppermute(block, 'tensor', swaps[k])  110 us
    ppermute x33, waiting for transfers between devices, swap_dp(): return lax.ppermute(block, 'dp', [(i, i ^ k) for i in range(n_dp)])  63.1 us
    ppermute x27, starting transfers between devices, swap(): return lax.ppermute(block, 'tensor', swaps[k])  40.9 us
    pallas_call x16, Pallas kernels, call(): pl.pallas_call(body, out_shape=outs, in_specs=specs, out_specs=jax.tree.m...  38.5 us
    ppermute x33, starting transfers between devices, swap_dp(): return lax.ppermute(block, 'dp', [(i, i ^ k) for i in range(n_dp)])  23.7 us
    unnamed x44, local copies, waits for them, and re-layouts  6.1 us
  transfers between devices with their start and end apart: 60, of which 33 were waited for; matrix products, arithmetic and copies ran while one was open for 1% of the time, Pallas kernels for 4%

profile of v2, /device:TPU:0, one launch (start us, length us, event | category | flops | bytes accessed | tf_op | source)
XLA Modules:
  0.0 286.2 jit_solution(12970630736580507342)
XLA Ops:
  1.5 5.1 %collective-permute-start.2 = (f32[24,768]{1,0:T(8,128)S(1)}, f32[24,768]{1,0:T(8,128)S(1)}, u32[]{:S(2)}, u32[]{:S(2)}) collective-permute-start(f32[24,768]{1,0:T(8,128)S(1)} %dynamic-slice_convert_fusion), channel_id=1, source_target_pairs={{0,3},{1,2},{2,1},{3,0},{4,7},{5,6},{6,5},{7,4},{8,11},{9,10},{10,... | collective-permute-start | bytes 221192 | tf_op jit(solution)/shard_map/ppermute | solution.py:380
  13.4 6.7 %shard_map.322 = (bf16[512,768]{1,0:T(8,128)(2,1)S(1)}, bf16[512,192]{1,0:T(8,128)(2,1)S(1)}, bf16[512,192]{1,0:T(8,128)(2,1)S(1)}, bf16[512,192]{1,0:T(8,128)(2...) custom-call(s32[2]{0:T(128)S(1)} %pad_add_fusion.ids.me, ...), custom_call_target="tpu_custom_call" | custom-call | flops 654311424 | bytes 4030464 | tf_op jit(solution)/shard_map/pallas_call | solution.py:64
  28.0 7.3 %collective-permute-done.7.refs_6_ = f32[4,24,768]{2,1,0:T(8,128)S(1)} collective-permute-done((f32[4,24,768]{2,1,0:T(8,128)S(1)}, f32[4,24,768]{2,1,0:T(8,128)S(1)}, u32[]{:S(2)}, u32[]{:S(2)}) %collective-permute-start.7) | collective-permute-done | bytes 294944 | tf_op jit(solution)/shard_map/ppermute | solution.py:384
  35.4 3.7 %collective-permute-done.6.refs_4_ = f32[4,24,768]{2,1,0:T(8,128)S(1)} collective-permute-done((f32[4,24,768]{2,1,0:T(8,128)S(1)}, f32[4,24,768]{2,1,0:T(8,128)S(1)}, u32[]{:S(2)}, u32[]{:S(2)}) %collective-permute-start.6) | collective-permute-done | bytes 294944 | tf_op jit(solution)/shard_map/ppermute | solution.py:384
  39.2 5.0 %collective-permute-done.4.m1 = f32[512,192]{1,0:T(8,128)S(1)} collective-permute-done((f32[512,192]{1,0:T(8,128)S(1)}, f32[512,192]{1,0:T(8,128)S(1)}, u32[]{:S(2)}, u32[]{:S(2)}) %collective-permute-start.4) | collective-permute-done | bytes 393248 | tf_op jit(solution)/shard_map/ppermute | solution.py:380
  50.5 7.0 %collective-permute-done.8.m3 = f32[512,192]{1,0:T(8,128)S(1)} collective-permute-done((f32[512,192]{1,0:T(8,128)S(1)}, f32[512,192]{1,0:T(8,128)S(1)}, u32[]{:S(2)}, u32[]{:S(2)}) %collective-permute-start.8) | collective-permute-done | bytes 393248 | tf_op jit(solution)/shard_map/ppermute | solution.py:380
  57.6 4.7 %shard_map.324 = (f32[128,768]{1,0:T(8,128)S(1)}, f32[128,768]{1,0:T(8,128)S(1)}, f32[128,768]{1,0:T(8,128)S(1)}, f32[128,768]{1,0:T(8,128)S(1)}, bf16[512,768]{...) custom-call(bf16[512,768]{1,0:T(8,128)(2,1)S(1)} %get-tuple-element., ...), custom_call_target="tpu_custom_call" | custom-call | flops 1811939328 | bytes 9830400 | tf_op jit(solution)/shard_map/pallas_call | solution.py:64
  64.4 8.2 %collective-permute-done.13 = f32[128,768]{1,0:T(8,128)S(1)} collective-permute-done((f32[128,768]{1,0:T(8,128)S(1)}, f32[128,768]{1,0:T(8,128)S(1)}, u32[]{:S(2)}, u32[]{:S(2)}) %collective-permute-start.13) | collective-permute-done | bytes 393248 | tf_op jit(solution)/shard_map/ppermute | solution.py:380
  74.6 13.0 %collective-permute-done.15 = f32[128,768]{1,0:T(8,128)S(1)} collective-permute-done((f32[128,768]{1,0:T(8,128)S(1)}, f32[128,768]{1,0:T(8,128)S(1)}, u32[]{:S(2)}, u32[]{:S(2)}) %collective-permute-start.15) | collective-permute-done | bytes 393248 | tf_op jit(solution)/shard_map/ppermute | solution.py:380
  91.3 13.2 %collective-permute-done.17.r1 = f32[128,768]{1,0:T(8,128)S(1)} collective-permute-done((f32[128,768]{1,0:T(8,128)S(1)}, f32[128,768]{1,0:T(8,128)S(1)}, u32[]{:S(2)}, u32[]{:S(2)}) %collective-permute-start.17) | collective-permute-done | bytes 393248 | tf_op jit(solution)/shard_map/ppermute | solution.py:380
  106.5 8.4 %collective-permute-done.18.r3 = f32[128,768]{1,0:T(8,128)S(1)} collective-permute-done((f32[128,768]{1,0:T(8,128)S(1)}, f32[128,768]{1,0:T(8,128)S(1)}, u32[]{:S(2)}, u32[]{:S(2)}) %collective-permute-start.18) | collective-permute-done | bytes 393248 | tf_op jit(solution)/shard_map/ppermute | solution.py:380
  114.9 8.6 %shard_map.326 = (f32[128,768]{1,0:T(8,128)S(1)}, f32[128,768]{1,0:T(8,128)S(1)}, f32[128,768]{1,0:T(8,128)S(1)}, f32[128,768]{1,0:T(8,128)S(1)}, bf16[512,768]{...) custom-call(s32[2]{0:T(128)S(1)} %pad_add_fusion.ids.me, ...), custom_call_target="tpu_custom_call" | custom-call | flops 1207959552 | bytes 9437184 | tf_op jit(solution)/shard_map/pallas_call | solution.py:64
  125.9 4.4 %collective-permute-done.20.theirs = f32[4,192,768]{2,1,0:T(8,128)S(1)} collective-permute-done((f32[4,192,768]{2,1,0:T(8,128)S(1)}, f32[4,192,768]{2,1,0:T(8,128)S(1)}, u32[]{:S(2)}, u32[]{:S(2)}) %collective-permute-start.20) | collective-permute-done | bytes 2359328 | tf_op jit(solution)/shard_map/ppermute | solution.py:384
  130.6 6.8 %collective-permute-done.19 = f32[128,768]{1,0:T(8,128)S(1)} collective-permute-done((f32[128,768]{1,0:T(8,128)S(1)}, f32[128,768]{1,0:T(8,128)S(1)}, u32[]{:S(2)}, u32[]{:S(2)}) %collective-permute-start.19) | collective-permute-done | bytes 393248 | tf_op jit(solution)/shard_map/ppermute | solution.py:380
  143.3 16.5 %collective-permute-done.21.across = f32[128,768]{1,0:T(8,128)S(1)} collective-permute-done((f32[128,768]{1,0:T(8,128)S(1)}, f32[128,768]{1,0:T(8,128)S(1)}, u32[]{:S(2)}, u32[]{:S(2)}) %collective-permute-start.21) | collective-permute-done | bytes 393248 | tf_op jit(solution)/shard_map/ppermute | solution.py:380
  167.0 3.7 %collective-permute-done.25.e1 = f32[144,192]{1,0:T(8,128)S(1)} collective-permute-done((f32[144,192]{1,0:T(8,128)S(1)}, f32[144,192]{1,0:T(8,128)S(1)}, u32[]{:S(2)}, u32[]{:S(2)}) %collective-permute-start.25) | collective-permute-done | bytes 110624 | tf_op jit(solution)/shard_map/ppermute | solution.py:380
  170.7 5.9 %collective-permute-done.26.e2 = f32[144,192]{1,0:T(8,128)S(1)} collective-permute-done((f32[144,192]{1,0:T(8,128)S(1)}, f32[144,192]{1,0:T(8,128)S(1)}, u32[]{:S(2)}, u32[]{:S(2)}) %collective-permute-start.26) | collective-permute-done | bytes 110624 | tf_op jit(solution)/shard_map/ppermute | solution.py:380
  188.4 5.2 %collective-permute-done.32 = f32[96,768]{1,0:T(8,128)S(1)} collective-permute-done((f32[96,768]{1,0:T(8,128)S(1)}, f32[96,768]{1,0:T(8,128)S(1)}, u32[]{:S(2)}, u32[]{:S(2)}) %collective-permute-start.32) | collective-permute-done | bytes 294944 | tf_op jit(solution)/shard_map/ppermute | solution.py:384
  193.6 6.1 %collective-permute-done.33 = f32[96,768]{1,0:T(8,128)S(1)} collective-permute-done((f32[96,768]{1,0:T(8,128)S(1)}, f32[96,768]{1,0:T(8,128)S(1)}, u32[]{:S(2)}, u32[]{:S(2)}) %collective-permute-start.33) | collective-permute-done | bytes 294944 | tf_op jit(solution)/shard_map/ppermute | solution.py:384
  206.1 17.6 %collective-permute-done.40 = f32[80,768]{1,0:T(8,128)S(1)} collective-permute-done((f32[80,768]{1,0:T(8,128)S(1)}, f32[80,768]{1,0:T(8,128)S(1)}, u32[]{:S(2)}, u32[]{:S(2)}) %collective-permute-start.40) | collective-permute-done | bytes 245792 | tf_op jit(solution)/shard_map/ppermute | solution.py:384
  227.1 6.1 %collective-permute-done.37 = f32[128,768]{1,0:T(8,128)S(1)} collective-permute-done((f32[128,768]{1,0:T(8,128)S(1)}, f32[128,768]{1,0:T(8,128)S(1)}, u32[]{:S(2)}, u32[]{:S(2)}) %collective-permute-start.37) | collective-permute-done | bytes 393248 | tf_op jit(solution)/shard_map/ppermute | solution.py:380
  239.4 6.0 %collective-permute-done.46.refs_6_ = f32[240,768]{1,0:T(8,128)S(1)} collective-permute-done((f32[240,768]{1,0:T(8,128)S(1)}, f32[240,768]{1,0:T(8,128)S(1)}, u32[]{:S(2)}, u32[]{:S(2)}) %collective-permute-start.46) | collective-permute-done | bytes 737312 | tf_op jit(solution)/shard_map/ppermute | solution.py:384
  246.4 8.4 %collective-permute-done.50 = f32[24,768]{1,0:T(8,128)S(1)} collective-permute-done((f32[24,768]{1,0:T(8,128)S(1)}, f32[24,768]{1,0:T(8,128)S(1)}, u32[]{:S(2)}, u32[]{:S(2)}) %collective-permute-start.50) | collective-permute-done | bytes 73760 | tf_op jit(solution)/shard_map/ppermute | solution.py:380
  254.9 3.6 %collective-permute-start.48 = (f32[24,768]{1,0:T(8,128)S(1)}, f32[24,768]{1,0:T(8,128)S(1)}, u32[]{:S(2)}, u32[]{:S(2)}) collective-permute-start(f32[24,768]{1,0:T(8,128)S(1)} %get-tuple-element.299), channel_id=1, source_target_pairs={{0,1},{1,0},{2,3},{3,2},{4,5},{5,4},{6,7},{7,6},{8,9},{9,8},{10,11... | collective-permute-start | bytes 221192 | tf_op jit(solution)/shard_map/ppermute | solution.py:380
  (180 shorter events, 103.8 us)
Async XLA Ops:
  1.5 18.5 %collective-permute-start.2 = (f32[24,768]{1,0:T(8,128)S(1)}, f32[24,768]{1,0:T(8,128)S(1)}, u32[]{:S(2)}, u32[]{:S(2)}) collective-permute-start(f32[24,768]{1,0:T(8,128)S(1)} %dynamic-slice_convert_fusion), channel_id=1, source_target_pairs={{0,3},{1,2},{2,1},{3,0},{4,7},{5,6},{6,5},{7,4},{8,11},{9,10},{10,... | collective-permute-start | bytes 221192 | tf_op jit(solution)/shard_map/ppermute | solution.py:380
  20.1 24.2 %collective-permute-start.4 = (f32[512,192]{1,0:T(8,128)S(1)}, f32[512,192]{1,0:T(8,128)S(1)}, u32[]{:S(2)}, u32[]{:S(2)}) collective-permute-start(f32[512,192]{1,0:T(8,128)S(1)} %get-tuple-element.156.m0), channel_id=1, source_target_pairs={{0,1},{1,0},{2,3},{3,2},{4,5},{5,4},{6,7},{7,6},{8,9},{9,8},{10,11... | collective-permute-start | bytes 1179656 | tf_op jit(solution)/shard_map/ppermute | solution.py:380
  21.5 25.1 %collective-permute-start.3 = (f32[512,192]{1,0:T(8,128)S(1)}, f32[512,192]{1,0:T(8,128)S(1)}, u32[]{:S(2)}, u32[]{:S(2)}) collective-permute-start(f32[512,192]{1,0:T(8,128)S(1)} %get-tuple-element.156.m0), channel_id=1, source_target_pairs={{0,2},{1,3},{2,0},{3,1},{4,6},{5,7},{6,4},{7,5},{8,10},{9,11},{10,... | collective-permute-start | bytes 1179656 | tf_op jit(solution)/shard_map/ppermute | solution.py:380
  72.7 14.9 %collective-permute-start.15 = (f32[128,768]{1,0:T(8,128)S(1)}, f32[128,768]{1,0:T(8,128)S(1)}, u32[]{:S(2)}, u32[]{:S(2)}) collective-permute-start(f32[128,768]{1,0:T(8,128)S(1)} %add.74), channel_id=1, source_target_pairs={{0,2},{1,3},{2,0},{3,1},{4,6},{5,7},{6,4},{7,5},{8,10},{9,11},{10,... | collective-permute-start | bytes 1179656 | tf_op jit(solution)/shard_map/ppermute | solution.py:380
  72.8 14.8 %collective-permute-start.14 = (f32[128,768]{1,0:T(8,128)S(1)}, f32[128,768]{1,0:T(8,128)S(1)}, u32[]{:S(2)}, u32[]{:S(2)}) collective-permute-start(f32[128,768]{1,0:T(8,128)S(1)} %get-tuple-element.173), channel_id=1, source_target_pairs={{0,1},{1,0},{2,3},{3,2},{4,5},{5,4},{6,7},{7,6},{8,9},{9,8},{10,11... | collective-permute-start | bytes 1179656 | tf_op jit(solution)/shard_map/ppermute | solution.py:380
  87.7 16.8 %collective-permute-start.17 = (f32[128,768]{1,0:T(8,128)S(1)}, f32[128,768]{1,0:T(8,128)S(1)}, u32[]{:S(2)}, u32[]{:S(2)}) collective-permute-start(f32[128,768]{1,0:T(8,128)S(1)} %add_add_fusion.2.r0), channel_id=1, source_target_pairs={{0,1},{1,0},{2,3},{3,2},{4,5},{5,4},{6,7},{7,6},{8,9},{9,8},{10,11... | collective-permute-start | bytes 1179656 | tf_op jit(solution)/shard_map/ppermute | solution.py:380
  90.2 16.3 %collective-permute-start.16 = (f32[128,768]{1,0:T(8,128)S(1)}, f32[128,768]{1,0:T(8,128)S(1)}, u32[]{:S(2)}, u32[]{:S(2)}) collective-permute-start(f32[128,768]{1,0:T(8,128)S(1)} %add_add_fusion.2.r0), channel_id=1, source_target_pairs={{0,2},{1,3},{2,0},{3,1},{4,6},{5,7},{6,4},{7,5},{8,10},{9,11},{10,... | collective-permute-start | bytes 1179656 | tf_op jit(solution)/shard_map/ppermute | solution.py:380
  137.3 22.4 %collective-permute-start.23 = (f32[192,768]{1,0:T(8,128)S(1)}, f32[192,768]{1,0:T(8,128)S(1)}, u32[]{:S(2)}, u32[]{:S(2)}) collective-permute-start(f32[192,768]{1,0:T(8,128)S(1)} %get-tuple-element.198), channel_id=1, source_target_pairs={{0,8},{4,12},{8,0},{12,4},{16,24},{20,28},{24,16},{28,20},{1,9},{5... | collective-permute-start | bytes 1769480 | tf_op jit(solution)/shard_map/ppermute | solution.py:384
  138.9 20.9 %collective-permute-start.24 = (f32[192,768]{1,0:T(8,128)S(1)}, f32[192,768]{1,0:T(8,128)S(1)}, u32[]{:S(2)}, u32[]{:S(2)}) collective-permute-start(f32[192,768]{1,0:T(8,128)S(1)} %get-tuple-element.199), channel_id=1, source_target_pairs={{0,16},{4,20},{8,24},{12,28},{16,0},{20,4},{24,8},{28,12},{1,17},{... | collective-permute-start | bytes 1769480 | tf_op jit(solution)/shard_map/ppermute | solution.py:384
  140.4 19.4 %collective-permute-start.21 = (f32[128,768]{1,0:T(8,128)S(1)}, f32[128,768]{1,0:T(8,128)S(1)}, u32[]{:S(2)}, u32[]{:S(2)}) collective-permute-start(f32[128,768]{1,0:T(8,128)S(1)} %add.76), channel_id=1, source_target_pairs={{0,2},{1,3},{2,0},{3,1},{4,6},{5,7},{6,4},{7,5},{8,10},{9,11},{10,... | collective-permute-start | bytes 1179656 | tf_op jit(solution)/shard_map/ppermute | solution.py:380
  141.5 18.3 %collective-permute-start.22 = (f32[128,768]{1,0:T(8,128)S(1)}, f32[128,768]{1,0:T(8,128)S(1)}, u32[]{:S(2)}, u32[]{:S(2)}) collective-permute-start(f32[128,768]{1,0:T(8,128)S(1)} %get-tuple-element.196), channel_id=1, source_target_pairs={{0,1},{1,0},{2,3},{3,2},{4,5},{5,4},{6,7},{7,6},{8,9},{9,8},{10,11... | collective-permute-start | bytes 1179656 | tf_op jit(solution)/shard_map/ppermute | solution.py:380
  161.9 16.6 %collective-permute-start.29 = (f32[192,768]{1,0:T(8,128)S(1)}, f32[192,768]{1,0:T(8,128)S(1)}, u32[]{:S(2)}, u32[]{:S(2)}) collective-permute-start(f32[192,768]{1,0:T(8,128)S(1)} %get-tuple-element.217), channel_id=1, source_target_pairs={{0,24},{4,28},{8,16},{12,20},{16,8},{20,12},{24,0},{28,4},{1,25},{... | collective-permute-start | bytes 1769480 | tf_op jit(solution)/shard_map/ppermute | solution.py:384
  184.3 15.4 %collective-permute-start.33 = (f32[96,768]{1,0:T(8,128)S(1)}, f32[96,768]{1,0:T(8,128)S(1)}, u32[]{:S(2)}, u32[]{:S(2)}) collective-permute-start(f32[96,768]{1,0:T(8,128)S(1)} %get-tuple-element.246), channel_id=1, source_target_pairs={{0,16},{4,20},{8,24},{12,28},{16,0},{20,4},{24,8},{28,12},{1,17},{... | collective-permute-start | bytes 884744 | tf_op jit(solution)/shard_map/ppermute | solution.py:384
  184.8 14.8 %collective-permute-start.34 = (f32[96,768]{1,0:T(8,128)S(1)}, f32[96,768]{1,0:T(8,128)S(1)}, u32[]{:S(2)}, u32[]{:S(2)}) collective-permute-start(f32[96,768]{1,0:T(8,128)S(1)} %get-tuple-element.247), channel_id=1, source_target_pairs={{0,24},{4,28},{8,16},{12,20},{16,8},{20,12},{24,0},{28,4},{1,25},{... | collective-permute-start | bytes 884744 | tf_op jit(solution)/shard_map/ppermute | solution.py:384
  199.7 33.6 %collective-permute-start.39 = (f32[240,768]{1,0:T(8,128)S(1)}, f32[240,768]{1,0:T(8,128)S(1)}, u32[]{:S(2)}, u32[]{:S(2)}) collective-permute-start(f32[240,768]{1,0:T(8,128)S(1)} %pad_maximum_fusion.refs_0_), channel_id=1, source_target_pairs={{0,16},{4,20},{8,24},{12,28},{16,0},{20,4},{24,8},{28,12},{1,17},{... | collective-permute-start | bytes 2211848 | tf_op jit(solution)/shard_map/ppermute | solution.py:384
  200.8 32.4 %collective-permute-start.38 = (f32[240,768]{1,0:T(8,128)S(1)}, f32[240,768]{1,0:T(8,128)S(1)}, u32[]{:S(2)}, u32[]{:S(2)}) collective-permute-start(f32[240,768]{1,0:T(8,128)S(1)} %pad_maximum_fusion.refs_0_), channel_id=1, source_target_pairs={{0,8},{4,12},{8,0},{12,4},{16,24},{20,28},{24,16},{28,20},{1,9},{5... | collective-permute-start | bytes 2211848 | tf_op jit(solution)/shard_map/ppermute | solution.py:384
  201.7 22.1 %collective-permute-start.40 = (f32[80,768]{1,0:T(8,128)S(1)}, f32[80,768]{1,0:T(8,128)S(1)}, u32[]{:S(2)}, u32[]{:S(2)}) collective-permute-start(f32[80,768]{1,0:T(8,128)S(1)} %get-tuple-element.257), channel_id=1, source_target_pairs={{0,8},{4,12},{8,0},{12,4},{16,24},{20,28},{24,16},{28,20},{1,9},{5... | collective-permute-start | bytes 737288 | tf_op jit(solution)/shard_map/ppermute | solution.py:384
  202.9 22.7 %collective-permute-start.41 = (f32[80,768]{1,0:T(8,128)S(1)}, f32[80,768]{1,0:T(8,128)S(1)}, u32[]{:S(2)}, u32[]{:S(2)}) collective-permute-start(f32[80,768]{1,0:T(8,128)S(1)} %get-tuple-element.258), channel_id=1, source_target_pairs={{0,16},{4,20},{8,24},{12,28},{16,0},{20,4},{24,8},{28,12},{1,17},{... | collective-permute-start | bytes 737288 | tf_op jit(solution)/shard_map/ppermute | solution.py:384
  203.8 23.4 %collective-permute-start.36 = (f32[128,768]{1,0:T(8,128)S(1)}, f32[128,768]{1,0:T(8,128)S(1)}, u32[]{:S(2)}, u32[]{:S(2)}) collective-permute-start(f32[128,768]{1,0:T(8,128)S(1)} %add.80), channel_id=1, source_target_pairs={{0,2},{1,3},{2,0},{3,1},{4,6},{5,7},{6,4},{7,5},{8,10},{9,11},{10,... | collective-permute-start | bytes 1179656 | tf_op jit(solution)/shard_map/ppermute | solution.py:380
  225.6 19.8 %collective-permute-start.46 = (f32[240,768]{1,0:T(8,128)S(1)}, f32[240,768]{1,0:T(8,128)S(1)}, u32[]{:S(2)}, u32[]{:S(2)}) collective-permute-start(f32[240,768]{1,0:T(8,128)S(1)} %pad_maximum_fusion.refs_0_), channel_id=1, source_target_pairs={{0,24},{4,28},{8,16},{12,20},{16,8},{20,12},{24,0},{28,4},{1,25},{... | collective-permute-start | bytes 2211848 | tf_op jit(solution)/shard_map/ppermute | solution.py:384
  233.4 28.2 %collective-permute-start.45 = (f32[128,768]{1,0:T(8,128)S(1)}, f32[128,768]{1,0:T(8,128)S(1)}, u32[]{:S(2)}, u32[]{:S(2)}) collective-permute-start(f32[128,768]{1,0:T(8,128)S(1)} %add_add_fusion.1.r0), channel_id=1, source_target_pairs={{0,1},{1,0},{2,3},{3,2},{4,5},{5,4},{6,7},{7,6},{8,9},{9,8},{10,11... | collective-permute-start | bytes 1179656 | tf_op jit(solution)/shard_map/ppermute | solution.py:380
  234.9 26.6 %collective-permute-start.44 = (f32[128,768]{1,0:T(8,128)S(1)}, f32[128,768]{1,0:T(8,128)S(1)}, u32[]{:S(2)}, u32[]{:S(2)}) collective-permute-start(f32[128,768]{1,0:T(8,128)S(1)} %add_add_fusion.1.r0), channel_id=1, source_target_pairs={{0,2},{1,3},{2,0},{3,1},{4,6},{5,7},{6,4},{7,5},{8,10},{9,11},{10,... | collective-permute-start | bytes 1179656 | tf_op jit(solution)/shard_map/ppermute | solution.py:380
  236.0 25.6 %collective-permute-start.47 = (f32[80,768]{1,0:T(8,128)S(1)}, f32[80,768]{1,0:T(8,128)S(1)}, u32[]{:S(2)}, u32[]{:S(2)}) collective-permute-start(f32[80,768]{1,0:T(8,128)S(1)} %get-tuple-element.269), channel_id=1, source_target_pairs={{0,24},{4,28},{8,16},{12,20},{16,8},{20,12},{24,0},{28,4},{1,25},{... | collective-permute-start | bytes 737288 | tf_op jit(solution)/shard_map/ppermute | solution.py:384
  237.5 17.4 %collective-permute-start.50 = (f32[24,768]{1,0:T(8,128)S(1)}, f32[24,768]{1,0:T(8,128)S(1)}, u32[]{:S(2)}, u32[]{:S(2)}) collective-permute-start(f32[24,768]{1,0:T(8,128)S(1)} %get-tuple-element.297), channel_id=1, source_target_pairs={{0,3},{1,2},{2,1},{3,0},{4,7},{5,6},{6,5},{7,4},{8,11},{9,10},{10,... | collective-permute-start | bytes 221192 | tf_op jit(solution)/shard_map/ppermute | solution.py:380
  (58 other events, 804.4 us)

commit v3 on v2

--- a/solution.py
+++ b/solution.py
@@ -14,6 +14,7 @@
 highest = lax.Precision.HIGHEST
 f32 = jnp.float32
 bf16 = jnp.bfloat16
+order = 10**9
 swaps = {k: [(i, i ^ k) for i in range(4)] for k in (1, 2, 3)}
 
 
@@ -56,11 +57,11 @@
     return jax.ShapeDtypeStruct(extent, kind)
 
 
-def call(body, outs, ins, flops=0, moved=0, scratch=(), limit=32):
+def call(body, outs, ins, flops=0, moved=0, scratch=(), limit=32, raw=0):
     specs = [
         pl.BlockSpec(memory_space=pltpu.SMEM if item.dtype == jnp.int32 else pltpu.VMEM)
-        for item in ins
-    ]
+        for item in ins[: len(ins) - raw]
+    ] + [pl.BlockSpec(memory_space=pltpu.HBM)] * raw
     return pl.pallas_call(
         body,
         out_shape=outs,
@@ -90,16 +91,57 @@
     return ((at // rows) ^ me) * rows + at % rows
 
 
-def attend(ids, lens, tok, wq, wk, wv, bq, bv, tok_x, q_out, k_out, v_out, probs_out, low_out, wide_out):
+def packed_rows(rows, cols):
+    return rows * (cols // 128) + (rows // 2 if cols % 128 else 0)
+
+
+def pack_into(out, block):
+    rows, cols = block.shape
+    full = cols // 128
+    for n in range(full):
+        out[n * rows : (n + 1) * rows, :] = block[:, n * 128 : (n + 1) * 128]
+    if cols % 128:
+        half = rows // 2
+        out[full * rows : full * rows + half, :HDIM] = block[:half, full * 128 :]
+        out[full * rows : full * rows + half, HDIM:] = block[half:, full * 128 :]
+
+
+def packed_parts(block, cols, slots, start, rows):
+    full = cols // 128
+    for n in range(full):
+        yield n * 128, block[n * slots + start : n * slots + start + rows, :]
+    if cols % 128:
+        half = slots // 2
+        side = start // half
+        at = full * slots + start - side * half
+        yield full * 128, block[at : at + rows, side * HDIM : (side + 1) * HDIM]
+
+
+def attend(ids, lengths, tok, wq_in, wk_in, wv_in, bq_in, bv_in, *refs):
+    tok_x, q_out, k_out, v_out, probs_out, packed, low, wq, wk, wv, bq, bv, lens, sems = refs
     me = ids[0]
     slots, cols = q_out.shape
     rows = slots // 4
-    for j in range(4):
-        tok_x[j * rows : (j + 1) * rows, :] = tok[chunk(me, j, rows), :]
+    moves = [
+        (lengths, lens),
+        (wk_in, wk),
+        *[(tok.at[chunk(me, j, rows), :], tok_x.at[j * rows : (j + 1) * rows, :]) for j in range(4)],
+        (wv_in, wv),
+        (bv_in, bv),
+        (wq_in, wq),
+        (bq_in, bq),
+    ]
+    moves = [pltpu.make_async_copy(a, b, sems.at[n]) for n, (a, b) in enumerate(moves)]
+    for move in moves:
+        move.start()
+    for move in moves[:6]:
+        move.wait()
     t = tok_x[...]
+    k_out[...] = nt(t, wk[...]).astype(bf16)
+    for move in moves[6:]:
+        move.wait()
+    v_out[...] = (nt(t, wv[...]) + bv[...]).astype(bf16)
     q_out[...] = (nt(t, wq[...]) + bq[...]).astype(bf16)
-    k_out[...] = nt(t, wk[...]).astype(bf16)
-    v_out[...] = (nt(t, wv[...]) + bv[...]).astype(bf16)
     seg_row = segment_of(lens, row_places(me, (1, slots), 1, rows))
     seg_col = segment_of(lens, row_places(me, (slots, 1), 0, rows))
     scale = HDIM**-0.5
@@ -112,8 +154,8 @@
             e = jnp.exp(s - jnp.max(s, axis=-1, keepdims=True))
             p = (e * (1.0 / jnp.sum(e, axis=-1, keepdims=True))).astype(bf16)
             probs_out[h, at, :] = p
-            low_out[at, lane] = nn(p, v_out[:, lane]).astype(bf16)
-        wide_out[at, :] = low_out[at, :].astype(f32)
+            low[at, lane] = nn(p, v_out[:, lane]).astype(bf16)
+    pack_into(packed, low[...].astype(f32))
 
 
 def join_w_out(ids, *refs):
@@ -134,45 +176,74 @@
         out[r : r + rows, :] = cdf + u * (0.3989422804014327 * jnp.exp(-0.5 * u * u))
 
 
-def feed(tok_x, m0, m1, m2, m3, w_all, b_out, g_attn, b_attn, w_up, b_up, w_down, b_down, *outs):
-    p0, p1, p2, p3, low, upper, act, normal_own, inverse_own, resid_own = outs
-    parts = (p0, p1, p2, p3)
+def feed_chunk(j, tok_x, mixed, w_all, b_out, g_attn, b_attn, w_up, b_up, w_down, low, upper, act, part):
+    rows = part.shape[0]
+    at = slice(j * rows, (j + 1) * rows)
+    total = tok_x[at, :].astype(f32) + b_out[...]
+    for k in range(4):
+        for col, block in packed_parts(mixed[k], w_all.shape[1], 4 * rows, (j ^ k) * rows, rows):
+            total = total + nn(block.astype(bf16), w_all[k, col : col + block.shape[1], :])
+    normal, inverse = norm_stats(total)
+    normed = normal * g_attn[...] + b_attn[...]
+    low[...] = normed.astype(bf16)
+    upper[...] = nn(low[...], w_up[...]) + b_up[...]
+    half = rows // 2
+    for r in (0, half):
+        u = upper[r : r + half, :]
+        cdf = 0.5 * (1.0 + lax.erf(u * 0.7071067811865476))
+        act[r : r + half, :] = (u * cdf).astype(bf16)
+    part[...] = nn(act[...], w_down[...])
+    return normed, normal, inverse
+
+
+def feed_first(tok_x, m0, m1, m2, m3, w_all, b_out, g_attn, b_attn, w_up, b_up, w_down, *outs):
+    part, low, upper, act = outs
     mixed = (m0, m1, m2, m3)
+    ins = (tok_x, mixed, w_all, b_out, g_attn, b_attn, w_up, b_up, w_down)
+    feed_chunk(3, *ins, low, upper, act, part)
+
+
+def feed_rest(tok_x, m0, m1, m2, m3, w_all, b_out, g_attn, b_attn, w_up, b_up, w_down, b_down, *refs):
+    (low3, upper3, act3), outs = refs[:3], refs[3:]
+    p0, p1, p2, low, upper, act, normal_own, inverse_own, resid_own = outs
+    parts = (p0, p1, p2)
+    mixed = (m0, m1, m2, m3)
+    ins = (tok_x, mixed, w_all, b_out, g_attn, b_attn, w_up, b_up, w_down)
     rows = p0.shape[0]
-    for j in (3, 2, 1, 0):
+    for full, piece in ((low, low3), (upper, upper3), (act, act3)):
+        full[3 * rows :, :] = piece[...]
+    for j in (2, 1, 0):
         at = slice(j * rows, (j + 1) * rows)
-        total = tok_x[at, :].astype(f32) + b_out[...]
-        for k in range(4):
-            i = j ^ k
-            total = total + nn(mixed[k][i * rows : (i + 1) * rows, :].astype(bf16), w_all[k])
-        normal, inverse = norm_stats(total)
-        normed = normal * g_attn[...] + b_attn[...]
-        low[at, :] = normed.astype(bf16)
-        up = nn(low[at, :], w_up[...]) + b_up[...]
-        upper[at, :] = up
-        half = rows // 2
-        for r in (0, half):
-            u = upper[j * rows + r : j * rows + r + half, :]
-            cdf = 0.5 * (1.0 + lax.erf(u * 0.7071067811865476))
-            act[j * rows + r : j * rows + r + half, :] = (u * cdf).astype(bf16)
-        parts[j][...] = nn(act[at, :], w_down[...])
-        if j == 0:
-            normal_own[...] = normal
-            inverse_own[...] = jnp.broadcast_to(inverse, inverse_own.shape)
-            resid_own[...] = normed + b_down[...]
-
-
-def finish(ids, lens, r0, r1, r2, r3, g_ffn, b_ffn, out_grad, pool_grad, grad_of, w_down, w_up, *refs):
-    outs, (normal_ref, inverse_ref, pooled_grad) = refs[:-3], refs[-3:]
-    p0, p1, p2, p3, layer_out, pools, d_own, low_out, up_out, side = outs
+        views = (low.at[at, :], upper.at[at, :], act.at[at, :], parts[j])
+        normed, normal, inverse = feed_chunk(j, *ins, *views)
+    normal_own[...] = normal
+    inverse_own[...] = jnp.broadcast_to(inverse, inverse_own.shape)
+    resid_own[...] = normed + b_down[...]
+
+
+def finish_chunk(seg, normal, inverse, gain, spread, out_grad, grad_of, w_down, w_up, low, up, part):
+    slot_row = lax.broadcasted_iota(jnp.int32, (1, SENTS), 1)
+    belongs = jnp.where(seg == slot_row, 1.0, 0.0)
+    d_final = out_grad.astype(f32) + nn(belongs, spread, highest)
+    d_resid = norm_back(d_final * gain, normal, inverse)
+    low[...] = d_resid.astype(bf16)
+    d_upper = nt(low[...], w_down[...]) * grad_of
+    up[...] = d_upper.astype(bf16)
+    part[...] = nt(up[...], w_up[...])
+    return d_resid, [col_sum(d_final), col_sum(d_final * normal), col_sum(d_resid), col_sum(d_upper)]
+
+
+def finish_first(
+    ids, lens, r0, r1, r2, r3, g_ffn, b_ffn, out_grad, pool_grad, grad_of, w_down, w_up, *refs
+):
+    outs, (pooled_grad,) = refs[:-1], refs[-1:]
+    part, layer_out, pools, normal_ref, inverse_ref, spread_out, low, up, side = outs
     me = ids[0]
-    parts = (p0, p1, p2, p3)
     rows, width = r0.shape
     gain, shift = g_ffn[...], b_ffn[...]
     seg_row = segment_of(lens, row_places(me, (1, 4 * rows), 1, rows))
     seg_col = segment_of(lens, row_places(me, (4 * rows, 1), 0, rows))
     slot_col = lax.broadcasted_iota(jnp.int32, (SENTS, 1), 0)
-    slot_row = lax.broadcasted_iota(jnp.int32, (1, SENTS), 1)
     pooled = jnp.zeros((SENTS, width), f32)
     for j, block in enumerate((r0, r1, r2, r3)):
         at = slice(j * rows, (j + 1) * rows)
@@ -202,31 +273,59 @@
     rest = offset % width
     pools[2 * SENTS :, rest:] = jnp.zeros((SENTS, width - rest), f32)
     spread = pooled_grad[...] / denom
-    sums = [jnp.zeros((1, width), f32) for _ in range(4)]
-    for j in (3, 2, 1, 0):
-        at = slice(j * rows, (j + 1) * rows)
-        belongs = jnp.where(seg_col[at] == slot_row, 1.0, 0.0)
-        d_final = out_grad[chunk(me, j, rows), :].astype(f32) + nn(belongs, spread, highest)
-        normal = normal_ref[at, :]
-        sums[0] = sums[0] + col_sum(d_final)
-        sums[1] = sums[1] + col_sum(d_final * normal)
-        d_resid = norm_back(d_final * gain, normal, inverse_ref[at, :1])
-        sums[2] = sums[2] + col_sum(d_resid)
-        low_out[at, :] = d_resid.astype(bf16)
-        d_upper = nt(low_out[at, :], w_down[...]) * grad_of[at, :]
-        sums[3] = sums[3] + col_sum(d_upper)
-        up_out[at, :] = d_upper.astype(bf16)
-        parts[j][...] = nt(up_out[at, :], w_up[...])
-        if j == 0:
-            d_own[...] = d_resid
+    spread_out[...] = spread
+    _, sums = finish_chunk(
+        seg_col[3 * rows :],
+        normal_ref[3 * rows :, :],
+        inverse_ref[3 * rows :, :1],
+        gain,
+        spread,
+        out_grad[chunk(me, 3, rows), :],
+        grad_of[3 * rows :, :],
+        w_down,
+        w_up,
+        low,
+        up,
+        part,
+    )
     for n in range(4):
         side[n : n + 1, :] = sums[n]
     side[4:, :] = jnp.zeros((4, width), f32)
 
 
-def ffn_grads(ids, low, up_low, act, resid_low, even, odd, held):
-    width = low.shape[1]
-    held[:width, :] = tn(low[...], up_low[...])
+def finish_rest(ids, lens, g_ffn, out_grad, grad_of, w_down, w_up, *refs):
+    ins, outs, (resid_low, upper_low, held) = refs[:8], refs[8:-3], refs[-3:]
+    normal_ref, inverse_ref, spread, low3, up3, side3, normed_low, act = ins
+    p0, p1, p2, d_own, side, even, odd = outs
+    parts = (p0, p1, p2)
+    me = ids[0]
+    rows, width = p0.shape
+    seg_col = segment_of(lens, row_places(me, (4 * rows, 1), 0, rows))
+    resid_low[3 * rows :, :] = low3[...]
+    upper_low[3 * rows :, :] = up3[...]
+    total = [side3[n : n + 1, :] for n in range(4)]
+    for j in (2, 1, 0):
+        at = slice(j * rows, (j + 1) * rows)
+        d_resid, sums = finish_chunk(
+            seg_col[at],
+            normal_ref[at, :],
+            inverse_ref[at, :1],
+            g_ffn[...],
+            spread[...],
+            out_grad[chunk(me, j, rows), :],
+            grad_of[at, :],
+            w_down,
+            w_up,
+            resid_low.at[at, :],
+            upper_low.at[at, :],
+            parts[j],
+        )
+        total = [a + b for a, b in zip(total, sums)]
+    d_own[...] = d_resid
+    for n in range(4):
+        side[n : n + 1, :] = total[n]
+    side[4:, :] = jnp.zeros((4, width), f32)
+    held[:width, :] = tn(normed_low[...], upper_low[...])
     held[width:, :] = tn(act[...], resid_low[...])
     step = even.shape[1]
     for d in range(8):
@@ -238,25 +337,29 @@
     e0, e1, e2, e3, d_hidden_out, low_out = outs
     d_normed = d_resid[...] + (own[...] + near[...] + across[...])
     rows, width = d_normed.shape
-    cols = e0.shape[1]
+    cols = w_all.shape[1]
     side = [None, col_sum(d_normed * normal[...]), col_sum(d_normed)]
     d_hidden = norm_back(d_normed * g_attn[...], normal[...], inverse[:, :1])
     side[0] = col_sum(d_hidden)
     d_hidden_out[...] = d_hidden
     low_out[...] = d_hidden.astype(bf16)
+    base = packed_rows(rows, cols)
     for k, out in enumerate((e0, e1, e2, e3)):
-        out[:rows, :] = nt(low_out[...], w_all[k]).astype(bf16).astype(f32)
+        pack_into(out, nt(low_out[...], w_all[k]).astype(bf16).astype(f32))
+        out[base:, :] = jnp.zeros((out.shape[0] - base, 128), f32)
         for v in range(3):
             for s in range(width // cols):
-                r = rows + 4 * v + s
-                out[r : r + 1, :] = side[v][:, s * cols : (s + 1) * cols]
-        out[rows + 12 :, :] = jnp.zeros((4, cols), f32)
+                for n in range(0, cols, 128):
+                    r = base + (n // 128) * 16 + 4 * v + s
+                    m = min(128, cols - n)
+                    out[r : r + 1, :m] = side[v][:, s * cols + n : s * cols + n + m]
 
 
 def out_grads(ids, m0, m1, m2, m3, hidden_low, even, odd, held):
     rows = hidden_low.shape[0]
     for k, block in enumerate((m0, m1, m2, m3)):
-        held[k] = tn(block[k * rows : (k + 1) * rows, :].astype(bf16), hidden_low[...])
+        for col, part in packed_parts(block, held.shape[1], 4 * rows, k * rows, rows):
+            held[k, col : col + part.shape[1], :] = tn(part.astype(bf16), hidden_low[...])
     step = even.shape[2]
     for d in range(8):
         at = pl.ds(pl.multiple_of((ids[1] ^ d) * step, 8), step)
@@ -270,9 +373,17 @@
     slots, cols = q.shape
     rows = slots // 4
     scale = HDIM**-0.5
+    half = rows // 2
     for j, block in enumerate((e0, e1, e2, e3)):
-        d_mixed[j * rows : (j + 1) * rows, :] = block[:rows, :].astype(bf16)
-    shared[...] = (e0[rows:, :] + e1[rows:, :]) + (e2[rows:, :] + e3[rows:, :])
+        for r in (0, half):
+            for col, part in packed_parts(block, cols, rows, r, half):
+                at = slice(j * rows + r, j * rows + r + half)
+                d_mixed[at, col : col + part.shape[1]] = part.astype(bf16)
+    base = packed_rows(rows, cols)
+    side = (e0[base:, :] + e1[base:, :]) + (e2[base:, :] + e3[base:, :])
+    for n in range(0, cols, 128):
+        m = min(128, cols - n)
+        shared[:, n : n + m] = side[(n // 128) * 16 : (n // 128) * 16 + 16, :m]
     for h in range(cols // HDIM):
         lane = slice(h * HDIM, (h + 1) * HDIM)
         for j in range(4):
@@ -324,38 +435,89 @@
         out[d // 2, step:, :] = held[pl.ds(pl.multiple_of(total + c * 8, 8), 8), :]
 
 
-def fold(mine, theirs, a0, a1, a2, a3):
-    for n, out in enumerate((a0, a1, a2, a3)):
-        out[...] = mine[n] + theirs[n]
+def fold(mine, theirs, *refs):
+    extra, outs = refs[: len(refs) - 4], refs[len(refs) - 4 :]
+    rows = mine.shape[1]
+    for n, out in enumerate(outs):
+        out[:rows, :] = mine[n] + theirs[n]
+        if n and extra:
+            out[rows:, :] = extra[0][...]
+
+
+def fold_halves(mine, theirs, extra, own, to_x, to_y, keep_y, keep_x):
+    half = mine.shape[1] // 2
+    more = extra.shape[0] // 2
+    own[...] = mine[0] + theirs[0]
+    for n, (out, at) in enumerate(((to_x, slice(0, half)), (to_y, slice(half, 2 * half)))):
+        for m, block in enumerate((1 + n, 3)):
+            out[m * half : (m + 1) * half, :] = mine[block, at, :] + theirs[block, at, :]
+        out[2 * half :, :] = extra[n * more : (n + 1) * more, :]
+    keep_y[...] = mine[2, :half, :] + theirs[2, :half, :]
+    keep_x[...] = mine[1, half:, :] + theirs[1, half:, :]
+
+
+def add(a, b, out):
+    out[...] = a[...] + b[...]
+
+
+def cut(block, out):
+    out[...] = block[: out.shape[0], :]
+
+
+def join_terms(part1, part2, far, *refs):
+    blocks, (near_out, across_out, terms) = refs[:-3], refs[-3:]
+    rows = part1.shape[0]
+    near_out[:rows, :] = part1[...]
+    across_out[...] = part2[...] + far[...]
+    piece = terms.shape[1]
+    for n in range(4):
+        at = slice(n * piece, (n + 1) * piece)
+        total = blocks[0][at, :]
+        for block in blocks[1:]:
+            total = total + block[at, :]
+        terms[n] = total
+    near_out[rows:, :] = terms[3]
+
+
+def join_own(own, near, across, d_hidden, terms, near_out, across_out):
+    rows = own.shape[0]
+    piece = terms.shape[1]
+    total = own[...] + near[:rows, :] + across[...] + d_hidden[...]
+    near_out[:rows, :] = total
+    across_out[:rows, :] = total
+    near_out[rows:, :] = terms[1]
+    across_out[rows:, :] = terms[2] + near[rows : rows + piece, :]
 
 
 def place(me, r0, r1, r2, r3, out):
-    rows = r0.shape[0]
+    rows = r3.shape[0]
     for j, block in enumerate((r0, r1, r2, r3)):
-        out[chunk(me[0], j, rows), :] = block[...]
-
-
-def unpack_ffn(ids, *refs):
-    blocks, (up_out, down_out, pools_out, held) = refs[:8], refs[8:]
+        out[chunk(me[0], j, rows), :] = block[:rows, :]
+
+
+def unpack_ffn(ids, mine, theirs, up_out, down_out, pools_out, held):
     half = up_out.shape[0]
     step = 2 * half // 8
     wide = pools_out.shape[0]
     width = up_out.shape[1]
-    for d, block in enumerate(blocks):
+    for d in range(8):
+        block = theirs if d & 1 else mine
+        start = (d // 2) * step
         c = ids[1] ^ d
         at = pl.ds(pl.multiple_of((c % 4) * step, 8), step)
 
         @pl.when(c < 4)
-        def _(block=block, at=at):
-            up_out[at, :] = block[:step, :]
+        def _(block=block, at=at, start=start):
+            up_out[at, :] = block[start : start + step, :]
 
         @pl.when(c >= 4)
-        def _(block=block, at=at):
-            down_out[at, :] = block[:step, :]
+        def _(block=block, at=at, start=start):
+            down_out[at, :] = block[start : start + step, :]
 
         to = pl.ds(pl.multiple_of(c * SENTS, 8), SENTS)
+        start = 4 * step + (d // 2) * 3 * SENTS
         for n in range(3):
-            held[n, to, :] = block[step + n * SENTS : step + (n + 1) * SENTS, :]
+            held[n, to, :] = block[start + n * SENTS : start + (n + 1) * SENTS, :]
     for n in range(3):
         m = min(width, wide - n * width)
         pools_out[n * width : n * width + m, :] = held[n].T[:m, :]
@@ -395,12 +557,22 @@
     return lax.psum(block, "dp", axis_index_groups=groups)
 
 
-def dp_fold(even, odd, n_dp):
+def core_swap(even, odd, n_dp):
     other = swap_dp(odd, 1, n_dp)
     flat = even.shape[-2] if even.ndim == 3 else even.shape[1] * even.shape[2]
-    even = even.reshape(4, flat, even.shape[-1])
-    other = other.reshape(even.shape)
-    return call(fold, [shape(*even.shape[1:])] * 4, [even, other], moved=3 * even.size * 4)
+    return even.reshape(4, flat, even.shape[-1]), other.reshape(4, flat, even.shape[-1])
+
+
+def fold_call(even, other, extra=()):
+    _, rows, width = even.shape
+    more = sum(item.shape[0] for item in extra)
+    blocks = call(
+        fold,
+        [shape(rows, width)] + [shape(rows + more, width)] * 3,
+        [even, other, *extra],
+        moved=3 * even.size * 4,
+    )
+    return list(blocks)
 
 
 def with_other_core(blocks, n_dp):
@@ -445,7 +617,7 @@
         slice_own = lax.dynamic_slice_in_dim(w_out, group * piece, piece, 0).astype(f32)
         slices = [slice_own] + [swap(slice_own, n) for n in (1, 2, 3)]
 
-        tok_x, q, k, v, probs, mixed_low, mixed = call(
+        tok_x, q, k, v, probs, mixed = call(
             attend,
             [
                 shape(slots, width, kind=bf16),
@@ -453,12 +625,20 @@
                 shape(slots, cols, kind=bf16),
                 shape(slots, cols, kind=bf16),
                 shape(heads, slots, slots, kind=bf16),
-                shape(slots, cols, kind=bf16),
-                shape(slots, cols),
+                shape(packed_rows(slots, cols), 128),
             ],
-            [ids, lengths, tokens, wq, wk, wv, row(b_query), row(b_value)],
+            [ids]
+            + [
+                pltpu.with_memory_space_constraint(item, pltpu.HBM)
+                for item in (lengths, tokens, wq, wk, wv, row(b_query), row(b_value))
+            ],
             flops=2 * slots * width * 3 * cols + 4 * slots * slots * cols,
             moved=slots * width * 4 + 3 * cols * width * 2 + heads * slots * slots * 2,
+            scratch=[pltpu.VMEM((slots, cols), bf16)]
+            + [pltpu.VMEM((cols, width), bf16)] * 3
+            + [pltpu.VMEM((1, cols), f32)] * 2
+            + [pltpu.SMEM((1, SENTS), jnp.int32), pltpu.SemaphoreType.DMA((10,))],
+            raw=7,
         )
         mixed, *slices = together(mixed, *slices)
         slices = jnp.stack(slices)
@@ -473,9 +653,24 @@
             moved=4 * cols * width * 6,
             scratch=[pltpu.VMEM((4, cols, width), f32)],
         )
+        feed_ins = [tok_x, *mixed_all, w_all, row(b_out), row(g_attn), row(b_attn)]
+        feed_ins += [w_up, row(b_up), w_down]
+        part3, low3, upper3, act3 = call(
+            feed_first,
+            [
+                shape(rows, width),
+                shape(rows, width, kind=bf16),
+                shape(rows, units),
+                shape(rows, units, kind=bf16),
+            ],
+            feed_ins,
+            flops=2 * rows * width * (width + 2 * units),
+            moved=rows * width * 4 + 3 * width * units * 2,
+        )
+        far = swap(part3, 1)
         *parts, normed_low, upper, act, normal_own, inverse_own, resid_own = call(
-            feed,
-            [shape(rows, width)] * 4
+            feed_rest,
+            [shape(rows, width)] * 3
             + [
                 shape(slots, width, kind=bf16),
                 shape(slots, units),
@@ -484,12 +679,10 @@
                 shape(rows, 128),
                 shape(rows, width),
             ],
-            [tok_x, *mixed_all, w_all, row(b_out), row(g_attn), row(b_attn)]
-            + [w_up, row(b_up), w_down, row(b_down)],
-            flops=2 * slots * width * (width + 2 * units),
-            moved=4 * slots * width * 4 + 3 * width * units * 2,
-        )
-        far = swap(parts[3], 1)
+            feed_ins + [row(b_down), low3, upper3, act3],
+            flops=6 * rows * width * (width + 2 * units),
+            moved=3 * slots * width * 4 + 3 * width * units * 2,
+        )
         slope = call(
             gelu_grad, shape(slots, units), [upper], moved=8 * slots * units, flops=slots * units
         )
@@ -499,51 +692,67 @@
         across, near = swap(own, 2), swap(own, 1)
         across, near = together(across, near)
         resid = [own, near, across, swap(across, 1)]
-        *parts, layer_out, own_pools, d_resid, resid_low, upper_low, side = call(
-            finish,
-            [shape(rows, width)] * 4
-            + [
+        part3, layer_out, own_pools, normal, inverse, spread, low3, up3, side3 = call(
+            finish_first,
+            [
+                shape(rows, width),
                 shape(slots, width, kind=bf16),
                 shape(3 * SENTS, width),
-                shape(rows, width),
-                shape(slots, width, kind=bf16),
-                shape(slots, units, kind=bf16),
+                shape(slots, width),
+                shape(slots, 128),
+                shape(SENTS, width),
+                shape(rows, width, kind=bf16),
+                shape(rows, units, kind=bf16),
                 shape(8, width),
             ],
             [ids, lengths, *resid, row(g_ffn), row(b_ffn), out_grad, pool_grad, slope]
             + [w_down, w_up],
-            flops=4 * slots * width * units,
+            flops=4 * rows * width * units,
             moved=6 * slots * width * 4,
+            scratch=[pltpu.VMEM((SENTS, width), f32)],
+        )
+        far = swap(part3, 1)
+        step = 2 * width // 8
+        *parts, d_resid, side, even, odd = call(
+            finish_rest,
+            [shape(rows, width)] * 4 + [shape(8, width)] + [shape(4, step, width)] * 2,
+            [ids, lengths, row(g_ffn), out_grad, slope, w_down, w_up]
+            + [normal, inverse, spread, low3, up3, side3, normed_low, act],
+            flops=8 * slots * width * units,
+            moved=6 * slots * width * 4 + 8 * width * units,
             scratch=[
-                pltpu.VMEM((slots, width), f32),
-                pltpu.VMEM((slots, 128), f32),
-                pltpu.VMEM((SENTS, width), f32),
+                pltpu.VMEM((slots, width), bf16),
+                pltpu.VMEM((slots, units), bf16),
+                pltpu.VMEM((2 * width, width), f32),
             ],
         )
-        far = swap(parts[3], 1)
-        step = 2 * width // 8
-        even, odd = call(
-            ffn_grads,
-            [shape(4, step, width)] * 2,
-            [ids, normed_low, upper_low, act, resid_low],
-            flops=4 * slots * width * units,
-            moved=4 * slots * width * 2 + 8 * width * units,
-            scratch=[pltpu.VMEM((2 * width, width), f32)],
-        )
-        ffn = dp_fold(even, odd, n_dp)
-        far, part2, part1, *ffn = together(far, parts[2], parts[1], *ffn)
-        across, near = swap(part2 + far, 2), swap(part1, 1)
-        ffn[1], ffn[2] = swap_dp(ffn[1], 2, n_dp), swap_dp(ffn[2], 4, n_dp)
-        across, near, *ffn = together(across, near, *ffn)
+        even, other = core_swap(even, odd, n_dp)
+        part2 = call(add, shape(rows, width), [parts[2], far], flops=100 * order)
+        part2, part1, even, other = together(part2, parts[1], even, other)
+        across, near = swap(part2, 2), swap(part1, 1)
+        half, more = step // 2, 3 * SENTS // 2
+        ffn_own, to_x, to_y, keep_y, keep_x = call(
+            fold_halves,
+            [shape(step, width)] + [shape(step + more, width)] * 2 + [shape(half, width)] * 2,
+            [even, other, own_pools],
+            moved=3 * even.size * 4,
+        )
+        from_x, from_y = swap_dp(to_x, 2, n_dp), swap_dp(to_y, 4, n_dp)
         *sent, d_hidden, hidden_low = call(
             back_hidden,
-            [shape(rows + 16, cols)] * 4 + [shape(rows, width), shape(rows, width, kind=bf16)],
+            [shape(packed_rows(rows, cols) + 16 * -(-cols // 128), 128)] * 4
+            + [shape(rows, width), shape(rows, width, kind=bf16)],
             [parts[0], near, across, d_resid, normal_own, inverse_own, row(g_attn), w_all],
-            flops=2 * rows * width * 4 * cols,
+            flops=30 * order,
             moved=6 * rows * width * 4,
         )
+        *sent, d_hidden, hidden_low, from_x, from_y, keep_x, keep_y = together(
+            *sent, d_hidden, hidden_low, from_x, from_y, keep_x, keep_y
+        )
         d_mixed = [sent[0]] + [swap(sent[n], n) for n in (1, 2, 3)]
-        ffn[3] = swap_dp(ffn[3], 6, n_dp)
+        to_y = jnp.concatenate([keep_y + from_x[half:step], own_pools[:more], from_x[step:]])
+        to_x = jnp.concatenate([keep_x + from_y[half:step], own_pools[more:], from_y[step:]])
+        last_y, last_x = swap_dp(to_y, 4, n_dp), swap_dp(to_x, 2, n_dp)
         even, odd = call(
             out_grads,
             [shape(4, 4, piece, width)] * 2,
@@ -552,16 +761,14 @@
             moved=8 * 4 * cols * width,
             scratch=[pltpu.VMEM((4, cols, width), f32)],
         )
-        out = dp_fold(even, odd, n_dp)
-        *joined, ffn_last = together(*d_mixed, *out, ffn[3])
-        d_mixed, out = joined[:4], joined[4:]
-        ffn_sum = rest_of_dp(ffn[0] + ffn[1] + ffn[2] + ffn_last, n_dp)
+        even, other = core_swap(even, odd, n_dp)
+        d_mixed = together(*d_mixed)
         *parts, grads, bias, shared = call(
             attend_back,
             [shape(rows, width)] * 4
             + [shape(slots, 3 * cols, kind=bf16), shape(8, cols), shape(16, cols)],
             [*d_mixed, probs, q, k, v, wq, wk, wv],
-            flops=8 * slots * slots * cols + 6 * slots * width * cols,
+            flops=10 * order,
             moved=heads * slots * slots * 2 + 2 * slots * width * 4,
             scratch=[
                 pltpu.VMEM((slots, cols), bf16),
@@ -569,7 +776,14 @@
                 pltpu.VMEM((slots, slots), bf16),
             ],
         )
-        far = swap(parts[3], 1)
+        part3, out_even, out_other, last_x, last_y = together(parts[3], even, other, last_x, last_y)
+        ffn_sum = jnp.concatenate([from_x[:half] + last_y[:half], from_y[:half] + last_x[:half]])
+        ffn_sum = rest_of_dp(ffn_own + ffn_sum, n_dp)
+        all_pools = [own_pools, from_x[step:], last_x[half : half + more]]
+        all_pools += [last_y[half : half + more], from_y[step:]]
+        all_pools += [last_y[half + more :], last_x[half + more :]]
+        far = swap(part3, 1)
+        out = fold_call(out_even, out_other)
         out[1:] = [swap_dp(out[n], 2 * n, n_dp) for n in (1, 2, 3)]
         even, odd = call(
             qkv_grads,
@@ -579,42 +793,55 @@
             moved=8 * 3 * cols * width,
             scratch=[pltpu.VMEM((3 * cols + 64, width), f32)],
         )
-        qkv = dp_fold(even, odd, n_dp)
-        ffn_own = jnp.concatenate([ffn_sum, own_pools])
-        far, part2, part1, ffn_own, *joined = together(
-            far, parts[2], parts[1], ffn_own, *qkv, *out
-        )
-        qkv, out = joined[:4], joined[4:]
-        across, near = swap(part2 + far, 2), swap(part1, 1)
-        ffn_x, ffn_y = swap_dp(ffn_own, 2, n_dp), swap_dp(ffn_own, 4, n_dp)
-        qkv[1], qkv[2] = swap_dp(qkv[1], 2, n_dp), swap_dp(qkv[2], 4, n_dp)
-        out_sum = rest_of_dp(sum(out), n_dp).reshape(4, piece, width)
-        across, near, ffn_x, ffn_y, out_sum, *qkv = together(
-            across, near, ffn_x, ffn_y, out_sum, *qkv
-        )
-        own = parts[0] + near + across + d_hidden
-        across, near = swap(own, 2), swap(own, 1)
-        ffn_d = swap_dp(ffn_own, 6, n_dp)
-        qkv[3] = swap_dp(qkv[3], 6, n_dp)
-        out_terms = [out_sum[0]] + [swap(out_sum[n], n) for n in (1, 2, 3)]
-        across, near, ffn_d, *joined = together(across, near, ffn_d, *qkv, *out_terms)
-        qkv, out_terms = joined[:4], joined[4:]
-        far = swap(across, 1)
-        attn_own = jnp.concatenate([rest_of_dp(sum(qkv), n_dp), sum(out_terms)])
+        even, other = core_swap(even, odd, n_dp)
+        if n_dp > 8:
+            out = [rest_of_dp(sum(out), n_dp)]
+        part1, part2, terms = call(
+            join_terms,
+            [shape(rows + piece, width), shape(rows, width), shape(4, piece, width)],
+            [parts[1], parts[2], far, *out],
+            flops=20 * order,
+        )
+        part2, part1, terms, even, other = together(part2, part1, terms, even, other)
+        across, near = swap(part2, 2), swap(part1, 1)
+        qkv = fold_call(even, other, [ffn_sum])
+        from_x, from_y = swap_dp(qkv[1], 2, n_dp), swap_dp(qkv[2], 4, n_dp)
+        own_near, own_across = call(
+            join_own,
+            [shape(rows + piece, width)] * 2,
+            [parts[0], near, across, d_hidden, terms],
+            flops=30 * order,
+            moved=7 * rows * width * 4,
+        )
+        own_near, own_across, from_x, from_y, qkv_last = together(
+            own_near, own_across, from_x, from_y, qkv[3]
+        )
+        across, near = swap(own_across, 2), swap(own_near, 1)
+        from_d = swap_dp(qkv_last, 6, n_dp)
+        across, near = together(across, near)
+        across_rows = call(cut, shape(rows, width), [across], flops=20 * order)
+        across_rows, near, across, from_d = together(across_rows, near, across, from_d)
+        far = swap(across_rows, 1)
+        low = 3 * piece + 8
+        qkv_sum = rest_of_dp(qkv[0] + from_x[:low] + from_y[:low] + from_d[:low], n_dp)
+        attn_own = jnp.concatenate([qkv_sum, terms[0] + near[rows:] + across[rows:]])
         attn_blocks = [attn_own] + [swap_dp(attn_own, 2 * n, n_dp) for n in (1, 2, 3)]
-        ffn_blocks = with_other_core([ffn_own, ffn_x, ffn_y, ffn_d], n_dp)
-        d_tokens = call(
-            place, shape(slots, width), [ids, own, near, across, far], moved=8 * slots * width
-        )
-        attn_blocks = with_other_core(attn_blocks, n_dp)
+        mine = jnp.concatenate([ffn_sum, from_x[low:], from_y[low:], from_d[low:], *all_pools])
         wide = pool_grad.shape[1]
         d_w_up, d_w_down, pools = call(
             unpack_ffn,
             [shape(width, units), shape(units, width), shape(wide, 8 * SENTS)],
-            [ids, *ffn_blocks],
+            [ids, mine, swap_dp(mine, 1, n_dp)],
             moved=16 * width * units,
             scratch=[pltpu.VMEM((3, 8 * SENTS, width), f32)],
         )
+        d_tokens = call(
+            place, shape(slots, width), [ids, own_near, near, across, far], moved=8 * slots * width
+        )
+        d_w_up, d_w_down, pools, d_tokens, *attn_blocks = together(
+            d_w_up, d_w_down, pools, d_tokens, *attn_blocks
+        )
+        attn_blocks = with_other_core(attn_blocks, n_dp)
         pools = pools.T
         if n_dp > 8:
             third = [own_pools[n * SENTS : (n + 1) * SENTS] for n in range(3)]
@@ -627,6 +854,9 @@
             moved=8 * 4 * cols * width,
             scratch=[pltpu.VMEM((3 * cols, width), f32)],
         )
+        b_q, b_v = vectors[4, :cols], vectors[4, cols : 2 * cols]
+        d_b_out, d_g_attn, d_b_attn = vectors[8], vectors[9], vectors[10]
+        d_b_up, d_b_down, d_g_ffn, d_b_ffn = vectors[3], vectors[2], vectors[1], vectors[0]
         return (
             layer_out,
             pools,
@@ -634,18 +864,18 @@
             d_w_query.T,
             d_w_key.T,
             d_w_value.T,
-            vectors[4, :cols],
-            vectors[4, cols : 2 * cols],
+            b_q,
+            b_v,
             d_w_out,
-            vectors[8],
-            vectors[9],
-            vectors[10],
+            d_b_out,
+            d_g_attn,
+            d_b_attn,
             d_w_up,
-            vectors[3],
+            d_b_up,
             d_w_down,
-            vectors[2],
-            vectors[1],
-            vectors[0],
+            d_b_down,
+            d_g_ffn,
+            d_b_ffn,
         )
 
     return shards

time: 287 us -> 249 us (0.87)
  waiting for transfers between devices: 173 us -> 143 us
  local copies, waits for them, and re-layouts: 7.44 us -> 1.61 us
  starting transfers between devices: 64.7 us -> 59.4 us
  Pallas kernels: 38.5 us -> 41.7 us
    ppermute x33 -> x28, waiting for transfers between devices: 63.1 us -> 41.5 us  [swap_dp(): return lax.ppermute(block, 'dp', [(i, i ^ k) for i in range(n_dp)])]
    ppermute x27 -> x24, waiting for transfers between devices: 110 us -> 102 us  [swap(): return lax.ppermute(block, 'tensor', swaps[k])]
    unnamed x44 -> x43, local copies, waits for them, and re-layouts: 6.1 us -> 0.26 us
    ppermute x27 -> x24, starting transfers between devices: 40.9 us -> 36.9 us  [swap(): return lax.ppermute(block, 'tensor', swaps[k])]
    pallas_call x16 -> x21, Pallas kernels: 38.5 us -> 41.7 us  [call(): pl.pallas_call(body, out_shape=outs, in_specs=specs, out_specs=jax.tree.m...]
    ppermute x33 -> x28, starting transfers between devices: 23.7 us -> 22.5 us  [swap_dp(): return lax.ppermute(block, 'dp', [(i, i ^ k) for i in range(n_dp)])]
  transfers between devices with their start and end apart: 60 -> 52, of which waited for: 33 -> 35; matrix products, arithmetic and copies ran while one was open for 1% -> 0% of each run, Pallas kernels for 4% -> 13%
where the time goes in v3:
time: 249 us
  waiting for transfers between devices  143 us (57%)
  starting transfers between devices  59.4 us (24%)
  Pallas kernels  41.7 us (17%)
    ppermute x24, waiting for transfers between devices, swap(): return lax.ppermute(block, 'tensor', swaps[k])  102 us
    pallas_call x21, Pallas kernels, call(): pl.pallas_call(body, out_shape=outs, in_specs=specs, out_specs=jax.tree.m...  41.7 us
    ppermute x28, waiting for transfers between devices, swap_dp(): return lax.ppermute(block, 'dp', [(i, i ^ k) for i in range(n_dp)])  41.5 us
    ppermute x24, starting transfers between devices, swap(): return lax.ppermute(block, 'tensor', swaps[k])  36.9 us
    ppermute x28, starting transfers between devices, swap_dp(): return lax.ppermute(block, 'dp', [(i, i ^ k) for i in range(n_dp)])  22.5 us
  transfers between devices with their start and end apart: 52, of which 35 were waited for; matrix products, arithmetic and copies ran while one was open for 0% of the time, Pallas kernels for 13%

profile of v3, /device:TPU:0, one launch (start us, length us, event | category | flops | bytes accessed | tf_op | source)
XLA Modules:
  0.0 248.6 jit_solution(7876073539972989249)
XLA Ops:
  7.2 8.1 %shard_map.322 = (bf16[512,768]{1,0:T(8,128)(2,1)S(1)}, bf16[512,192]{1,0:T(8,128)(2,1)S(1)}, bf16[512,192]{1,0:T(8,128)(2,1)S(1)}, bf16[512,192]{1,0:T(8,128)(2...) custom-call(s32[2]{0:T(128)S(1)} %pad_add_fusion.ids.me, s32[1,16]{1,0:T(1,128)} %lens.3, ...), custom_call_target="tpu_custom_call" | custom-call | flops 654311424 | bytes 4030464 | tf_op jit(solution)/shard_map/pallas_call | solution.py:65
  23.5 6.4 %collective-permute-done.5.refs_2_ = f32[4,24,768]{2,1,0:T(8,128)S(1)} collective-permute-done((f32[4,24,768]{2,1,0:T(8,128)S(1)}, f32[4,24,768]{2,1,0:T(8,128)S(1)}, u32[]{:S(2)}, u32[]{:S(2)}) %collective-permute-start.5) | collective-permute-done | bytes 294944 | tf_op jit(solution)/shard_map/ppermute | solution.py:546
  29.8 5.0 %collective-permute-done.6.refs_4_ = f32[4,24,768]{2,1,0:T(8,128)S(1)} collective-permute-done((f32[4,24,768]{2,1,0:T(8,128)S(1)}, f32[4,24,768]{2,1,0:T(8,128)S(1)}, u32[]{:S(2)}, u32[]{:S(2)}) %collective-permute-start.6) | collective-permute-done | bytes 294944 | tf_op jit(solution)/shard_map/ppermute | solution.py:546
  39.5 5.8 %collective-permute-done.8.m3 = f32[768,128]{1,0:T(8,128)S(1)} collective-permute-done((f32[768,128]{1,0:T(8,128)S(1)}, f32[768,128]{1,0:T(8,128)S(1)}, u32[]{:S(2)}, u32[]{:S(2)}) %collective-permute-start.8) | collective-permute-done | bytes 393248 | tf_op jit(solution)/shard_map/ppermute | solution.py:542
  47.5 4.1 %shard_map.325 = (f32[128,768]{1,0:T(8,128)S(1)}, f32[128,768]{1,0:T(8,128)S(1)}, f32[128,768]{1,0:T(8,128)S(1)}, bf16[512,768]{1,0:T(8,128)(2,1)S(1)}, f32[512,...) custom-call(bf16[512,768]{1,0:T(8,128)(2,1)S(1)} %get-tuple-element., ...), custom_call_target="tpu_custom_call" | custom-call | flops 1358954496 | bytes 8257536 | tf_op jit(solution)/shard_map/pallas_call | solution.py:65
  52.2 3.8 %collective-permute-done.13 = f32[128,768]{1,0:T(8,128)S(1)} collective-permute-done((f32[128,768]{1,0:T(8,128)S(1)}, f32[128,768]{1,0:T(8,128)S(1)}, u32[]{:S(2)}, u32[]{:S(2)}) %collective-permute-start.13) | collective-permute-done | bytes 393248 | tf_op jit(solution)/shard_map/ppermute | solution.py:542
  61.0 14.3 %collective-permute-done.15 = f32[128,768]{1,0:T(8,128)S(1)} collective-permute-done((f32[128,768]{1,0:T(8,128)S(1)}, f32[128,768]{1,0:T(8,128)S(1)}, u32[]{:S(2)}, u32[]{:S(2)}) %collective-permute-start.15) | collective-permute-done | bytes 393248 | tf_op jit(solution)/shard_map/ppermute | solution.py:542
  79.5 15.3 %collective-permute-done.16.r2 = f32[128,768]{1,0:T(8,128)S(1)} collective-permute-done((f32[128,768]{1,0:T(8,128)S(1)}, f32[128,768]{1,0:T(8,128)S(1)}, u32[]{:S(2)}, u32[]{:S(2)}) %collective-permute-start.16) | collective-permute-done | bytes 393248 | tf_op jit(solution)/shard_map/ppermute | solution.py:542
  94.9 8.9 %collective-permute-done.18.r3 = f32[128,768]{1,0:T(8,128)S(1)} collective-permute-done((f32[128,768]{1,0:T(8,128)S(1)}, f32[128,768]{1,0:T(8,128)S(1)}, u32[]{:S(2)}, u32[]{:S(2)}) %collective-permute-start.18) | collective-permute-done | bytes 393248 | tf_op jit(solution)/shard_map/ppermute | solution.py:542
  103.8 4.8 %shard_map.327 = (f32[128,768]{1,0:T(8,128)S(1)}, bf16[512,768]{1,0:T(8,128)(2,1)}, f32[48,768]{1,0:T(8,128)S(1)}, f32[512,768]{1,0:T(8,128)S(1)}, f32[512,128]{...) custom-call(s32[2]{0:T(128)S(1)} %pad_add_fusion.ids.me, ...), custom_call_target="tpu_custom_call" | custom-call | flops 301989888 | bytes 9437184 | tf_op jit(solution)/shard_map/pallas_call | solution.py:65
  109.1 6.3 %shard_map.328 = (f32[128,768]{1,0:T(8,128)S(1)}, f32[128,768]{1,0:T(8,128)S(1)}, f32[128,768]{1,0:T(8,128)S(1)}, f32[128,768]{1,0:T(8,128)S(1)}, f32[8,768]{1,0...) custom-call(s32[2]{0:T(128)S(1)} %pad_add_fusion.ids.me, s32[1,16]{1,0:T(1,128)S(1)} %copy-done.6, ...), custom_call_target="tpu_custom_call" | custom-call | flops 2415919104 | bytes 14155776 | tf_op jit(solution)/shard_map/pallas_call | solution.py:65
  116.7 3.3 %collective-permute-done.20.theirs = f32[4,192,768]{2,1,0:T(8,128)S(1)} collective-permute-done((f32[4,192,768]{2,1,0:T(8,128)S(1)}, f32[4,192,768]{2,1,0:T(8,128)S(1)}, u32[]{:S(2)}, u32[]{:S(2)}) %collective-permute-start.20) | collective-permute-done | bytes 2359328 | tf_op jit(solution)/shard_map/ppermute | solution.py:546
  121.5 3.4 %collective-permute-start.22 = (f32[128,768]{1,0:T(8,128)S(1)}, f32[128,768]{1,0:T(8,128)S(1)}, u32[]{:S(2)}, u32[]{:S(2)}) collective-permute-start(f32[128,768]{1,0:T(8,128)S(1)} %shard_map.329), channel_id=1, source_target_pairs={{0,2},{1,3},{2,0},{3,1},{4,6},{5,7},{6,4},{7,5},{8,10},{9,11},{10,... | collective-permute-start | bytes 1179656 | tf_op jit(solution)/shard_map/ppermute | solution.py:542
  128.4 11.2 %collective-permute-done.21.near = f32[128,768]{1,0:T(8,128)S(1)} collective-permute-done((f32[128,768]{1,0:T(8,128)S(1)}, f32[128,768]{1,0:T(8,128)S(1)}, u32[]{:S(2)}, u32[]{:S(2)}) %collective-permute-start.21) | collective-permute-done | bytes 393248 | tf_op jit(solution)/shard_map/ppermute | solution.py:542
  152.3 3.7 %collective-permute-done.26.e2 = f32[224,128]{1,0:T(8,128)S(1)} collective-permute-done((f32[224,128]{1,0:T(8,128)S(1)}, f32[224,128]{1,0:T(8,128)S(1)}, u32[]{:S(2)}, u32[]{:S(2)}) %collective-permute-start.26) | collective-permute-done | bytes 114720 | tf_op jit(solution)/shard_map/ppermute | solution.py:542
  156.1 3.5 %shard_map.332 = (f32[128,768]{1,0:T(8,128)S(1)}, f32[128,768]{1,0:T(8,128)S(1)}, f32[128,768]{1,0:T(8,128)S(1)}, f32[128,768]{1,0:T(8,128)S(1)}, bf16[512,576]{...) custom-call(f32[224,128]{1,0:T(8,128)S(1)} %get-tuple-element.227.e0, ...), custom_call_target="tpu_custom_call" | custom-call | flops 10000000000 | bytes 4718592 | tf_op jit(solution)/shard_map/pallas_call | solution.py:65
  159.5 3.9 %collective-permute-done.29 = f32[144,768]{1,0:T(8,128)S(1)} collective-permute-done((f32[144,768]{1,0:T(8,128)S(1)}, f32[144,768]{1,0:T(8,128)S(1)}, u32[]{:S(2)}, u32[]{:S(2)}) %collective-permute-start.29) | collective-permute-done | bytes 442400 | tf_op jit(solution)/shard_map/ppermute | solution.py:546
  169.6 4.7 %collective-permute-done.32.refs_1_ = f32[96,768]{1,0:T(8,128)S(1)} collective-permute-done((f32[96,768]{1,0:T(8,128)S(1)}, f32[96,768]{1,0:T(8,128)S(1)}, u32[]{:S(2)}, u32[]{:S(2)}) %collective-permute-start.32) | collective-permute-done | bytes 294944 | tf_op jit(solution)/shard_map/ppermute | solution.py:546
  174.2 5.9 %collective-permute-done.33.refs_2_ = f32[96,768]{1,0:T(8,128)S(1)} collective-permute-done((f32[96,768]{1,0:T(8,128)S(1)}, f32[96,768]{1,0:T(8,128)S(1)}, u32[]{:S(2)}, u32[]{:S(2)}) %collective-permute-start.33) | collective-permute-done | bytes 294944 | tf_op jit(solution)/shard_map/ppermute | solution.py:546
  186.5 11.0 %collective-permute-done.37.across = f32[128,768]{1,0:T(8,128)S(1)} collective-permute-done((f32[128,768]{1,0:T(8,128)S(1)}, f32[128,768]{1,0:T(8,128)S(1)}, u32[]{:S(2)}, u32[]{:S(2)}) %collective-permute-start.37) | collective-permute-done | bytes 393248 | tf_op jit(solution)/shard_map/ppermute | solution.py:542
  198.8 3.4 %collective-permute-done.38 = f32[272,768]{1,0:T(8,128)S(1)} collective-permute-done((f32[272,768]{1,0:T(8,128)S(1)}, f32[272,768]{1,0:T(8,128)S(1)}, u32[]{:S(2)}, u32[]{:S(2)}) %collective-permute-start.38) | collective-permute-done | bytes 835616 | tf_op jit(solution)/shard_map/ppermute | solution.py:546
  206.7 17.0 %collective-permute-done.40.block.r2 = f32[152,768]{1,0:T(8,128)S(1)} collective-permute-done((f32[152,768]{1,0:T(8,128)S(1)}, f32[152,768]{1,0:T(8,128)S(1)}, u32[]{:S(2)}, u32[]{:S(2)}) %collective-permute-start.40) | collective-permute-done | bytes 466976 | tf_op jit(solution)/shard_map/ppermute | solution.py:542
  227.8 7.8 %collective-permute-done.44.r3 = f32[128,768]{1,0:T(8,128)S(1)} collective-permute-done((f32[128,768]{1,0:T(8,128)S(1)}, f32[128,768]{1,0:T(8,128)S(1)}, u32[]{:S(2)}, u32[]{:S(2)}) %collective-permute-start.44) | collective-permute-done | bytes 393248 | tf_op jit(solution)/shard_map/ppermute | solution.py:542
  237.3 3.5 %shard_map.340 = (f32[768,768]{1,0:T(8,128)}, f32[768,768]{1,0:T(8,128)}, f32[1728,128]{1,0:T(8,128)}) custom-call(s32[2]{0:T(128)S(1)} %pad_add_fusion.ids.me, f32[960,768]{1,0:T(8,128)S(1)} %slice_dynamic-update-slice_fusion.3.mine, f32[960,768]{1,0:T(8,128)S(1)} %collective-permute-done.43.theirs), custom_call_target="tpu_custom_call" | custom-call | bytes 9437184 | tf_op jit(solution)/shard_map/pallas_call | solution.py:65
  (171 shorter events, 82.4 us)
Async XLA Ops:
  1.5 13.9 %collective-permute-start = (f32[24,768]{1,0:T(8,128)S(1)}, f32[24,768]{1,0:T(8,128)S(1)}, u32[]{:S(2)}, u32[]{:S(2)}) collective-permute-start(f32[24,768]{1,0:T(8,128)S(1)} %dynamic-slice_convert_fusion), channel_id=1, source_target_pairs={{0,1},{1,0},{2,3},{3,2},{4,5},{5,4},{6,7},{7,6},{8,9},{9,8},{10,11... | collective-permute-start | bytes 221192 | tf_op jit(solution)/shard_map/ppermute | solution.py:542
  15.4 19.8 %collective-permute-start.3 = (f32[768,128]{1,0:T(8,128)S(1)}, f32[768,128]{1,0:T(8,128)S(1)}, u32[]{:S(2)}, u32[]{:S(2)}) collective-permute-start(f32[768,128]{1,0:T(8,128)S(1)} %get-tuple-element.162.m0), channel_id=1, source_target_pairs={{0,2},{1,3},{2,0},{3,1},{4,6},{5,7},{6,4},{7,5},{8,10},{9,11},{10,... | collective-permute-start | bytes 1179656 | tf_op jit(solution)/shard_map/ppermute | solution.py:542
  17.4 17.9 %collective-permute-start.4 = (f32[768,128]{1,0:T(8,128)S(1)}, f32[768,128]{1,0:T(8,128)S(1)}, u32[]{:S(2)}, u32[]{:S(2)}) collective-permute-start(f32[768,128]{1,0:T(8,128)S(1)} %get-tuple-element.162.m0), channel_id=1, source_target_pairs={{0,1},{1,0},{2,3},{3,2},{4,5},{5,4},{6,7},{7,6},{8,9},{9,8},{10,11... | collective-permute-start | bytes 1179656 | tf_op jit(solution)/shard_map/ppermute | solution.py:542
  56.1 19.2 %collective-permute-start.15 = (f32[128,768]{1,0:T(8,128)S(1)}, f32[128,768]{1,0:T(8,128)S(1)}, u32[]{:S(2)}, u32[]{:S(2)}) collective-permute-start(f32[128,768]{1,0:T(8,128)S(1)} %add.53), channel_id=1, source_target_pairs={{0,2},{1,3},{2,0},{3,1},{4,6},{5,7},{6,4},{7,5},{8,10},{9,11},{10,... | collective-permute-start | bytes 1179656 | tf_op jit(solution)/shard_map/ppermute | solution.py:542
  59.3 16.1 %collective-permute-start.14 = (f32[128,768]{1,0:T(8,128)S(1)}, f32[128,768]{1,0:T(8,128)S(1)}, u32[]{:S(2)}, u32[]{:S(2)}) collective-permute-start(f32[128,768]{1,0:T(8,128)S(1)} %get-tuple-element.182), channel_id=1, source_target_pairs={{0,1},{1,0},{2,3},{3,2},{4,5},{5,4},{6,7},{7,6},{8,9},{9,8},{10,11... | collective-permute-start | bytes 1179656 | tf_op jit(solution)/shard_map/ppermute | solution.py:542
  75.5 19.2 %collective-permute-start.16 = (f32[128,768]{1,0:T(8,128)S(1)}, f32[128,768]{1,0:T(8,128)S(1)}, u32[]{:S(2)}, u32[]{:S(2)}) collective-permute-start(f32[128,768]{1,0:T(8,128)S(1)} %add_add_fusion.r0), channel_id=1, source_target_pairs={{0,2},{1,3},{2,0},{3,1},{4,6},{5,7},{6,4},{7,5},{8,10},{9,11},{10,... | collective-permute-start | bytes 1179656 | tf_op jit(solution)/shard_map/ppermute | solution.py:542
  77.1 17.7 %collective-permute-start.17 = (f32[128,768]{1,0:T(8,128)S(1)}, f32[128,768]{1,0:T(8,128)S(1)}, u32[]{:S(2)}, u32[]{:S(2)}) collective-permute-start(f32[128,768]{1,0:T(8,128)S(1)} %add_add_fusion.r0), channel_id=1, source_target_pairs={{0,1},{1,0},{2,3},{3,2},{4,5},{5,4},{6,7},{7,6},{8,9},{9,8},{10,11... | collective-permute-start | bytes 1179656 | tf_op jit(solution)/shard_map/ppermute | solution.py:542
  120.0 19.6 %collective-permute-start.21 = (f32[128,768]{1,0:T(8,128)S(1)}, f32[128,768]{1,0:T(8,128)S(1)}, u32[]{:S(2)}, u32[]{:S(2)}) collective-permute-start(f32[128,768]{1,0:T(8,128)S(1)} %get-tuple-element.207), channel_id=1, source_target_pairs={{0,1},{1,0},{2,3},{3,2},{4,5},{5,4},{6,7},{7,6},{8,9},{9,8},{10,11... | collective-permute-start | bytes 1179656 | tf_op jit(solution)/shard_map/ppermute | solution.py:542
  121.5 18.1 %collective-permute-start.22 = (f32[128,768]{1,0:T(8,128)S(1)}, f32[128,768]{1,0:T(8,128)S(1)}, u32[]{:S(2)}, u32[]{:S(2)}) collective-permute-start(f32[128,768]{1,0:T(8,128)S(1)} %shard_map.329), channel_id=1, source_target_pairs={{0,2},{1,3},{2,0},{3,1},{4,6},{5,7},{6,4},{7,5},{8,10},{9,11},{10,... | collective-permute-start | bytes 1179656 | tf_op jit(solution)/shard_map/ppermute | solution.py:542
  125.3 16.5 %collective-permute-start.23 = (f32[216,768]{1,0:T(8,128)S(1)}, f32[216,768]{1,0:T(8,128)S(1)}, u32[]{:S(2)}, u32[]{:S(2)}) collective-permute-start(f32[216,768]{1,0:T(8,128)S(1)} %get-tuple-element.218), channel_id=1, source_target_pairs={{0,8},{4,12},{8,0},{12,4},{16,24},{20,28},{24,16},{28,20},{1,9},{5... | collective-permute-start | bytes 1990664 | tf_op jit(solution)/shard_map/ppermute | solution.py:546
  126.9 16.1 %collective-permute-start.24 = (f32[216,768]{1,0:T(8,128)S(1)}, f32[216,768]{1,0:T(8,128)S(1)}, u32[]{:S(2)}, u32[]{:S(2)}) collective-permute-start(f32[216,768]{1,0:T(8,128)S(1)} %get-tuple-element.219), channel_id=1, source_target_pairs={{0,16},{4,20},{8,24},{12,28},{16,0},{20,4},{24,8},{28,12},{1,17},{... | collective-permute-start | bytes 1990664 | tf_op jit(solution)/shard_map/ppermute | solution.py:546
  163.4 16.8 %collective-permute-start.31 = (f32[128,768]{1,0:T(8,128)S(1)}, f32[128,768]{1,0:T(8,128)S(1)}, u32[]{:S(2)}, u32[]{:S(2)}) collective-permute-start(f32[128,768]{1,0:T(8,128)S(1)} %get-tuple-element.247), channel_id=1, source_target_pairs={{0,1},{1,0},{2,3},{3,2},{4,5},{5,4},{6,7},{7,6},{8,9},{9,8},{10,11... | collective-permute-start | bytes 1179656 | tf_op jit(solution)/shard_map/ppermute | solution.py:542
  165.9 14.3 %collective-permute-start.33 = (f32[96,768]{1,0:T(8,128)S(1)}, f32[96,768]{1,0:T(8,128)S(1)}, u32[]{:S(2)}, u32[]{:S(2)}) collective-permute-start(f32[96,768]{1,0:T(8,128)S(1)} %get-tuple-element.252), channel_id=1, source_target_pairs={{0,16},{4,20},{8,24},{12,28},{16,0},{20,4},{24,8},{28,12},{1,17},{... | collective-permute-start | bytes 884744 | tf_op jit(solution)/shard_map/ppermute | solution.py:546
  166.4 13.8 %collective-permute-start.34 = (f32[96,768]{1,0:T(8,128)S(1)}, f32[96,768]{1,0:T(8,128)S(1)}, u32[]{:S(2)}, u32[]{:S(2)}) collective-permute-start(f32[96,768]{1,0:T(8,128)S(1)} %get-tuple-element.253), channel_id=1, source_target_pairs={{0,24},{4,28},{8,16},{12,20},{16,8},{20,12},{24,0},{28,4},{1,25},{... | collective-permute-start | bytes 884744 | tf_op jit(solution)/shard_map/ppermute | solution.py:546
  180.3 18.4 %collective-permute-start.36 = (f32[152,768]{1,0:T(8,128)S(1)}, f32[152,768]{1,0:T(8,128)S(1)}, u32[]{:S(2)}, u32[]{:S(2)}) collective-permute-start(f32[152,768]{1,0:T(8,128)S(1)} %get-tuple-element.263), channel_id=1, source_target_pairs={{0,1},{1,0},{2,3},{3,2},{4,5},{5,4},{6,7},{7,6},{8,9},{9,8},{10,11... | collective-permute-start | bytes 1400840 | tf_op jit(solution)/shard_map/ppermute | solution.py:542
  181.6 15.8 %collective-permute-start.37 = (f32[128,768]{1,0:T(8,128)S(1)}, f32[128,768]{1,0:T(8,128)S(1)}, u32[]{:S(2)}, u32[]{:S(2)}) collective-permute-start(f32[128,768]{1,0:T(8,128)S(1)} %get-tuple-element.264), channel_id=1, source_target_pairs={{0,2},{1,3},{2,0},{3,1},{4,6},{5,7},{6,4},{7,5},{8,10},{9,11},{10,... | collective-permute-start | bytes 1179656 | tf_op jit(solution)/shard_map/ppermute | solution.py:542
  184.6 17.5 %collective-permute-start.38 = (f32[272,768]{1,0:T(8,128)S(1)}, f32[272,768]{1,0:T(8,128)S(1)}, u32[]{:S(2)}, u32[]{:S(2)}) collective-permute-start(f32[272,768]{1,0:T(8,128)S(1)} %get-tuple-element.271), channel_id=1, source_target_pairs={{0,8},{4,12},{8,0},{12,4},{16,24},{20,28},{24,16},{28,20},{1,9},{5... | collective-permute-start | bytes 2506760 | tf_op jit(solution)/shard_map/ppermute | solution.py:546
  185.2 18.2 %collective-permute-start.39 = (f32[272,768]{1,0:T(8,128)S(1)}, f32[272,768]{1,0:T(8,128)S(1)}, u32[]{:S(2)}, u32[]{:S(2)}) collective-permute-start(f32[272,768]{1,0:T(8,128)S(1)} %get-tuple-element.272), channel_id=1, source_target_pairs={{0,16},{4,20},{8,24},{12,28},{16,0},{20,4},{24,8},{28,12},{1,17},{... | collective-permute-start | bytes 2506760 | tf_op jit(solution)/shard_map/ppermute | solution.py:546
  203.4 20.3 %collective-permute-start.40 = (f32[152,768]{1,0:T(8,128)S(1)}, f32[152,768]{1,0:T(8,128)S(1)}, u32[]{:S(2)}, u32[]{:S(2)}) collective-permute-start(f32[152,768]{1,0:T(8,128)S(1)} %get-tuple-element.276), channel_id=1, source_target_pairs={{0,2},{1,3},{2,0},{3,1},{4,6},{5,7},{6,4},{7,5},{8,10},{9,11},{10,... | collective-permute-start | bytes 1400840 | tf_op jit(solution)/shard_map/ppermute | solution.py:542
  203.7 20.0 %collective-permute-start.41 = (f32[152,768]{1,0:T(8,128)S(1)}, f32[152,768]{1,0:T(8,128)S(1)}, u32[]{:S(2)}, u32[]{:S(2)}) collective-permute-start(f32[152,768]{1,0:T(8,128)S(1)} %get-tuple-element.277.r0), channel_id=1, source_target_pairs={{0,1},{1,0},{2,3},{3,2},{4,5},{5,4},{6,7},{7,6},{8,9},{9,8},{10,11... | collective-permute-start | bytes 1400840 | tf_op jit(solution)/shard_map/ppermute | solution.py:542
  205.2 18.6 %collective-permute-start.42 = (f32[272,768]{1,0:T(8,128)S(1)}, f32[272,768]{1,0:T(8,128)S(1)}, u32[]{:S(2)}, u32[]{:S(2)}) collective-permute-start(f32[272,768]{1,0:T(8,128)S(1)} %get-tuple-element.280), channel_id=1, source_target_pairs={{0,24},{4,28},{8,16},{12,20},{16,8},{20,12},{24,0},{28,4},{1,25},{... | collective-permute-start | bytes 2506760 | tf_op jit(solution)/shard_map/ppermute | solution.py:546
  224.2 16.6 %collective-permute-start.45 = (f32[104,768]{1,0:T(8,128)S(1)}, f32[104,768]{1,0:T(8,128)S(1)}, u32[]{:S(2)}, u32[]{:S(2)}) collective-permute-start(f32[104,768]{1,0:T(8,128)S(1)} %pad_maximum_fusion.2.refs_0_), channel_id=1, source_target_pairs={{0,8},{4,12},{8,0},{12,4},{16,24},{20,28},{24,16},{28,20},{1,9},{5... | collective-permute-start | bytes 958472 | tf_op jit(solution)/shard_map/ppermute | solution.py:546
  224.9 15.9 %collective-permute-start.46 = (f32[104,768]{1,0:T(8,128)S(1)}, f32[104,768]{1,0:T(8,128)S(1)}, u32[]{:S(2)}, u32[]{:S(2)}) collective-permute-start(f32[104,768]{1,0:T(8,128)S(1)} %pad_maximum_fusion.2.refs_0_), channel_id=1, source_target_pairs={{0,16},{4,20},{8,24},{12,28},{16,0},{20,4},{24,8},{28,12},{1,17},{... | collective-permute-start | bytes 958472 | tf_op jit(solution)/shard_map/ppermute | solution.py:546
  226.6 15.6 %collective-permute-start.47 = (f32[104,768]{1,0:T(8,128)S(1)}, f32[104,768]{1,0:T(8,128)S(1)}, u32[]{:S(2)}, u32[]{:S(2)}) collective-permute-start(f32[104,768]{1,0:T(8,128)S(1)} %pad_maximum_fusion.2.refs_0_), channel_id=1, source_target_pairs={{0,24},{4,28},{8,16},{12,20},{16,8},{20,12},{24,0},{28,4},{1,25},{... | collective-permute-start | bytes 958472 | tf_op jit(solution)/shard_map/ppermute | solution.py:546
  (45 other events, 778.1 us)

commit v4 on v3

--- a/solution.py
+++ b/solution.py
@@ -233,27 +233,44 @@
     return d_resid, [col_sum(d_final), col_sum(d_final * normal), col_sum(d_resid), col_sum(d_upper)]
 
 
+def finish_rows(block, seg, gain, shift, normal_out, inverse_out, low_out):
+    normal, inverse = norm_stats(block[...])
+    normal_out[...] = normal
+    inverse_out[...] = jnp.broadcast_to(inverse, inverse_out.shape)
+    final = normal * gain + shift
+    low_out[...] = final.astype(bf16)
+    slot_col = lax.broadcasted_iota(jnp.int32, (SENTS, 1), 0)
+    return nn(jnp.where(slot_col == seg, 1.0, 0.0), final, highest)
+
+
+def finish_early(ids, lens, r0, r1, r2, g_ffn, b_ffn, normal_ref, inverse_ref, final_low, pooled_out):
+    rows, width = r0.shape
+    seg_row = segment_of(lens, row_places(ids[0], (1, 4 * rows), 1, rows))
+    pooled = jnp.zeros((SENTS, width), f32)
+    for j, block in enumerate((r0, r1, r2)):
+        at = slice(j * rows, (j + 1) * rows)
+        views = (normal_ref.at[at, :], inverse_ref.at[at, :], final_low.at[at, :])
+        pooled = pooled + finish_rows(block, seg_row[:, at], g_ffn[...], b_ffn[...], *views)
+    pooled_out[...] = pooled
+
+
 def finish_first(
-    ids, lens, r0, r1, r2, r3, g_ffn, b_ffn, out_grad, pool_grad, grad_of, w_down, w_up, *refs
+    ids, lens, r3, early, pooled_in, g_ffn, b_ffn, out_grad, pool_grad, grad_of, w_down, w_up, *refs
 ):
-    outs, (pooled_grad,) = refs[:-1], refs[-1:]
-    part, layer_out, pools, normal_ref, inverse_ref, spread_out, low, up, side = outs
+    outs, (normal_ref, inverse_ref, final_low, pooled_grad) = refs[:-4], refs[-4:]
+    part, layer_out, pools, spread_out, low, up, side = outs
     me = ids[0]
-    rows, width = r0.shape
-    gain, shift = g_ffn[...], b_ffn[...]
+    rows, width = r3.shape
+    gain = g_ffn[...]
     seg_row = segment_of(lens, row_places(me, (1, 4 * rows), 1, rows))
     seg_col = segment_of(lens, row_places(me, (4 * rows, 1), 0, rows))
     slot_col = lax.broadcasted_iota(jnp.int32, (SENTS, 1), 0)
-    pooled = jnp.zeros((SENTS, width), f32)
-    for j, block in enumerate((r0, r1, r2, r3)):
-        at = slice(j * rows, (j + 1) * rows)
-        normal, inverse = norm_stats(block[...])
-        normal_ref[at, :] = normal
-        inverse_ref[at, :] = jnp.broadcast_to(inverse, (rows, 128))
-        final = normal * gain + shift
-        layer_out[chunk(me, j, rows), :] = final.astype(bf16)
-        member = jnp.where(slot_col == seg_row[:, at], 1.0, 0.0)
-        pooled = pooled + nn(member, final, highest)
+    for j in range(3):
+        layer_out[chunk(me, j, rows), :] = early[j * rows : (j + 1) * rows, :]
+    pooled = pooled_in[...] + finish_rows(
+        r3, seg_row[:, 3 * rows :], gain, b_ffn[...], normal_ref, inverse_ref, final_low
+    )
+    layer_out[chunk(me, 3, rows), :] = final_low[...]
     denom = jnp.zeros((SENTS, 1), f32)
     for s in range(SENTS):
         size = jnp.maximum(lens[0, s], 1).astype(f32)
@@ -276,8 +293,8 @@
     spread_out[...] = spread
     _, sums = finish_chunk(
         seg_col[3 * rows :],
-        normal_ref[3 * rows :, :],
-        inverse_ref[3 * rows :, :1],
+        normal_ref[...],
+        inverse_ref[:, :1],
         gain,
         spread,
         out_grad[chunk(me, 3, rows), :],
@@ -460,37 +477,63 @@
     out[...] = a[...] + b[...]
 
 
-def cut(block, out):
-    out[...] = block[: out.shape[0], :]
-
-
-def join_terms(part1, part2, far, *refs):
-    blocks, (near_out, across_out, terms) = refs[:-3], refs[-3:]
+def join_terms(part1, part2, far, o0, o1, o2, o3, near_out, across_out):
     rows = part1.shape[0]
+    piece = o3.shape[0]
     near_out[:rows, :] = part1[...]
+    near_out[rows:, :] = (o0[3 * piece :, :] + o1[3 * piece :, :]) + (o2[3 * piece :, :] + o3[...])
     across_out[...] = part2[...] + far[...]
-    piece = terms.shape[1]
-    for n in range(4):
-        at = slice(n * piece, (n + 1) * piece)
-        total = blocks[0][at, :]
-        for block in blocks[1:]:
-            total = total + block[at, :]
-        terms[n] = total
-    near_out[rows:, :] = terms[3]
-
-
-def join_own(own, near, across, d_hidden, terms, near_out, across_out):
+
+
+def join_own(own, near, across, d_hidden, o0, o1, o2, o3, near_out, across_out, term):
     rows = own.shape[0]
-    piece = terms.shape[1]
+    piece = term.shape[0]
     total = own[...] + near[:rows, :] + across[...] + d_hidden[...]
     near_out[:rows, :] = total
     across_out[:rows, :] = total
-    near_out[rows:, :] = terms[1]
-    across_out[rows:, :] = terms[2] + near[rows : rows + piece, :]
+    for n, out, at in ((0, term, 0), (1, near_out, rows), (2, across_out, rows)):
+        rest = slice(n * piece, (n + 1) * piece)
+        sums = (o0[rest, :] + o1[rest, :]) + (o2[rest, :] + o3[rest, :])
+        if n == 2:
+            sums = sums + near[rows:, :]
+        out[at : at + piece, :] = sums
+
+
+def join_far(across, near, term, out, out_own):
+    rows = out.shape[0]
+    out[...] = across[:rows, :]
+    out_own[...] = term[...] + near[rows:, :] + across[rows:, :]
+
+
+def spread_halves(out, start, extra, half, from_x, from_y, last_y, last_x):
+    more = extra.shape[0] // 2
+    out[start : start + 2 * more, :] = extra[...]
+    start += 2 * more
+    for block, at in (
+        (from_x, 2 * half),
+        (last_x, half),
+        (last_y, half),
+        (from_y, 2 * half),
+        (last_y, half + more),
+        (last_x, half + more),
+    ):
+        out[start : start + more, :] = block[at : at + more, :]
+        start += more
+    return start
+
+
+def collect(own, ffn_sum, from_x, from_y, last_y, last_x, out_own, pools, *refs):
+    pool_moves, (qkv_sum, mine) = refs[:4], refs[4:]
+    qkv_sum[own.shape[0] :, :] = out_own[...]
+    half = own.shape[0] // 2
+    qkv_sum[:half, :] = own[:half, :] + from_x[:half, :] + last_y[:half, :]
+    qkv_sum[half : 2 * half, :] = own[half:, :] + from_y[:half, :] + last_x[:half, :]
+    start = spread_halves(mine, 0, ffn_sum, half, from_x, from_y, last_y, last_x)
+    spread_halves(mine, start, pools, ffn_sum.shape[0] // 2, *pool_moves)
 
 
 def place(me, r0, r1, r2, r3, out):
-    rows = r3.shape[0]
+    rows = out.shape[0] // 4
     for j, block in enumerate((r0, r1, r2, r3)):
         out[chunk(me[0], j, rows), :] = block[:rows, :]
 
@@ -524,7 +567,8 @@
 
 
 def unpack_attn(ids, *refs):
-    blocks, (q_out, k_out, v_out, o_out, side, held) = refs[:8], refs[8:]
+    blocks, outs, (held, side) = refs[:8], refs[8:-2], refs[-2:]
+    q_out, k_out, v_out, o_out, *vectors = outs
     cols = o_out.shape[0]
     step = 3 * cols // 8
     small = cols // 8
@@ -536,6 +580,10 @@
     q_out[...] = held[:cols, :]
     k_out[...] = held[cols : 2 * cols, :]
     v_out[...] = held[2 * cols :, :]
+    vectors[0][...] = side[4, :cols]
+    vectors[1][...] = side[4, cols : 2 * cols]
+    for n, r in enumerate((8, 9, 10, 3, 2, 1, 0)):
+        vectors[2 + n][...] = side[r, :]
 
 
 def swap(block, k):
@@ -563,16 +611,28 @@
     return even.reshape(4, flat, even.shape[-1]), other.reshape(4, flat, even.shape[-1])
 
 
-def fold_call(even, other, extra=()):
+def halves_start(even, other, extra):
     _, rows, width = even.shape
-    more = sum(item.shape[0] for item in extra)
-    blocks = call(
-        fold,
-        [shape(rows, width)] + [shape(rows + more, width)] * 3,
-        [even, other, *extra],
+    half, more = rows // 2, extra.shape[0] // 2
+    return call(
+        fold_halves,
+        [shape(rows, width)] + [shape(rows + more, width)] * 2 + [shape(half, width)] * 2,
+        [even, other, extra],
         moved=3 * even.size * 4,
     )
-    return list(blocks)
+
+
+def halves_next(keep_y, keep_x, extra, from_x, from_y):
+    half, more = keep_y.shape[0], extra.shape[0] // 2
+    to_y = [keep_y + from_x[half : 2 * half], extra[:more], from_x[2 * half :]]
+    to_x = [keep_x + from_y[half : 2 * half], extra[more:], from_y[2 * half :]]
+    return jnp.concatenate(to_y), jnp.concatenate(to_x)
+
+
+def halves_end(own, from_x, from_y, last_y, last_x):
+    half = own.shape[0] // 2
+    terms = [from_x[:half] + last_y[:half], from_y[:half] + last_x[:half]]
+    return own + jnp.concatenate(terms)
 
 
 def with_other_core(blocks, n_dp):
@@ -692,24 +752,35 @@
         across, near = swap(own, 2), swap(own, 1)
         across, near = together(across, near)
         resid = [own, near, across, swap(across, 1)]
-        part3, layer_out, own_pools, normal, inverse, spread, low3, up3, side3 = call(
+        normal, inverse, early, pooled = call(
+            finish_early,
+            [shape(3 * rows, width), shape(3 * rows, 128)]
+            + [shape(3 * rows, width, kind=bf16), shape(SENTS, width)],
+            [ids, lengths, *resid[:3], row(g_ffn), row(b_ffn)],
+            flops=slots * width * 100,
+            moved=3 * slots * width * 4,
+        )
+        part3, layer_out, own_pools, spread, low3, up3, side3 = call(
             finish_first,
             [
                 shape(rows, width),
                 shape(slots, width, kind=bf16),
                 shape(3 * SENTS, width),
-                shape(slots, width),
-                shape(slots, 128),
                 shape(SENTS, width),
                 shape(rows, width, kind=bf16),
                 shape(rows, units, kind=bf16),
                 shape(8, width),
             ],
-            [ids, lengths, *resid, row(g_ffn), row(b_ffn), out_grad, pool_grad, slope]
-            + [w_down, w_up],
+            [ids, lengths, resid[3], early, pooled, row(g_ffn), row(b_ffn), out_grad, pool_grad]
+            + [slope, w_down, w_up],
             flops=4 * rows * width * units,
             moved=6 * slots * width * 4,
-            scratch=[pltpu.VMEM((SENTS, width), f32)],
+            scratch=[
+                pltpu.VMEM((rows, width), f32),
+                pltpu.VMEM((rows, 128), f32),
+                pltpu.VMEM((rows, width), bf16),
+                pltpu.VMEM((SENTS, width), f32),
+            ],
         )
         far = swap(part3, 1)
         step = 2 * width // 8
@@ -730,13 +801,7 @@
         part2 = call(add, shape(rows, width), [parts[2], far], flops=100 * order)
         part2, part1, even, other = together(part2, parts[1], even, other)
         across, near = swap(part2, 2), swap(part1, 1)
-        half, more = step // 2, 3 * SENTS // 2
-        ffn_own, to_x, to_y, keep_y, keep_x = call(
-            fold_halves,
-            [shape(step, width)] + [shape(step + more, width)] * 2 + [shape(half, width)] * 2,
-            [even, other, own_pools],
-            moved=3 * even.size * 4,
-        )
+        ffn_own, to_x, to_y, keep_y, keep_x = halves_start(even, other, own_pools)
         from_x, from_y = swap_dp(to_x, 2, n_dp), swap_dp(to_y, 4, n_dp)
         *sent, d_hidden, hidden_low = call(
             back_hidden,
@@ -750,8 +815,7 @@
             *sent, d_hidden, hidden_low, from_x, from_y, keep_x, keep_y
         )
         d_mixed = [sent[0]] + [swap(sent[n], n) for n in (1, 2, 3)]
-        to_y = jnp.concatenate([keep_y + from_x[half:step], own_pools[:more], from_x[step:]])
-        to_x = jnp.concatenate([keep_x + from_y[half:step], own_pools[more:], from_y[step:]])
+        to_y, to_x = halves_next(keep_y, keep_x, own_pools, from_x, from_y)
         last_y, last_x = swap_dp(to_y, 4, n_dp), swap_dp(to_x, 2, n_dp)
         even, odd = call(
             out_grads,
@@ -777,14 +841,16 @@
             ],
         )
         part3, out_even, out_other, last_x, last_y = together(parts[3], even, other, last_x, last_y)
-        ffn_sum = jnp.concatenate([from_x[:half] + last_y[:half], from_y[:half] + last_x[:half]])
-        ffn_sum = rest_of_dp(ffn_own + ffn_sum, n_dp)
-        all_pools = [own_pools, from_x[step:], last_x[half : half + more]]
-        all_pools += [last_y[half : half + more], from_y[step:]]
-        all_pools += [last_y[half + more :], last_x[half + more :]]
         far = swap(part3, 1)
-        out = fold_call(out_even, out_other)
-        out[1:] = [swap_dp(out[n], 2 * n, n_dp) for n in (1, 2, 3)]
+        ffn_sum = rest_of_dp(halves_end(ffn_own, from_x, from_y, last_y, last_x), n_dp)
+        pool_moves = [from_x, from_y, last_y, last_x]
+        out = call(
+            fold,
+            [shape(4 * piece, width)] * 4,
+            [out_even, out_other],
+            moved=3 * out_even.size * 4,
+        )
+        out_x, out_y = swap_dp(out[1], 2, n_dp), swap_dp(out[2], 4, n_dp)
         even, odd = call(
             qkv_grads,
             [shape(4, 3 * piece + 8, width)] * 2,
@@ -794,39 +860,63 @@
             scratch=[pltpu.VMEM((3 * cols + 64, width), f32)],
         )
         even, other = core_swap(even, odd, n_dp)
+        out_d = swap_dp(out[3][3 * piece :], 6, n_dp)
+        pieces = [out[0], out_x, out_y, out_d]
         if n_dp > 8:
-            out = [rest_of_dp(sum(out), n_dp)]
-        part1, part2, terms = call(
+            pieces[3] = rest_of_dp(sum(item[-piece:] for item in pieces), n_dp)
+            pieces[:3] = [jnp.zeros_like(item) for item in pieces[:3]]
+        part1, part2 = call(
             join_terms,
-            [shape(rows + piece, width), shape(rows, width), shape(4, piece, width)],
-            [parts[1], parts[2], far, *out],
+            [shape(rows + piece, width), shape(rows, width)],
+            [parts[1], parts[2], far, *pieces],
             flops=20 * order,
         )
-        part2, part1, terms, even, other = together(part2, part1, terms, even, other)
+        part2, part1, even, other, out_x, out_y, out_d = together(
+            part2, part1, even, other, out_x, out_y, out[3][: 3 * piece]
+        )
         across, near = swap(part2, 2), swap(part1, 1)
-        qkv = fold_call(even, other, [ffn_sum])
-        from_x, from_y = swap_dp(qkv[1], 2, n_dp), swap_dp(qkv[2], 4, n_dp)
-        own_near, own_across = call(
+        out_d = swap_dp(out_d, 6, n_dp)
+        qkv_own, to_x, to_y, keep_y, keep_x = halves_start(even, other, ffn_sum)
+        from_x, from_y = swap_dp(to_x, 2, n_dp), swap_dp(to_y, 4, n_dp)
+        pieces = [out[0], out_x, out_y, out_d]
+        if n_dp > 8:
+            pieces[0] = rest_of_dp(sum(item[: 3 * piece] for item in pieces), n_dp)
+            pieces[1:] = [jnp.zeros_like(pieces[0])] * 3
+        own_near, own_across, term = call(
             join_own,
-            [shape(rows + piece, width)] * 2,
-            [parts[0], near, across, d_hidden, terms],
+            [shape(rows + piece, width)] * 2 + [shape(piece, width)],
+            [parts[0], near, across, d_hidden, *pieces],
             flops=30 * order,
             moved=7 * rows * width * 4,
         )
-        own_near, own_across, from_x, from_y, qkv_last = together(
-            own_near, own_across, from_x, from_y, qkv[3]
+        own_near, own_across, from_x, from_y, keep_x, keep_y = together(
+            own_near, own_across, from_x, from_y, keep_x, keep_y
         )
         across, near = swap(own_across, 2), swap(own_near, 1)
-        from_d = swap_dp(qkv_last, 6, n_dp)
-        across, near = together(across, near)
-        across_rows = call(cut, shape(rows, width), [across], flops=20 * order)
-        across_rows, near, across, from_d = together(across_rows, near, across, from_d)
-        far = swap(across_rows, 1)
-        low = 3 * piece + 8
-        qkv_sum = rest_of_dp(qkv[0] + from_x[:low] + from_y[:low] + from_d[:low], n_dp)
-        attn_own = jnp.concatenate([qkv_sum, terms[0] + near[rows:] + across[rows:]])
+        to_y, to_x = halves_next(keep_y, keep_x, ffn_sum, from_x, from_y)
+        last_y, last_x = swap_dp(to_y, 4, n_dp), swap_dp(to_x, 2, n_dp)
+        far, out_own = call(
+            join_far,
+            [shape(rows, width), shape(piece, width)],
+            [across, near, term],
+            flops=30 * order,
+        )
+        far, near, across, out_own, last_y, last_x = together(
+            far, near, across, out_own, last_y, last_x
+        )
+        far = swap(far, 1)
+        attn_own, mine = call(
+            collect,
+            [shape(4 * piece + 8, width), shape(4 * (step + 3 * SENTS), width)],
+            [qkv_own, ffn_sum, from_x, from_y, last_y, last_x, out_own]
+            + [own_pools, *pool_moves],
+            flops=1 * order,
+            moved=8 * 4 * step * width,
+        )
+        if n_dp > 8:
+            low = 3 * piece + 8
+            attn_own = jnp.concatenate([rest_of_dp(attn_own[:low], n_dp), attn_own[low:]])
         attn_blocks = [attn_own] + [swap_dp(attn_own, 2 * n, n_dp) for n in (1, 2, 3)]
-        mine = jnp.concatenate([ffn_sum, from_x[low:], from_y[low:], from_d[low:], *all_pools])
         wide = pool_grad.shape[1]
         d_w_up, d_w_down, pools = call(
             unpack_ffn,
@@ -836,27 +926,24 @@
             scratch=[pltpu.VMEM((3, 8 * SENTS, width), f32)],
         )
         d_tokens = call(
-            place, shape(slots, width), [ids, own_near, near, across, far], moved=8 * slots * width
+            place, shape(slots, width), [ids, own_near, near, across, far], flops=30 * order
         )
         d_w_up, d_w_down, pools, d_tokens, *attn_blocks = together(
             d_w_up, d_w_down, pools, d_tokens, *attn_blocks
         )
-        attn_blocks = with_other_core(attn_blocks, n_dp)
+        d_w_query, d_w_key, d_w_value, d_w_out, *vectors = call(
+            unpack_attn,
+            [shape(cols, width)] * 4 + [shape(cols)] * 2 + [shape(width)] * 7,
+            [ids, *with_other_core(attn_blocks, n_dp)],
+            moved=8 * 4 * cols * width,
+            scratch=[pltpu.VMEM((3 * cols, width), f32), pltpu.VMEM((64, width), f32)],
+        )
+        b_q, b_v, d_b_out, d_g_attn, d_b_attn, d_b_up, d_b_down, d_g_ffn, d_b_ffn = vectors
         pools = pools.T
         if n_dp > 8:
             third = [own_pools[n * SENTS : (n + 1) * SENTS] for n in range(3)]
             third = jnp.concatenate(third, axis=1)[:, :wide]
             pools = lax.all_gather(third, "dp", axis=0, tiled=True)
-        d_w_query, d_w_key, d_w_value, d_w_out, vectors = call(
-            unpack_attn,
-            [shape(cols, width)] * 4 + [shape(64, width)],
-            [ids, *attn_blocks],
-            moved=8 * 4 * cols * width,
-            scratch=[pltpu.VMEM((3 * cols, width), f32)],
-        )
-        b_q, b_v = vectors[4, :cols], vectors[4, cols : 2 * cols]
-        d_b_out, d_g_attn, d_b_attn = vectors[8], vectors[9], vectors[10]
-        d_b_up, d_b_down, d_g_ffn, d_b_ffn = vectors[3], vectors[2], vectors[1], vectors[0]
         return (
             layer_out,
             pools,

time: 249 us -> 243 us (0.976)
  waiting for transfers between devices: 143 us -> 135 us
  starting transfers between devices: 59.4 us -> 62.4 us
    ppermute x24, waiting for transfers between devices: 102 us -> 93.1 us  [swap(): return lax.ppermute(block, 'tensor', swaps[k])]
    ppermute x28 -> x30, starting transfers between devices: 22.5 us -> 24.8 us  [swap_dp(): return lax.ppermute(block, 'dp', [(i, i ^ k) for i in range(n_dp)])]
    pallas_call x21 -> x23, Pallas kernels: 41.7 us -> 42.4 us  [call(): pl.pallas_call(body, out_shape=outs, in_specs=specs, out_specs=jax.tree.m...]
    ppermute x28 -> x30, waiting for transfers between devices: 41.5 us -> 41.5 us  [swap_dp(): return lax.ppermute(block, 'dp', [(i, i ^ k) for i in range(n_dp)])]
  transfers between devices with their start and end apart: 52 -> 54, of which waited for: 35 -> 36; matrix products, arithmetic and copies ran while one was open for 0% -> 0% of each run, Pallas kernels for 13% -> 14%
where the time goes in v4:
time: 243 us
  waiting for transfers between devices  135 us (56%)
  starting transfers between devices  62.4 us (26%)
  Pallas kernels  42.4 us (17%)
    ppermute x24, waiting for transfers between devices, swap(): return lax.ppermute(block, 'tensor', swaps[k])  93.1 us
    pallas_call x23, Pallas kernels, call(): pl.pallas_call(body, out_shape=outs, in_specs=specs, out_specs=jax.tree.m...  42.4 us
    ppermute x30, waiting for transfers between devices, swap_dp(): return lax.ppermute(block, 'dp', [(i, i ^ k) for i in range(n_dp)])  41.5 us
    ppermute x24, starting transfers between devices, swap(): return lax.ppermute(block, 'tensor', swaps[k])  37.6 us
    ppermute x30, starting transfers between devices, swap_dp(): return lax.ppermute(block, 'dp', [(i, i ^ k) for i in range(n_dp)])  24.8 us
  transfers between devices with their start and end apart: 54, of which 36 were waited for; matrix products, arithmetic and copies ran while one was open for 0% of the time, Pallas kernels for 14%

profile of v4, /device:TPU:0, one launch (start us, length us, event | category | flops | bytes accessed | tf_op | source)
XLA Modules:
  0.0 242.5 jit_solution(9645353031340272127)
XLA Ops:
  7.2 8.0 %shard_map.322 = (bf16[512,768]{1,0:T(8,128)(2,1)S(1)}, bf16[512,192]{1,0:T(8,128)(2,1)S(1)}, bf16[512,192]{1,0:T(8,128)(2,1)S(1)}, bf16[512,192]{1,0:T(8,128)(2...) custom-call(s32[2]{0:T(128)S(1)} %pad_add_fusion.ids.me, s32[1,16]{1,0:T(1,128)} %lens.5, ...), custom_call_target="tpu_custom_call" | custom-call | flops 654311424 | bytes 4030464 | tf_op jit(solution)/shard_map/pallas_call | solution.py:65
  23.3 6.4 %collective-permute-done.5.refs_2_ = f32[4,24,768]{2,1,0:T(8,128)S(1)} collective-permute-done((f32[4,24,768]{2,1,0:T(8,128)S(1)}, f32[4,24,768]{2,1,0:T(8,128)S(1)}, u32[]{:S(2)}, u32[]{:S(2)}) %collective-permute-start.5) | collective-permute-done | bytes 294944 | tf_op jit(solution)/shard_map/ppermute | solution.py:594
  29.7 5.0 %collective-permute-done.6.refs_4_ = f32[4,24,768]{2,1,0:T(8,128)S(1)} collective-permute-done((f32[4,24,768]{2,1,0:T(8,128)S(1)}, f32[4,24,768]{2,1,0:T(8,128)S(1)}, u32[]{:S(2)}, u32[]{:S(2)}) %collective-permute-start.6) | collective-permute-done | bytes 294944 | tf_op jit(solution)/shard_map/ppermute | solution.py:594
  39.4 5.8 %collective-permute-done.8.m3 = f32[768,128]{1,0:T(8,128)S(1)} collective-permute-done((f32[768,128]{1,0:T(8,128)S(1)}, f32[768,128]{1,0:T(8,128)S(1)}, u32[]{:S(2)}, u32[]{:S(2)}) %collective-permute-start.8) | collective-permute-done | bytes 393248 | tf_op jit(solution)/shard_map/ppermute | solution.py:590
  47.3 4.1 %shard_map.325 = (f32[128,768]{1,0:T(8,128)S(1)}, f32[128,768]{1,0:T(8,128)S(1)}, f32[128,768]{1,0:T(8,128)S(1)}, bf16[512,768]{1,0:T(8,128)(2,1)S(1)}, f32[512,...) custom-call(bf16[512,768]{1,0:T(8,128)(2,1)S(1)} %get-tuple-element., ...), custom_call_target="tpu_custom_call" | custom-call | flops 1358954496 | bytes 8257536 | tf_op jit(solution)/shard_map/pallas_call | solution.py:65
  52.0 3.8 %collective-permute-done.13 = f32[128,768]{1,0:T(8,128)S(1)} collective-permute-done((f32[128,768]{1,0:T(8,128)S(1)}, f32[128,768]{1,0:T(8,128)S(1)}, u32[]{:S(2)}, u32[]{:S(2)}) %collective-permute-start.13) | collective-permute-done | bytes 393248 | tf_op jit(solution)/shard_map/ppermute | solution.py:590
  55.9 3.2 %collective-permute-start.15 = (f32[128,768]{1,0:T(8,128)S(1)}, f32[128,768]{1,0:T(8,128)S(1)}, u32[]{:S(2)}, u32[]{:S(2)}) collective-permute-start(f32[128,768]{1,0:T(8,128)S(1)} %add.44), channel_id=1, source_target_pairs={{0,2},{1,3},{2,0},{3,1},{4,6},{5,7},{6,4},{7,5},{8,10},{9,11},{10,... | collective-permute-start | bytes 1179656 | tf_op jit(solution)/shard_map/ppermute | solution.py:590
  60.9 14.3 %collective-permute-done.15 = f32[128,768]{1,0:T(8,128)S(1)} collective-permute-done((f32[128,768]{1,0:T(8,128)S(1)}, f32[128,768]{1,0:T(8,128)S(1)}, u32[]{:S(2)}, u32[]{:S(2)}) %collective-permute-start.15) | collective-permute-done | bytes 393248 | tf_op jit(solution)/shard_map/ppermute | solution.py:590
  79.3 15.3 %collective-permute-done.16.r2 = f32[128,768]{1,0:T(8,128)S(1)} collective-permute-done((f32[128,768]{1,0:T(8,128)S(1)}, f32[128,768]{1,0:T(8,128)S(1)}, u32[]{:S(2)}, u32[]{:S(2)}) %collective-permute-start.16) | collective-permute-done | bytes 393248 | tf_op jit(solution)/shard_map/ppermute | solution.py:590
  96.3 7.3 %collective-permute-done.18.r3 = f32[128,768]{1,0:T(8,128)S(1)} collective-permute-done((f32[128,768]{1,0:T(8,128)S(1)}, f32[128,768]{1,0:T(8,128)S(1)}, u32[]{:S(2)}, u32[]{:S(2)}) %collective-permute-start.18) | collective-permute-done | bytes 393248 | tf_op jit(solution)/shard_map/ppermute | solution.py:590
  103.6 3.8 %shard_map.328 = (f32[128,768]{1,0:T(8,128)S(1)}, bf16[512,768]{1,0:T(8,128)(2,1)}, f32[48,768]{1,0:T(8,128)S(1)}, f32[16,768]{1,0:T(8,128)S(1)}, bf16[128,768]{...) custom-call(s32[2]{0:T(128)S(1)} %pad_add_fusion.ids.me, s32[1,16]{1,0:T(1,128)S(1)} %copy-done.6, ...), custom_call_target="tpu_custom_call" | custom-call | flops 301989888 | bytes 9437184 | tf_op jit(solution)/shard_map/pallas_call | solution.py:65
  107.9 6.3 %shard_map.329 = (f32[128,768]{1,0:T(8,128)S(1)}, f32[128,768]{1,0:T(8,128)S(1)}, f32[128,768]{1,0:T(8,128)S(1)}, f32[128,768]{1,0:T(8,128)S(1)}, f32[8,768]{1,0...) custom-call(s32[2]{0:T(128)S(1)} %pad_add_fusion.ids.me, s32[1,16]{1,0:T(1,128)S(1)} %copy-done.6, ...), custom_call_target="tpu_custom_call" | custom-call | flops 2415919104 | bytes 14155776 | tf_op jit(solution)/shard_map/pallas_call | solution.py:65
  115.5 3.3 %collective-permute-done.20.theirs = f32[4,192,768]{2,1,0:T(8,128)S(1)} collective-permute-done((f32[4,192,768]{2,1,0:T(8,128)S(1)}, f32[4,192,768]{2,1,0:T(8,128)S(1)}, u32[]{:S(2)}, u32[]{:S(2)}) %collective-permute-start.20) | collective-permute-done | bytes 2359328 | tf_op jit(solution)/shard_map/ppermute | solution.py:594
  120.4 3.4 %collective-permute-start.22 = (f32[128,768]{1,0:T(8,128)S(1)}, f32[128,768]{1,0:T(8,128)S(1)}, u32[]{:S(2)}, u32[]{:S(2)}) collective-permute-start(f32[128,768]{1,0:T(8,128)S(1)} %shard_map.330), channel_id=1, source_target_pairs={{0,2},{1,3},{2,0},{3,1},{4,6},{5,7},{6,4},{7,5},{8,10},{9,11},{10,... | collective-permute-start | bytes 1179656 | tf_op jit(solution)/shard_map/ppermute | solution.py:590
  127.2 11.2 %collective-permute-done.21.near = f32[128,768]{1,0:T(8,128)S(1)} collective-permute-done((f32[128,768]{1,0:T(8,128)S(1)}, f32[128,768]{1,0:T(8,128)S(1)}, u32[]{:S(2)}, u32[]{:S(2)}) %collective-permute-start.21) | collective-permute-done | bytes 393248 | tf_op jit(solution)/shard_map/ppermute | solution.py:590
  151.1 3.7 %collective-permute-done.26.e2 = f32[224,128]{1,0:T(8,128)S(1)} collective-permute-done((f32[224,128]{1,0:T(8,128)S(1)}, f32[224,128]{1,0:T(8,128)S(1)}, u32[]{:S(2)}, u32[]{:S(2)}) %collective-permute-start.26) | collective-permute-done | bytes 114720 | tf_op jit(solution)/shard_map/ppermute | solution.py:590
  154.8 3.5 %shard_map.333 = (f32[128,768]{1,0:T(8,128)S(1)}, f32[128,768]{1,0:T(8,128)S(1)}, f32[128,768]{1,0:T(8,128)S(1)}, f32[128,768]{1,0:T(8,128)S(1)}, bf16[512,576]{...) custom-call(f32[224,128]{1,0:T(8,128)S(1)} %get-tuple-element.245.e0, ...), custom_call_target="tpu_custom_call" | custom-call | flops 10000000000 | bytes 4718592 | tf_op jit(solution)/shard_map/pallas_call | solution.py:65
  158.3 3.9 %collective-permute-done.29.refs_3_ = f32[144,768]{1,0:T(8,128)S(1)} collective-permute-done((f32[144,768]{1,0:T(8,128)S(1)}, f32[144,768]{1,0:T(8,128)S(1)}, u32[]{:S(2)}, u32[]{:S(2)}) %collective-permute-start.29) | collective-permute-done | bytes 442400 | tf_op jit(solution)/shard_map/ppermute | solution.py:594
  168.6 4.5 %collective-permute-done.34.o3 = f32[24,768]{1,0:T(8,128)S(1)} collective-permute-done((f32[24,768]{1,0:T(8,128)S(1)}, f32[24,768]{1,0:T(8,128)S(1)}, u32[]{:S(2)}, u32[]{:S(2)}) %collective-permute-start.34) | collective-permute-done | bytes 73760 | tf_op jit(solution)/shard_map/ppermute | solution.py:594
  182.3 5.4 %collective-permute-done.38.o3 = f32[72,768]{1,0:T(8,128)S(1)} collective-permute-done((f32[72,768]{1,0:T(8,128)S(1)}, f32[72,768]{1,0:T(8,128)S(1)}, u32[]{:S(2)}, u32[]{:S(2)}) %collective-permute-start.38) | collective-permute-done | bytes 221216 | tf_op jit(solution)/shard_map/ppermute | solution.py:594
  187.7 4.9 %collective-permute-done.37.across = f32[128,768]{1,0:T(8,128)S(1)} collective-permute-done((f32[128,768]{1,0:T(8,128)S(1)}, f32[128,768]{1,0:T(8,128)S(1)}, u32[]{:S(2)}, u32[]{:S(2)}) %collective-permute-start.37) | collective-permute-done | bytes 393248 | tf_op jit(solution)/shard_map/ppermute | solution.py:590
  200.9 17.6 %collective-permute-done.41.across.r2 = f32[152,768]{1,0:T(8,128)S(1)} collective-permute-done((f32[152,768]{1,0:T(8,128)S(1)}, f32[152,768]{1,0:T(8,128)S(1)}, u32[]{:S(2)}, u32[]{:S(2)}) %collective-permute-start.41) | collective-permute-done | bytes 466976 | tf_op jit(solution)/shard_map/ppermute | solution.py:590
  222.5 6.1 %collective-permute-done.46.r3 = f32[128,768]{1,0:T(8,128)S(1)} collective-permute-done((f32[128,768]{1,0:T(8,128)S(1)}, f32[128,768]{1,0:T(8,128)S(1)}, u32[]{:S(2)}, u32[]{:S(2)}) %collective-permute-start.46) | collective-permute-done | bytes 393248 | tf_op jit(solution)/shard_map/ppermute | solution.py:590
  230.5 3.5 %shard_map.342 = (f32[768,768]{1,0:T(8,128)}, f32[768,768]{1,0:T(8,128)}, f32[1728,128]{1,0:T(8,128)}) custom-call(s32[2]{0:T(128)S(1)} %pad_add_fusion.ids.me, f32[960,768]{1,0:T(8,128)S(1)} %get-tuple-element.309.mine, f32[960,768]{1,0:T(8,128)S(1)} %collective-permute-done.45.theirs), custom_call_target="tpu_custom_call" | custom-call | bytes 9437184 | tf_op jit(solution)/shard_map/pallas_call | solution.py:65
  (171 shorter events, 87.0 us)
Async XLA Ops:
  1.5 13.7 %collective-permute-start = (f32[24,768]{1,0:T(8,128)S(1)}, f32[24,768]{1,0:T(8,128)S(1)}, u32[]{:S(2)}, u32[]{:S(2)}) collective-permute-start(f32[24,768]{1,0:T(8,128)S(1)} %dynamic-slice_convert_fusion), channel_id=1, source_target_pairs={{0,1},{1,0},{2,3},{3,2},{4,5},{5,4},{6,7},{7,6},{8,9},{9,8},{10,11... | collective-permute-start | bytes 221192 | tf_op jit(solution)/shard_map/ppermute | solution.py:590
  15.3 19.8 %collective-permute-start.3 = (f32[768,128]{1,0:T(8,128)S(1)}, f32[768,128]{1,0:T(8,128)S(1)}, u32[]{:S(2)}, u32[]{:S(2)}) collective-permute-start(f32[768,128]{1,0:T(8,128)S(1)} %get-tuple-element.180.m0), channel_id=1, source_target_pairs={{0,2},{1,3},{2,0},{3,1},{4,6},{5,7},{6,4},{7,5},{8,10},{9,11},{10,... | collective-permute-start | bytes 1179656 | tf_op jit(solution)/shard_map/ppermute | solution.py:590
  17.2 17.9 %collective-permute-start.4 = (f32[768,128]{1,0:T(8,128)S(1)}, f32[768,128]{1,0:T(8,128)S(1)}, u32[]{:S(2)}, u32[]{:S(2)}) collective-permute-start(f32[768,128]{1,0:T(8,128)S(1)} %get-tuple-element.180.m0), channel_id=1, source_target_pairs={{0,1},{1,0},{2,3},{3,2},{4,5},{5,4},{6,7},{7,6},{8,9},{9,8},{10,11... | collective-permute-start | bytes 1179656 | tf_op jit(solution)/shard_map/ppermute | solution.py:590
  21.3 13.4 %collective-permute-start.6 = (f32[4,24,768]{2,1,0:T(8,128)S(1)}, f32[4,24,768]{2,1,0:T(8,128)S(1)}, u32[]{:S(2)}, u32[]{:S(2)}) collective-permute-start(f32[4,24,768]{2,1,0:T(8,128)S(1)} %pad_maximum_fusion.4.refs_0_), channel_id=1, source_target_pairs={{0,16},{4,20},{8,24},{12,28},{16,0},{20,4},{24,8},{28,12},{1,17},{... | collective-permute-start | bytes 884744 | tf_op jit(solution)/shard_map/ppermute | solution.py:594
  55.9 19.2 %collective-permute-start.15 = (f32[128,768]{1,0:T(8,128)S(1)}, f32[128,768]{1,0:T(8,128)S(1)}, u32[]{:S(2)}, u32[]{:S(2)}) collective-permute-start(f32[128,768]{1,0:T(8,128)S(1)} %add.44), channel_id=1, source_target_pairs={{0,2},{1,3},{2,0},{3,1},{4,6},{5,7},{6,4},{7,5},{8,10},{9,11},{10,... | collective-permute-start | bytes 1179656 | tf_op jit(solution)/shard_map/ppermute | solution.py:590
  59.2 16.1 %collective-permute-start.14 = (f32[128,768]{1,0:T(8,128)S(1)}, f32[128,768]{1,0:T(8,128)S(1)}, u32[]{:S(2)}, u32[]{:S(2)}) collective-permute-start(f32[128,768]{1,0:T(8,128)S(1)} %get-tuple-element.200), channel_id=1, source_target_pairs={{0,1},{1,0},{2,3},{3,2},{4,5},{5,4},{6,7},{7,6},{8,9},{9,8},{10,11... | collective-permute-start | bytes 1179656 | tf_op jit(solution)/shard_map/ppermute | solution.py:590
  75.4 19.2 %collective-permute-start.16 = (f32[128,768]{1,0:T(8,128)S(1)}, f32[128,768]{1,0:T(8,128)S(1)}, u32[]{:S(2)}, u32[]{:S(2)}) collective-permute-start(f32[128,768]{1,0:T(8,128)S(1)} %add_add_fusion.r0), channel_id=1, source_target_pairs={{0,2},{1,3},{2,0},{3,1},{4,6},{5,7},{6,4},{7,5},{8,10},{9,11},{10,... | collective-permute-start | bytes 1179656 | tf_op jit(solution)/shard_map/ppermute | solution.py:590
  77.0 17.7 %collective-permute-start.17 = (f32[128,768]{1,0:T(8,128)S(1)}, f32[128,768]{1,0:T(8,128)S(1)}, u32[]{:S(2)}, u32[]{:S(2)}) collective-permute-start(f32[128,768]{1,0:T(8,128)S(1)} %add_add_fusion.r0), channel_id=1, source_target_pairs={{0,1},{1,0},{2,3},{3,2},{4,5},{5,4},{6,7},{7,6},{8,9},{9,8},{10,11... | collective-permute-start | bytes 1179656 | tf_op jit(solution)/shard_map/ppermute | solution.py:590
  118.8 19.6 %collective-permute-start.21 = (f32[128,768]{1,0:T(8,128)S(1)}, f32[128,768]{1,0:T(8,128)S(1)}, u32[]{:S(2)}, u32[]{:S(2)}) collective-permute-start(f32[128,768]{1,0:T(8,128)S(1)} %get-tuple-element.223), channel_id=1, source_target_pairs={{0,1},{1,0},{2,3},{3,2},{4,5},{5,4},{6,7},{7,6},{8,9},{9,8},{10,11... | collective-permute-start | bytes 1179656 | tf_op jit(solution)/shard_map/ppermute | solution.py:590
  120.4 18.0 %collective-permute-start.22 = (f32[128,768]{1,0:T(8,128)S(1)}, f32[128,768]{1,0:T(8,128)S(1)}, u32[]{:S(2)}, u32[]{:S(2)}) collective-permute-start(f32[128,768]{1,0:T(8,128)S(1)} %shard_map.330), channel_id=1, source_target_pairs={{0,2},{1,3},{2,0},{3,1},{4,6},{5,7},{6,4},{7,5},{8,10},{9,11},{10,... | collective-permute-start | bytes 1179656 | tf_op jit(solution)/shard_map/ppermute | solution.py:590
  124.1 16.5 %collective-permute-start.23 = (f32[216,768]{1,0:T(8,128)S(1)}, f32[216,768]{1,0:T(8,128)S(1)}, u32[]{:S(2)}, u32[]{:S(2)}) collective-permute-start(f32[216,768]{1,0:T(8,128)S(1)} %get-tuple-element.237), channel_id=1, source_target_pairs={{0,8},{4,12},{8,0},{12,4},{16,24},{20,28},{24,16},{28,20},{1,9},{5... | collective-permute-start | bytes 1990664 | tf_op jit(solution)/shard_map/ppermute | solution.py:594
  125.7 16.1 %collective-permute-start.24 = (f32[216,768]{1,0:T(8,128)S(1)}, f32[216,768]{1,0:T(8,128)S(1)}, u32[]{:S(2)}, u32[]{:S(2)}) collective-permute-start(f32[216,768]{1,0:T(8,128)S(1)} %get-tuple-element.238), channel_id=1, source_target_pairs={{0,16},{4,20},{8,24},{12,28},{16,0},{20,4},{24,8},{28,12},{1,17},{... | collective-permute-start | bytes 1990664 | tf_op jit(solution)/shard_map/ppermute | solution.py:594
  149.4 12.8 %collective-permute-start.28 = (f32[4,4,24,768]{3,2,1,0:T(8,128)S(1)}, f32[4,4,24,768]{3,2,1,0:T(8,128)S(1)}, u32[]{:S(2)}, u32[]{:S(2)}) collective-permute-start(f32[4,4,24,768]{3,2,1,0:T(8,128)S(1)} %get-tuple-element.258), channel_id=1, source_target_pairs={{0,4},{4,0},{8,12},{12,8},{16,20},{20,16},{24,28},{28,24},{1,5},{5... | collective-permute-start | bytes 3538952 | tf_op jit(solution)/shard_map/ppermute | solution.py:594
  174.4 19.4 %collective-permute-start.36 = (f32[152,768]{1,0:T(8,128)S(1)}, f32[152,768]{1,0:T(8,128)S(1)}, u32[]{:S(2)}, u32[]{:S(2)}) collective-permute-start(f32[152,768]{1,0:T(8,128)S(1)} %get-tuple-element.285), channel_id=1, source_target_pairs={{0,1},{1,0},{2,3},{3,2},{4,5},{5,4},{6,7},{7,6},{8,9},{9,8},{10,11... | collective-permute-start | bytes 1400840 | tf_op jit(solution)/shard_map/ppermute | solution.py:590
  175.7 16.9 %collective-permute-start.37 = (f32[128,768]{1,0:T(8,128)S(1)}, f32[128,768]{1,0:T(8,128)S(1)}, u32[]{:S(2)}, u32[]{:S(2)}) collective-permute-start(f32[128,768]{1,0:T(8,128)S(1)} %get-tuple-element.286), channel_id=1, source_target_pairs={{0,2},{1,3},{2,0},{3,1},{4,6},{5,7},{6,4},{7,5},{8,10},{9,11},{10,... | collective-permute-start | bytes 1179656 | tf_op jit(solution)/shard_map/ppermute | solution.py:590
  179.9 16.3 %collective-permute-start.39 = (f32[176,768]{1,0:T(8,128)S(1)}, f32[176,768]{1,0:T(8,128)S(1)}, u32[]{:S(2)}, u32[]{:S(2)}) collective-permute-start(f32[176,768]{1,0:T(8,128)S(1)} %get-tuple-element.293), channel_id=1, source_target_pairs={{0,8},{4,12},{8,0},{12,4},{16,24},{20,28},{24,16},{28,20},{1,9},{5... | collective-permute-start | bytes 1622024 | tf_op jit(solution)/shard_map/ppermute | solution.py:594
  180.7 15.5 %collective-permute-start.40 = (f32[176,768]{1,0:T(8,128)S(1)}, f32[176,768]{1,0:T(8,128)S(1)}, u32[]{:S(2)}, u32[]{:S(2)}) collective-permute-start(f32[176,768]{1,0:T(8,128)S(1)} %get-tuple-element.294), channel_id=1, source_target_pairs={{0,16},{4,20},{8,24},{12,28},{16,0},{20,4},{24,8},{28,12},{1,17},{... | collective-permute-start | bytes 1622024 | tf_op jit(solution)/shard_map/ppermute | solution.py:594
  196.3 22.2 %collective-permute-start.41 = (f32[152,768]{1,0:T(8,128)S(1)}, f32[152,768]{1,0:T(8,128)S(1)}, u32[]{:S(2)}, u32[]{:S(2)}) collective-permute-start(f32[152,768]{1,0:T(8,128)S(1)} %get-tuple-element.299), channel_id=1, source_target_pairs={{0,2},{1,3},{2,0},{3,1},{4,6},{5,7},{6,4},{7,5},{8,10},{9,11},{10,... | collective-permute-start | bytes 1400840 | tf_op jit(solution)/shard_map/ppermute | solution.py:590
  196.7 21.8 %collective-permute-start.42 = (f32[152,768]{1,0:T(8,128)S(1)}, f32[152,768]{1,0:T(8,128)S(1)}, u32[]{:S(2)}, u32[]{:S(2)}) collective-permute-start(f32[152,768]{1,0:T(8,128)S(1)} %get-tuple-element.300.r0), channel_id=1, source_target_pairs={{0,1},{1,0},{2,3},{3,2},{4,5},{5,4},{6,7},{7,6},{8,9},{9,8},{10,11... | collective-permute-start | bytes 1400840 | tf_op jit(solution)/shard_map/ppermute | solution.py:590
  198.9 19.7 %collective-permute-start.44 = (f32[232,768]{1,0:T(8,128)S(1)}, f32[232,768]{1,0:T(8,128)S(1)}, u32[]{:S(2)}, u32[]{:S(2)}) collective-permute-start(f32[232,768]{1,0:T(8,128)S(1)} %pad_maximum_fusion.1), channel_id=1, source_target_pairs={{0,8},{4,12},{8,0},{12,4},{16,24},{20,28},{24,16},{28,20},{1,9},{5... | collective-permute-start | bytes 2138120 | tf_op jit(solution)/shard_map/ppermute | solution.py:594
  199.3 19.3 %collective-permute-start.43 = (f32[232,768]{1,0:T(8,128)S(1)}, f32[232,768]{1,0:T(8,128)S(1)}, u32[]{:S(2)}, u32[]{:S(2)}) collective-permute-start(f32[232,768]{1,0:T(8,128)S(1)} %pad_maximum_fusion), channel_id=1, source_target_pairs={{0,16},{4,20},{8,24},{12,28},{16,0},{20,4},{24,8},{28,12},{1,17},{... | collective-permute-start | bytes 2138120 | tf_op jit(solution)/shard_map/ppermute | solution.py:594
  219.0 15.0 %collective-permute-start.47 = (f32[104,768]{1,0:T(8,128)S(1)}, f32[104,768]{1,0:T(8,128)S(1)}, u32[]{:S(2)}, u32[]{:S(2)}) collective-permute-start(f32[104,768]{1,0:T(8,128)S(1)} %get-tuple-element.319.refs_0_), channel_id=1, source_target_pairs={{0,8},{4,12},{8,0},{12,4},{16,24},{20,28},{24,16},{28,20},{1,9},{5... | collective-permute-start | bytes 958472 | tf_op jit(solution)/shard_map/ppermute | solution.py:594
  219.8 15.5 %collective-permute-start.48 = (f32[104,768]{1,0:T(8,128)S(1)}, f32[104,768]{1,0:T(8,128)S(1)}, u32[]{:S(2)}, u32[]{:S(2)}) collective-permute-start(f32[104,768]{1,0:T(8,128)S(1)} %get-tuple-element.319.refs_0_), channel_id=1, source_target_pairs={{0,16},{4,20},{8,24},{12,28},{16,0},{20,4},{24,8},{28,12},{1,17},{... | collective-permute-start | bytes 958472 | tf_op jit(solution)/shard_map/ppermute | solution.py:594
  221.1 16.1 %collective-permute-start.49 = (f32[104,768]{1,0:T(8,128)S(1)}, f32[104,768]{1,0:T(8,128)S(1)}, u32[]{:S(2)}, u32[]{:S(2)}) collective-permute-start(f32[104,768]{1,0:T(8,128)S(1)} %get-tuple-element.319.refs_0_), channel_id=1, source_target_pairs={{0,24},{4,28},{8,16},{12,20},{16,8},{20,12},{24,0},{28,4},{1,25},{... | collective-permute-start | bytes 958472 | tf_op jit(solution)/shard_map/ppermute | solution.py:594
  (47 other events, 625.3 us)

commit v5 on v4

--- a/solution.py
+++ b/solution.py
@@ -145,8 +145,9 @@
     seg_row = segment_of(lens, row_places(me, (1, slots), 1, rows))
     seg_col = segment_of(lens, row_places(me, (slots, 1), 0, rows))
     scale = HDIM**-0.5
-    for j in range(4):
-        at = slice(j * rows, (j + 1) * rows)
+    tall = slots
+    for r in range(0, slots, tall):
+        at = slice(r, r + tall)
         allowed = seg_col[at] == seg_row
         for h in range(cols // HDIM):
             lane = slice(h * HDIM, (h + 1) * HDIM)
@@ -461,14 +462,16 @@
             out[rows:, :] = extra[0][...]
 
 
-def fold_halves(mine, theirs, extra, own, to_x, to_y, keep_y, keep_x):
+def fold_halves(mine, theirs, *refs):
+    extra, (own, to_x, to_y, keep_y, keep_x) = refs[:-5], refs[-5:]
     half = mine.shape[1] // 2
-    more = extra.shape[0] // 2
     own[...] = mine[0] + theirs[0]
     for n, (out, at) in enumerate(((to_x, slice(0, half)), (to_y, slice(half, 2 * half)))):
         for m, block in enumerate((1 + n, 3)):
             out[m * half : (m + 1) * half, :] = mine[block, at, :] + theirs[block, at, :]
-        out[2 * half :, :] = extra[n * more : (n + 1) * more, :]
+        if extra:
+            more = extra[0].shape[0] // 2
+            out[2 * half :, :] = extra[0][n * more : (n + 1) * more, :]
     keep_y[...] = mine[2, :half, :] + theirs[2, :half, :]
     keep_x[...] = mine[1, half:, :] + theirs[1, half:, :]
 
@@ -505,31 +508,29 @@
     out_own[...] = term[...] + near[rows:, :] + across[rows:, :]
 
 
-def spread_halves(out, start, extra, half, from_x, from_y, last_y, last_x):
-    more = extra.shape[0] // 2
-    out[start : start + 2 * more, :] = extra[...]
-    start += 2 * more
-    for block, at in (
-        (from_x, 2 * half),
-        (last_x, half),
-        (last_y, half),
-        (from_y, 2 * half),
-        (last_y, half + more),
-        (last_x, half + more),
+def collect(own, extra, from_x, from_y, last_y, last_x, out_own, sums, mine):
+    half = own.shape[0] // 2
+    sums[:half, :] = own[:half, :] + from_x[:half, :] + last_y[:half, :]
+    sums[half : 2 * half, :] = own[half:, :] + from_y[:half, :] + last_x[:half, :]
+    sums[2 * half :, :] = out_own[...]
+    travel = extra.shape[0] // 2
+    more = 3 * SENTS // 2
+    part = travel - more
+    for n, (block, at) in enumerate(
+        (
+            (extra, 0),
+            (extra, travel),
+            (from_x, 2 * half),
+            (last_x, half),
+            (last_y, half),
+            (from_y, 2 * half),
+            (last_y, half + travel),
+            (last_x, half + travel),
+        )
     ):
-        out[start : start + more, :] = block[at : at + more, :]
-        start += more
-    return start
-
-
-def collect(own, ffn_sum, from_x, from_y, last_y, last_x, out_own, pools, *refs):
-    pool_moves, (qkv_sum, mine) = refs[:4], refs[4:]
-    qkv_sum[own.shape[0] :, :] = out_own[...]
-    half = own.shape[0] // 2
-    qkv_sum[:half, :] = own[:half, :] + from_x[:half, :] + last_y[:half, :]
-    qkv_sum[half : 2 * half, :] = own[half:, :] + from_y[:half, :] + last_x[:half, :]
-    start = spread_halves(mine, 0, ffn_sum, half, from_x, from_y, last_y, last_x)
-    spread_halves(mine, start, pools, ffn_sum.shape[0] // 2, *pool_moves)
+        mine[n * part : (n + 1) * part, :] = block[at : at + part, :]
+        to = 8 * part + n * more
+        mine[to : to + more, :] = block[at + part : at + travel, :]
 
 
 def place(me, r0, r1, r2, r3, out):
@@ -611,28 +612,15 @@
     return even.reshape(4, flat, even.shape[-1]), other.reshape(4, flat, even.shape[-1])
 
 
-def halves_start(even, other, extra):
+def halves_start(even, other, *extra):
     _, rows, width = even.shape
-    half, more = rows // 2, extra.shape[0] // 2
+    half, more = rows // 2, sum(item.shape[0] // 2 for item in extra)
     return call(
         fold_halves,
         [shape(rows, width)] + [shape(rows + more, width)] * 2 + [shape(half, width)] * 2,
-        [even, other, extra],
+        [even, other, *extra],
         moved=3 * even.size * 4,
     )
-
-
-def halves_next(keep_y, keep_x, extra, from_x, from_y):
-    half, more = keep_y.shape[0], extra.shape[0] // 2
-    to_y = [keep_y + from_x[half : 2 * half], extra[:more], from_x[2 * half :]]
-    to_x = [keep_x + from_y[half : 2 * half], extra[more:], from_y[2 * half :]]
-    return jnp.concatenate(to_y), jnp.concatenate(to_x)
-
-
-def halves_end(own, from_x, from_y, last_y, last_x):
-    half = own.shape[0] // 2
-    terms = [from_x[:half] + last_y[:half], from_y[:half] + last_x[:half]]
-    return own + jnp.concatenate(terms)
 
 
 def with_other_core(blocks, n_dp):
@@ -801,7 +789,7 @@
         part2 = call(add, shape(rows, width), [parts[2], far], flops=100 * order)
         part2, part1, even, other = together(part2, parts[1], even, other)
         across, near = swap(part2, 2), swap(part1, 1)
-        ffn_own, to_x, to_y, keep_y, keep_x = halves_start(even, other, own_pools)
+        ffn_own, to_x, to_y, keep_y, keep_x = halves_start(even, other)
         from_x, from_y = swap_dp(to_x, 2, n_dp), swap_dp(to_y, 4, n_dp)
         *sent, d_hidden, hidden_low = call(
             back_hidden,
@@ -815,7 +803,8 @@
             *sent, d_hidden, hidden_low, from_x, from_y, keep_x, keep_y
         )
         d_mixed = [sent[0]] + [swap(sent[n], n) for n in (1, 2, 3)]
-        to_y, to_x = halves_next(keep_y, keep_x, own_pools, from_x, from_y)
+        half = step // 2
+        to_y, to_x = keep_y + from_x[half:], keep_x + from_y[half:]
         last_y, last_x = swap_dp(to_y, 4, n_dp), swap_dp(to_x, 2, n_dp)
         even, odd = call(
             out_grads,
@@ -842,8 +831,12 @@
         )
         part3, out_even, out_other, last_x, last_y = together(parts[3], even, other, last_x, last_y)
         far = swap(part3, 1)
-        ffn_sum = rest_of_dp(halves_end(ffn_own, from_x, from_y, last_y, last_x), n_dp)
-        pool_moves = [from_x, from_y, last_y, last_x]
+        ffn_sum = [ffn_own[:half] + from_x[:half] + last_y, ffn_own[half:] + from_y[:half] + last_x]
+        if n_dp > 8:
+            ffn_sum = [rest_of_dp(item, n_dp) for item in ffn_sum]
+        more = 3 * SENTS // 2
+        extra = [ffn_sum[0], own_pools[:more], ffn_sum[1], own_pools[more:]]
+        extra = jnp.concatenate(extra)
         out = call(
             fold,
             [shape(4 * piece, width)] * 4,
@@ -876,7 +869,7 @@
         )
         across, near = swap(part2, 2), swap(part1, 1)
         out_d = swap_dp(out_d, 6, n_dp)
-        qkv_own, to_x, to_y, keep_y, keep_x = halves_start(even, other, ffn_sum)
+        qkv_own, to_x, to_y, keep_y, keep_x = halves_start(even, other, extra)
         from_x, from_y = swap_dp(to_x, 2, n_dp), swap_dp(to_y, 4, n_dp)
         pieces = [out[0], out_x, out_y, out_d]
         if n_dp > 8:
@@ -893,7 +886,10 @@
             own_near, own_across, from_x, from_y, keep_x, keep_y
         )
         across, near = swap(own_across, 2), swap(own_near, 1)
-        to_y, to_x = halves_next(keep_y, keep_x, ffn_sum, from_x, from_y)
+        low, travel = keep_y.shape[0], half + more
+        to_y = [keep_y + from_x[low : 2 * low], extra[:travel], from_x[2 * low :]]
+        to_x = [keep_x + from_y[low : 2 * low], extra[travel:], from_y[2 * low :]]
+        to_y, to_x = jnp.concatenate(to_y), jnp.concatenate(to_x)
         last_y, last_x = swap_dp(to_y, 4, n_dp), swap_dp(to_x, 2, n_dp)
         far, out_own = call(
             join_far,
@@ -908,8 +904,7 @@
         attn_own, mine = call(
             collect,
             [shape(4 * piece + 8, width), shape(4 * (step + 3 * SENTS), width)],
-            [qkv_own, ffn_sum, from_x, from_y, last_y, last_x, out_own]
-            + [own_pools, *pool_moves],
+            [qkv_own, extra, from_x, from_y, last_y, last_x, out_own],
             flops=1 * order,
             moved=8 * 4 * step * width,
         )

time: 243 us -> 231 us (0.951)
  starting transfers between devices: 62.4 us -> 49.3 us
  waiting for transfers between devices: 135 us -> 139 us
  Pallas kernels: 42.4 us -> 39.6 us
    ppermute x24, starting transfers between devices: 37.6 us -> 25.5 us  [swap(): return lax.ppermute(block, 'tensor', swaps[k])]
    ppermute x24, waiting for transfers between devices: 93.1 us -> 105 us  [swap(): return lax.ppermute(block, 'tensor', swaps[k])]
    ppermute x30, waiting for transfers between devices: 41.5 us -> 34.1 us  [swap_dp(): return lax.ppermute(block, 'dp', [(i, i ^ k) for i in range(n_dp)])]
    pallas_call x23, Pallas kernels: 42.4 us -> 39.6 us  [call(): pl.pallas_call(body, out_shape=outs, in_specs=specs, out_specs=jax.tree.m...]
  transfers between devices with their start and end apart: 54 -> 54, of which waited for: 36 -> 33; matrix products, arithmetic and copies ran while one was open for 0% -> 0% of each run, Pallas kernels for 14% -> 14%
where the time goes in v5:
time: 231 us
  waiting for transfers between devices  139 us (60%)
  starting transfers between devices  49.3 us (21%)
  Pallas kernels  39.6 us (17%)
    ppermute x24, waiting for transfers between devices, swap(): return lax.ppermute(block, 'tensor', swaps[k])  105 us
    pallas_call x23, Pallas kernels, call(): pl.pallas_call(body, out_shape=outs, in_specs=specs, out_specs=jax.tree.m...  39.6 us
    ppermute x30, waiting for transfers between devices, swap_dp(): return lax.ppermute(block, 'dp', [(i, i ^ k) for i in range(n_dp)])  34.1 us
    ppermute x24, starting transfers between devices, swap(): return lax.ppermute(block, 'tensor', swaps[k])  25.5 us
    ppermute x30, starting transfers between devices, swap_dp(): return lax.ppermute(block, 'dp', [(i, i ^ k) for i in range(n_dp)])  23.8 us
  transfers between devices with their start and end apart: 54, of which 33 were waited for; matrix products, arithmetic and copies ran while one was open for 0% of the time, Pallas kernels for 14%

profile of v5, /device:TPU:0, one launch (start us, length us, event | category | flops | bytes accessed | tf_op | source)
XLA Modules:
  0.0 230.6 jit_solution(1806264203711190079)
XLA Ops:
  1.5 5.1 %collective-permute-start.2 = (f32[24,768]{1,0:T(8,128)S(1)}, f32[24,768]{1,0:T(8,128)S(1)}, u32[]{:S(2)}, u32[]{:S(2)}) collective-permute-start(f32[24,768]{1,0:T(8,128)S(1)} %dynamic-slice_convert_fusion), channel_id=1, source_target_pairs={{0,3},{1,2},{2,1},{3,0},{4,7},{5,6},{6,5},{7,4},{8,11},{9,10},{10,... | collective-permute-start | bytes 221192 | tf_op jit(solution)/shard_map/ppermute | solution.py:591
  7.3 5.3 %shard_map.322 = (bf16[512,768]{1,0:T(8,128)(2,1)S(1)}, bf16[512,192]{1,0:T(8,128)(2,1)S(1)}, bf16[512,192]{1,0:T(8,128)(2,1)S(1)}, bf16[512,192]{1,0:T(8,128)(2...) custom-call(s32[2]{0:T(128)S(1)} %pad_add_fusion.ids.me, s32[1,16]{1,0:T(1,128)} %lens.5, ...), custom_call_target="tpu_custom_call" | custom-call | flops 654311424 | bytes 4030464 | tf_op jit(solution)/shard_map/pallas_call | solution.py:65
  20.6 7.3 %collective-permute-done.7.refs_6_ = f32[4,24,768]{2,1,0:T(8,128)S(1)} collective-permute-done((f32[4,24,768]{2,1,0:T(8,128)S(1)}, f32[4,24,768]{2,1,0:T(8,128)S(1)}, u32[]{:S(2)}, u32[]{:S(2)}) %collective-permute-start.7) | collective-permute-done | bytes 294944 | tf_op jit(solution)/shard_map/ppermute | solution.py:595
  27.9 3.7 %collective-permute-done.6.refs_4_ = f32[4,24,768]{2,1,0:T(8,128)S(1)} collective-permute-done((f32[4,24,768]{2,1,0:T(8,128)S(1)}, f32[4,24,768]{2,1,0:T(8,128)S(1)}, u32[]{:S(2)}, u32[]{:S(2)}) %collective-permute-start.6) | collective-permute-done | bytes 294944 | tf_op jit(solution)/shard_map/ppermute | solution.py:595
  37.5 5.2 %collective-permute-done.8.m3 = f32[768,128]{1,0:T(8,128)S(1)} collective-permute-done((f32[768,128]{1,0:T(8,128)S(1)}, f32[768,128]{1,0:T(8,128)S(1)}, u32[]{:S(2)}, u32[]{:S(2)}) %collective-permute-start.8) | collective-permute-done | bytes 393248 | tf_op jit(solution)/shard_map/ppermute | solution.py:591
  44.8 4.1 %shard_map.325 = (f32[128,768]{1,0:T(8,128)S(1)}, f32[128,768]{1,0:T(8,128)S(1)}, f32[128,768]{1,0:T(8,128)S(1)}, bf16[512,768]{1,0:T(8,128)(2,1)S(1)}, f32[512,...) custom-call(bf16[512,768]{1,0:T(8,128)(2,1)S(1)} %get-tuple-element., ...), custom_call_target="tpu_custom_call" | custom-call | flops 1358954496 | bytes 8257536 | tf_op jit(solution)/shard_map/pallas_call | solution.py:65
  49.5 4.2 %collective-permute-done.13 = f32[128,768]{1,0:T(8,128)S(1)} collective-permute-done((f32[128,768]{1,0:T(8,128)S(1)}, f32[128,768]{1,0:T(8,128)S(1)}, u32[]{:S(2)}, u32[]{:S(2)}) %collective-permute-start.13) | collective-permute-done | bytes 393248 | tf_op jit(solution)/shard_map/ppermute | solution.py:591
  55.4 14.2 %collective-permute-done.15 = f32[128,768]{1,0:T(8,128)S(1)} collective-permute-done((f32[128,768]{1,0:T(8,128)S(1)}, f32[128,768]{1,0:T(8,128)S(1)}, u32[]{:S(2)}, u32[]{:S(2)}) %collective-permute-start.15) | collective-permute-done | bytes 393248 | tf_op jit(solution)/shard_map/ppermute | solution.py:591
  71.6 14.5 %collective-permute-done.17.r1 = f32[128,768]{1,0:T(8,128)S(1)} collective-permute-done((f32[128,768]{1,0:T(8,128)S(1)}, f32[128,768]{1,0:T(8,128)S(1)}, u32[]{:S(2)}, u32[]{:S(2)}) %collective-permute-start.17) | collective-permute-done | bytes 393248 | tf_op jit(solution)/shard_map/ppermute | solution.py:591
  90.8 6.7 %collective-permute-done.18.r3 = f32[128,768]{1,0:T(8,128)S(1)} collective-permute-done((f32[128,768]{1,0:T(8,128)S(1)}, f32[128,768]{1,0:T(8,128)S(1)}, u32[]{:S(2)}, u32[]{:S(2)}) %collective-permute-start.18) | collective-permute-done | bytes 393248 | tf_op jit(solution)/shard_map/ppermute | solution.py:591
  97.5 3.6 %shard_map.328 = (f32[128,768]{1,0:T(8,128)S(1)}, bf16[512,768]{1,0:T(8,128)(2,1)}, f32[48,768]{1,0:T(8,128)S(1)}, f32[16,768]{1,0:T(8,128)S(1)}, bf16[128,768]{...) custom-call(s32[2]{0:T(128)S(1)} %pad_add_fusion.ids.me, s32[1,16]{1,0:T(1,128)S(1)} %copy-done.6, ...), custom_call_target="tpu_custom_call" | custom-call | flops 301989888 | bytes 9437184 | tf_op jit(solution)/shard_map/pallas_call | solution.py:65
  101.1 6.5 %shard_map.329 = (f32[128,768]{1,0:T(8,128)S(1)}, f32[128,768]{1,0:T(8,128)S(1)}, f32[128,768]{1,0:T(8,128)S(1)}, f32[128,768]{1,0:T(8,128)S(1)}, f32[8,768]{1,0...) custom-call(s32[2]{0:T(128)S(1)} %pad_add_fusion.ids.me, s32[1,16]{1,0:T(1,128)S(1)} %copy-done.6, ...), custom_call_target="tpu_custom_call" | custom-call | flops 2415919104 | bytes 14155776 | tf_op jit(solution)/shard_map/pallas_call | solution.py:65
  108.9 3.3 %collective-permute-done.20.theirs = f32[4,192,768]{2,1,0:T(8,128)S(1)} collective-permute-done((f32[4,192,768]{2,1,0:T(8,128)S(1)}, f32[4,192,768]{2,1,0:T(8,128)S(1)}, u32[]{:S(2)}, u32[]{:S(2)}) %collective-permute-start.20) | collective-permute-done | bytes 2359328 | tf_op jit(solution)/shard_map/ppermute | solution.py:595
  117.9 12.2 %collective-permute-done.21.near = f32[128,768]{1,0:T(8,128)S(1)} collective-permute-done((f32[128,768]{1,0:T(8,128)S(1)}, f32[128,768]{1,0:T(8,128)S(1)}, u32[]{:S(2)}, u32[]{:S(2)}) %collective-permute-start.21) | collective-permute-done | bytes 393248 | tf_op jit(solution)/shard_map/ppermute | solution.py:591
  130.1 4.3 %collective-permute-done.22.across = f32[128,768]{1,0:T(8,128)S(1)} collective-permute-done((f32[128,768]{1,0:T(8,128)S(1)}, f32[128,768]{1,0:T(8,128)S(1)}, u32[]{:S(2)}, u32[]{:S(2)}) %collective-permute-start.22) | collective-permute-done | bytes 393248 | tf_op jit(solution)/shard_map/ppermute | solution.py:591
  135.7 4.1 %collective-permute-start.27 = (f32[224,128]{1,0:T(8,128)S(1)}, f32[224,128]{1,0:T(8,128)S(1)}, u32[]{:S(2)}, u32[]{:S(2)}) collective-permute-start(f32[224,128]{1,0:T(8,128)S(1)} %get-tuple-element.243), channel_id=1, source_target_pairs={{0,3},{1,2},{2,1},{3,0},{4,7},{5,6},{6,5},{7,4},{8,11},{9,10},{10,... | collective-permute-start | bytes 344072 | tf_op jit(solution)/shard_map/ppermute | solution.py:591
  143.5 3.2 %collective-permute-done.26.e2 = f32[224,128]{1,0:T(8,128)S(1)} collective-permute-done((f32[224,128]{1,0:T(8,128)S(1)}, f32[224,128]{1,0:T(8,128)S(1)}, u32[]{:S(2)}, u32[]{:S(2)}) %collective-permute-start.26) | collective-permute-done | bytes 114720 | tf_op jit(solution)/shard_map/ppermute | solution.py:591
  146.7 3.5 %shard_map.333 = (f32[128,768]{1,0:T(8,128)S(1)}, f32[128,768]{1,0:T(8,128)S(1)}, f32[128,768]{1,0:T(8,128)S(1)}, f32[128,768]{1,0:T(8,128)S(1)}, bf16[512,576]{...) custom-call(f32[224,128]{1,0:T(8,128)S(1)} %get-tuple-element.244.e0, ...), custom_call_target="tpu_custom_call" | custom-call | flops 10000000000 | bytes 4718592 | tf_op jit(solution)/shard_map/pallas_call | solution.py:65
  158.3 5.0 %collective-permute-done.34.o3 = f32[24,768]{1,0:T(8,128)S(1)} collective-permute-done((f32[24,768]{1,0:T(8,128)S(1)}, f32[24,768]{1,0:T(8,128)S(1)}, u32[]{:S(2)}, u32[]{:S(2)}) %collective-permute-start.34) | collective-permute-done | bytes 73760 | tf_op jit(solution)/shard_map/ppermute | solution.py:595
  169.6 5.1 %collective-permute-done.38.o3 = f32[72,768]{1,0:T(8,128)S(1)} collective-permute-done((f32[72,768]{1,0:T(8,128)S(1)}, f32[72,768]{1,0:T(8,128)S(1)}, u32[]{:S(2)}, u32[]{:S(2)}) %collective-permute-start.38) | collective-permute-done | bytes 221216 | tf_op jit(solution)/shard_map/ppermute | solution.py:595
  174.7 10.3 %collective-permute-done.37.across = f32[128,768]{1,0:T(8,128)S(1)} collective-permute-done((f32[128,768]{1,0:T(8,128)S(1)}, f32[128,768]{1,0:T(8,128)S(1)}, u32[]{:S(2)}, u32[]{:S(2)}) %collective-permute-start.37) | collective-permute-done | bytes 393248 | tf_op jit(solution)/shard_map/ppermute | solution.py:591
  189.2 17.6 %collective-permute-done.41.across.r2 = f32[152,768]{1,0:T(8,128)S(1)} collective-permute-done((f32[152,768]{1,0:T(8,128)S(1)}, f32[152,768]{1,0:T(8,128)S(1)}, u32[]{:S(2)}, u32[]{:S(2)}) %collective-permute-start.41) | collective-permute-done | bytes 466976 | tf_op jit(solution)/shard_map/ppermute | solution.py:591
  211.2 5.8 %collective-permute-done.46.r3 = f32[128,768]{1,0:T(8,128)S(1)} collective-permute-done((f32[128,768]{1,0:T(8,128)S(1)}, f32[128,768]{1,0:T(8,128)S(1)}, u32[]{:S(2)}, u32[]{:S(2)}) %collective-permute-start.46) | collective-permute-done | bytes 393248 | tf_op jit(solution)/shard_map/ppermute | solution.py:591
  218.9 3.5 %shard_map.342 = (f32[768,768]{1,0:T(8,128)}, f32[768,768]{1,0:T(8,128)}, f32[1728,128]{1,0:T(8,128)}) custom-call(s32[2]{0:T(128)S(1)} %pad_add_fusion.ids.me, f32[960,768]{1,0:T(8,128)S(1)} %get-tuple-element.309.mine, f32[960,768]{1,0:T(8,128)S(1)} %collective-permute-done.45.theirs), custom_call_target="tpu_custom_call" | custom-call | bytes 9437184 | tf_op jit(solution)/shard_map/pallas_call | solution.py:65
  (166 shorter events, 70.9 us)
Async XLA Ops:
  12.8 19.0 %collective-permute-start.4 = (f32[768,128]{1,0:T(8,128)S(1)}, f32[768,128]{1,0:T(8,128)S(1)}, u32[]{:S(2)}, u32[]{:S(2)}) collective-permute-start(f32[768,128]{1,0:T(8,128)S(1)} %get-tuple-element.180.m0), channel_id=1, source_target_pairs={{0,1},{1,0},{2,3},{3,2},{4,5},{5,4},{6,7},{7,6},{8,9},{9,8},{10,11... | collective-permute-start | bytes 1179656 | tf_op jit(solution)/shard_map/ppermute | solution.py:591
  14.1 19.4 %collective-permute-start.3 = (f32[768,128]{1,0:T(8,128)S(1)}, f32[768,128]{1,0:T(8,128)S(1)}, u32[]{:S(2)}, u32[]{:S(2)}) collective-permute-start(f32[768,128]{1,0:T(8,128)S(1)} %get-tuple-element.180.m0), channel_id=1, source_target_pairs={{0,2},{1,3},{2,0},{3,1},{4,6},{5,7},{6,4},{7,5},{8,10},{9,11},{10,... | collective-permute-start | bytes 1179656 | tf_op jit(solution)/shard_map/ppermute | solution.py:591
  19.6 12.1 %collective-permute-start.6 = (f32[4,24,768]{2,1,0:T(8,128)S(1)}, f32[4,24,768]{2,1,0:T(8,128)S(1)}, u32[]{:S(2)}, u32[]{:S(2)}) collective-permute-start(f32[4,24,768]{2,1,0:T(8,128)S(1)} %pad_maximum_fusion.3.refs_0_), channel_id=1, source_target_pairs={{0,16},{4,20},{8,24},{12,28},{16,0},{20,4},{24,8},{28,12},{1,17},{... | collective-permute-start | bytes 884744 | tf_op jit(solution)/shard_map/ppermute | solution.py:595
  20.1 11.7 %collective-permute-start.5 = (f32[4,24,768]{2,1,0:T(8,128)S(1)}, f32[4,24,768]{2,1,0:T(8,128)S(1)}, u32[]{:S(2)}, u32[]{:S(2)}) collective-permute-start(f32[4,24,768]{2,1,0:T(8,128)S(1)} %pad_maximum_fusion.3.refs_0_), channel_id=1, source_target_pairs={{0,8},{4,12},{8,0},{12,4},{16,24},{20,28},{24,16},{28,20},{1,9},{5... | collective-permute-start | bytes 884744 | tf_op jit(solution)/shard_map/ppermute | solution.py:595
  53.8 15.8 %collective-permute-start.15 = (f32[128,768]{1,0:T(8,128)S(1)}, f32[128,768]{1,0:T(8,128)S(1)}, u32[]{:S(2)}, u32[]{:S(2)}) collective-permute-start(f32[128,768]{1,0:T(8,128)S(1)} %add.47), channel_id=1, source_target_pairs={{0,2},{1,3},{2,0},{3,1},{4,6},{5,7},{6,4},{7,5},{8,10},{9,11},{10,... | collective-permute-start | bytes 1179656 | tf_op jit(solution)/shard_map/ppermute | solution.py:591
  53.9 15.8 %collective-permute-start.14 = (f32[128,768]{1,0:T(8,128)S(1)}, f32[128,768]{1,0:T(8,128)S(1)}, u32[]{:S(2)}, u32[]{:S(2)}) collective-permute-start(f32[128,768]{1,0:T(8,128)S(1)} %get-tuple-element.200), channel_id=1, source_target_pairs={{0,1},{1,0},{2,3},{3,2},{4,5},{5,4},{6,7},{7,6},{8,9},{9,8},{10,11... | collective-permute-start | bytes 1179656 | tf_op jit(solution)/shard_map/ppermute | solution.py:591
  69.7 16.4 %collective-permute-start.17 = (f32[128,768]{1,0:T(8,128)S(1)}, f32[128,768]{1,0:T(8,128)S(1)}, u32[]{:S(2)}, u32[]{:S(2)}) collective-permute-start(f32[128,768]{1,0:T(8,128)S(1)} %add_add_fusion.r0), channel_id=1, source_target_pairs={{0,1},{1,0},{2,3},{3,2},{4,5},{5,4},{6,7},{7,6},{8,9},{9,8},{10,11... | collective-permute-start | bytes 1179656 | tf_op jit(solution)/shard_map/ppermute | solution.py:591
  70.4 18.8 %collective-permute-start.16 = (f32[128,768]{1,0:T(8,128)S(1)}, f32[128,768]{1,0:T(8,128)S(1)}, u32[]{:S(2)}, u32[]{:S(2)}) collective-permute-start(f32[128,768]{1,0:T(8,128)S(1)} %add_add_fusion.r0), channel_id=1, source_target_pairs={{0,2},{1,3},{2,0},{3,1},{4,6},{5,7},{6,4},{7,5},{8,10},{9,11},{10,... | collective-permute-start | bytes 1179656 | tf_op jit(solution)/shard_map/ppermute | solution.py:591
  112.2 17.9 %collective-permute-start.21 = (f32[128,768]{1,0:T(8,128)S(1)}, f32[128,768]{1,0:T(8,128)S(1)}, u32[]{:S(2)}, u32[]{:S(2)}) collective-permute-start(f32[128,768]{1,0:T(8,128)S(1)} %get-tuple-element.223), channel_id=1, source_target_pairs={{0,1},{1,0},{2,3},{3,2},{4,5},{5,4},{6,7},{7,6},{8,9},{9,8},{10,11... | collective-permute-start | bytes 1179656 | tf_op jit(solution)/shard_map/ppermute | solution.py:591
  114.2 20.2 %collective-permute-start.22 = (f32[128,768]{1,0:T(8,128)S(1)}, f32[128,768]{1,0:T(8,128)S(1)}, u32[]{:S(2)}, u32[]{:S(2)}) collective-permute-start(f32[128,768]{1,0:T(8,128)S(1)} %shard_map.330), channel_id=1, source_target_pairs={{0,2},{1,3},{2,0},{3,1},{4,6},{5,7},{6,4},{7,5},{8,10},{9,11},{10,... | collective-permute-start | bytes 1179656 | tf_op jit(solution)/shard_map/ppermute | solution.py:591
  115.0 20.3 %collective-permute-start.23 = (f32[192,768]{1,0:T(8,128)S(1)}, f32[192,768]{1,0:T(8,128)S(1)}, u32[]{:S(2)}, u32[]{:S(2)}) collective-permute-start(f32[192,768]{1,0:T(8,128)S(1)} %get-tuple-element.236), channel_id=1, source_target_pairs={{0,8},{4,12},{8,0},{12,4},{16,24},{20,28},{24,16},{28,20},{1,9},{5... | collective-permute-start | bytes 1769480 | tf_op jit(solution)/shard_map/ppermute | solution.py:595
  117.9 17.4 %collective-permute-start.24 = (f32[192,768]{1,0:T(8,128)S(1)}, f32[192,768]{1,0:T(8,128)S(1)}, u32[]{:S(2)}, u32[]{:S(2)}) collective-permute-start(f32[192,768]{1,0:T(8,128)S(1)} %get-tuple-element.237), channel_id=1, source_target_pairs={{0,16},{4,20},{8,24},{12,28},{16,0},{20,4},{24,8},{28,12},{1,17},{... | collective-permute-start | bytes 1769480 | tf_op jit(solution)/shard_map/ppermute | solution.py:595
  163.6 21.3 %collective-permute-start.36 = (f32[152,768]{1,0:T(8,128)S(1)}, f32[152,768]{1,0:T(8,128)S(1)}, u32[]{:S(2)}, u32[]{:S(2)}) collective-permute-start(f32[152,768]{1,0:T(8,128)S(1)} %get-tuple-element.285), channel_id=1, source_target_pairs={{0,1},{1,0},{2,3},{3,2},{4,5},{5,4},{6,7},{7,6},{8,9},{9,8},{10,11... | collective-permute-start | bytes 1400840 | tf_op jit(solution)/shard_map/ppermute | solution.py:591
  167.0 18.0 %collective-permute-start.37 = (f32[128,768]{1,0:T(8,128)S(1)}, f32[128,768]{1,0:T(8,128)S(1)}, u32[]{:S(2)}, u32[]{:S(2)}) collective-permute-start(f32[128,768]{1,0:T(8,128)S(1)} %get-tuple-element.286), channel_id=1, source_target_pairs={{0,2},{1,3},{2,0},{3,1},{4,6},{5,7},{6,4},{7,5},{8,10},{9,11},{10,... | collective-permute-start | bytes 1179656 | tf_op jit(solution)/shard_map/ppermute | solution.py:591
  167.5 17.6 %collective-permute-start.39 = (f32[200,768]{1,0:T(8,128)S(1)}, f32[200,768]{1,0:T(8,128)S(1)}, u32[]{:S(2)}, u32[]{:S(2)}) collective-permute-start(f32[200,768]{1,0:T(8,128)S(1)} %get-tuple-element.293), channel_id=1, source_target_pairs={{0,8},{4,12},{8,0},{12,4},{16,24},{20,28},{24,16},{28,20},{1,9},{5... | collective-permute-start | bytes 1843208 | tf_op jit(solution)/shard_map/ppermute | solution.py:595
  168.8 16.3 %collective-permute-start.40 = (f32[200,768]{1,0:T(8,128)S(1)}, f32[200,768]{1,0:T(8,128)S(1)}, u32[]{:S(2)}, u32[]{:S(2)}) collective-permute-start(f32[200,768]{1,0:T(8,128)S(1)} %get-tuple-element.294), channel_id=1, source_target_pairs={{0,16},{4,20},{8,24},{12,28},{16,0},{20,4},{24,8},{28,12},{1,17},{... | collective-permute-start | bytes 1843208 | tf_op jit(solution)/shard_map/ppermute | solution.py:595
  185.2 21.5 %collective-permute-start.41 = (f32[152,768]{1,0:T(8,128)S(1)}, f32[152,768]{1,0:T(8,128)S(1)}, u32[]{:S(2)}, u32[]{:S(2)}) collective-permute-start(f32[152,768]{1,0:T(8,128)S(1)} %get-tuple-element.299), channel_id=1, source_target_pairs={{0,2},{1,3},{2,0},{3,1},{4,6},{5,7},{6,4},{7,5},{8,10},{9,11},{10,... | collective-permute-start | bytes 1400840 | tf_op jit(solution)/shard_map/ppermute | solution.py:591
  186.0 20.8 %collective-permute-start.42 = (f32[152,768]{1,0:T(8,128)S(1)}, f32[152,768]{1,0:T(8,128)S(1)}, u32[]{:S(2)}, u32[]{:S(2)}) collective-permute-start(f32[152,768]{1,0:T(8,128)S(1)} %get-tuple-element.300.r0), channel_id=1, source_target_pairs={{0,1},{1,0},{2,3},{3,2},{4,5},{5,4},{6,7},{7,6},{8,9},{9,8},{10,11... | collective-permute-start | bytes 1400840 | tf_op jit(solution)/shard_map/ppermute | solution.py:591
  187.2 19.6 %collective-permute-start.44 = (f32[280,768]{1,0:T(8,128)S(1)}, f32[280,768]{1,0:T(8,128)S(1)}, u32[]{:S(2)}, u32[]{:S(2)}) collective-permute-start(f32[280,768]{1,0:T(8,128)S(1)} %pad_maximum_fusion.1), channel_id=1, source_target_pairs={{0,8},{4,12},{8,0},{12,4},{16,24},{20,28},{24,16},{28,20},{1,9},{5... | collective-permute-start | bytes 2580488 | tf_op jit(solution)/shard_map/ppermute | solution.py:595
  188.0 18.8 %collective-permute-start.43 = (f32[280,768]{1,0:T(8,128)S(1)}, f32[280,768]{1,0:T(8,128)S(1)}, u32[]{:S(2)}, u32[]{:S(2)}) collective-permute-start(f32[280,768]{1,0:T(8,128)S(1)} %pad_maximum_fusion), channel_id=1, source_target_pairs={{0,16},{4,20},{8,24},{12,28},{16,0},{20,4},{24,8},{28,12},{1,17},{... | collective-permute-start | bytes 2580488 | tf_op jit(solution)/shard_map/ppermute | solution.py:595
  207.6 11.3 %collective-permute-start.45 = (f32[960,768]{1,0:T(8,128)S(1)}, f32[960,768]{1,0:T(8,128)S(1)}, u32[]{:S(2)}, u32[]{:S(2)}) collective-permute-start(f32[960,768]{1,0:T(8,128)S(1)} %get-tuple-element.309.mine), channel_id=1, source_target_pairs={{0,4},{4,0},{8,12},{12,8},{16,20},{20,16},{24,28},{28,24},{1,5},{5... | collective-permute-start | bytes 8847368 | tf_op jit(solution)/shard_map/ppermute | solution.py:595
  207.7 14.6 %collective-permute-start.49 = (f32[104,768]{1,0:T(8,128)S(1)}, f32[104,768]{1,0:T(8,128)S(1)}, u32[]{:S(2)}, u32[]{:S(2)}) collective-permute-start(f32[104,768]{1,0:T(8,128)S(1)} %get-tuple-element.319.refs_0_), channel_id=1, source_target_pairs={{0,24},{4,28},{8,16},{12,20},{16,8},{20,12},{24,0},{28,4},{1,25},{... | collective-permute-start | bytes 958472 | tf_op jit(solution)/shard_map/ppermute | solution.py:595
  209.1 16.2 %collective-permute-start.48 = (f32[104,768]{1,0:T(8,128)S(1)}, f32[104,768]{1,0:T(8,128)S(1)}, u32[]{:S(2)}, u32[]{:S(2)}) collective-permute-start(f32[104,768]{1,0:T(8,128)S(1)} %get-tuple-element.319.refs_0_), channel_id=1, source_target_pairs={{0,16},{4,20},{8,24},{12,28},{16,0},{20,4},{24,8},{28,12},{1,17},{... | collective-permute-start | bytes 958472 | tf_op jit(solution)/shard_map/ppermute | solution.py:595
  210.0 15.4 %collective-permute-start.47 = (f32[104,768]{1,0:T(8,128)S(1)}, f32[104,768]{1,0:T(8,128)S(1)}, u32[]{:S(2)}, u32[]{:S(2)}) collective-permute-start(f32[104,768]{1,0:T(8,128)S(1)} %get-tuple-element.319.refs_0_), channel_id=1, source_target_pairs={{0,8},{4,12},{8,0},{12,4},{16,24},{20,28},{24,16},{28,20},{1,9},{5... | collective-permute-start | bytes 958472 | tf_op jit(solution)/shard_map/ppermute | solution.py:595
  (47 other events, 601.8 us)

commit v6 on v5

--- a/solution.py
+++ b/solution.py
@@ -222,7 +222,7 @@
     resid_own[...] = normed + b_down[...]
 
 
-def finish_chunk(seg, normal, inverse, gain, spread, out_grad, grad_of, w_down, w_up, low, up, part):
+def finish_chunk(seg, normal, inverse, gain, spread, out_grad, grad_of, w_down, w_up, low, up):
     slot_row = lax.broadcasted_iota(jnp.int32, (1, SENTS), 1)
     belongs = jnp.where(seg == slot_row, 1.0, 0.0)
     d_final = out_grad.astype(f32) + nn(belongs, spread, highest)
@@ -230,8 +230,8 @@
     low[...] = d_resid.astype(bf16)
     d_upper = nt(low[...], w_down[...]) * grad_of
     up[...] = d_upper.astype(bf16)
-    part[...] = nt(up[...], w_up[...])
-    return d_resid, [col_sum(d_final), col_sum(d_final * normal), col_sum(d_resid), col_sum(d_upper)]
+    part = nt(up[...], w_up[...])
+    return part, d_resid, [col_sum(d_final), col_sum(d_final * normal), col_sum(d_resid), col_sum(d_upper)]
 
 
 def finish_rows(block, seg, gain, shift, normal_out, inverse_out, low_out):
@@ -292,7 +292,7 @@
     pools[2 * SENTS :, rest:] = jnp.zeros((SENTS, width - rest), f32)
     spread = pooled_grad[...] / denom
     spread_out[...] = spread
-    _, sums = finish_chunk(
+    part[...], _, sums = finish_chunk(
         seg_col[3 * rows :],
         normal_ref[...],
         inverse_ref[:, :1],
@@ -304,7 +304,6 @@
         w_up,
         low,
         up,
-        part,
     )
     for n in range(4):
         side[n : n + 1, :] = sums[n]
@@ -315,33 +314,30 @@
     ins, outs, (resid_low, upper_low, held) = refs[:8], refs[8:-3], refs[-3:]
     normal_ref, inverse_ref, spread, low3, up3, side3, normed_low, act = ins
     p0, p1, p2, d_own, side, even, odd = outs
-    parts = (p0, p1, p2)
     me = ids[0]
     rows, width = p0.shape
     seg_col = segment_of(lens, row_places(me, (4 * rows, 1), 0, rows))
     resid_low[3 * rows :, :] = low3[...]
     upper_low[3 * rows :, :] = up3[...]
-    total = [side3[n : n + 1, :] for n in range(4)]
-    for j in (2, 1, 0):
-        at = slice(j * rows, (j + 1) * rows)
-        d_resid, sums = finish_chunk(
-            seg_col[at],
-            normal_ref[at, :],
-            inverse_ref[at, :1],
-            g_ffn[...],
-            spread[...],
-            out_grad[chunk(me, j, rows), :],
-            grad_of[at, :],
-            w_down,
-            w_up,
-            resid_low.at[at, :],
-            upper_low.at[at, :],
-            parts[j],
-        )
-        total = [a + b for a, b in zip(total, sums)]
-    d_own[...] = d_resid
+    at = slice(0, 3 * rows)
+    part, d_resid, sums = finish_chunk(
+        seg_col[at],
+        normal_ref[...],
+        inverse_ref[:, :1],
+        g_ffn[...],
+        spread[...],
+        jnp.concatenate([out_grad[chunk(me, j, rows), :] for j in range(3)]),
+        grad_of[at, :],
+        w_down,
+        w_up,
+        resid_low.at[at, :],
+        upper_low.at[at, :],
+    )
+    for j, out in enumerate((p0, p1, p2)):
+        out[...] = part[j * rows : (j + 1) * rows, :]
+    d_own[...] = d_resid[:rows, :]
     for n in range(4):
-        side[n : n + 1, :] = total[n]
+        side[n : n + 1, :] = side3[n : n + 1, :] + sums[n]
     side[4:, :] = jnp.zeros((4, width), f32)
     held[:width, :] = tn(normed_low[...], upper_low[...])
     held[width:, :] = tn(act[...], resid_low[...])
@@ -414,9 +410,9 @@
         d_query = nn(d_scores[...], k[:, lane])
         bias[0:1, lane] = col_sum(d_query)
         grads[:, lane] = d_query.astype(bf16)
-        d_key = tn(d_scores[...], q[:, lane])
+        d_key = tn(q[:, lane], d_scores[...]).T
         grads[:, cols + h * HDIM : cols + (h + 1) * HDIM] = d_key.astype(bf16)
-        d_value = tn(probs[h], d_mixed[:, lane])
+        d_value = tn(d_mixed[:, lane], probs[h]).T
         bias[1:2, lane] = col_sum(d_value)
         grads[:, 2 * cols + h * HDIM : 2 * cols + (h + 1) * HDIM] = d_value.astype(bf16)
     bias[2:, :] = jnp.zeros((6, cols), f32)

time: 231 us -> 230 us (level)
  no operation moved by 1% of the time
where the time goes in v6:
time: 230 us
  waiting for transfers between devices  139 us (60%)
  starting transfers between devices  49.2 us (21%)
  Pallas kernels  38.5 us (17%)
    ppermute x24, waiting for transfers between devices, swap(): return lax.ppermute(block, 'tensor', swaps[k])  105 us
    pallas_call x23, Pallas kernels, call(): pl.pallas_call(body, out_shape=outs, in_specs=specs, out_specs=jax.tree.m...  38.5 us
    ppermute x30, waiting for transfers between devices, swap_dp(): return lax.ppermute(block, 'dp', [(i, i ^ k) for i in range(n_dp)])  33.7 us
    ppermute x24, starting transfers between devices, swap(): return lax.ppermute(block, 'tensor', swaps[k])  25.4 us
    ppermute x30, starting transfers between devices, swap_dp(): return lax.ppermute(block, 'dp', [(i, i ^ k) for i in range(n_dp)])  23.8 us
  transfers between devices with their start and end apart: 54, of which 33 were waited for; matrix products, arithmetic and copies ran while one was open for 0% of the time, Pallas kernels for 14%

profile of v6, /device:TPU:0, one launch (start us, length us, event | category | flops | bytes accessed | tf_op | source)
XLA Modules:
  0.0 229.8 jit_solution(5707166094460667451)
XLA Ops:
  1.5 5.1 %collective-permute-start.2 = (f32[24,768]{1,0:T(8,128)S(1)}, f32[24,768]{1,0:T(8,128)S(1)}, u32[]{:S(2)}, u32[]{:S(2)}) collective-permute-start(f32[24,768]{1,0:T(8,128)S(1)} %dynamic-slice_convert_fusion), channel_id=1, source_target_pairs={{0,3},{1,2},{2,1},{3,0},{4,7},{5,6},{6,5},{7,4},{8,11},{9,10},{10,... | collective-permute-start | bytes 221192 | tf_op jit(solution)/shard_map/ppermute | solution.py:587
  7.3 5.3 %shard_map.322 = (bf16[512,768]{1,0:T(8,128)(2,1)S(1)}, bf16[512,192]{1,0:T(8,128)(2,1)S(1)}, bf16[512,192]{1,0:T(8,128)(2,1)S(1)}, bf16[512,192]{1,0:T(8,128)(2...) custom-call(s32[2]{0:T(128)S(1)} %pad_add_fusion.ids.me, s32[1,16]{1,0:T(1,128)} %lens.5, ...), custom_call_target="tpu_custom_call" | custom-call | flops 654311424 | bytes 4030464 | tf_op jit(solution)/shard_map/pallas_call | solution.py:65
  20.6 7.3 %collective-permute-done.7.refs_6_ = f32[4,24,768]{2,1,0:T(8,128)S(1)} collective-permute-done((f32[4,24,768]{2,1,0:T(8,128)S(1)}, f32[4,24,768]{2,1,0:T(8,128)S(1)}, u32[]{:S(2)}, u32[]{:S(2)}) %collective-permute-start.7) | collective-permute-done | bytes 294944 | tf_op jit(solution)/shard_map/ppermute | solution.py:591
  27.9 3.7 %collective-permute-done.6.refs_4_ = f32[4,24,768]{2,1,0:T(8,128)S(1)} collective-permute-done((f32[4,24,768]{2,1,0:T(8,128)S(1)}, f32[4,24,768]{2,1,0:T(8,128)S(1)}, u32[]{:S(2)}, u32[]{:S(2)}) %collective-permute-start.6) | collective-permute-done | bytes 294944 | tf_op jit(solution)/shard_map/ppermute | solution.py:591
  37.5 5.2 %collective-permute-done.8.m3 = f32[768,128]{1,0:T(8,128)S(1)} collective-permute-done((f32[768,128]{1,0:T(8,128)S(1)}, f32[768,128]{1,0:T(8,128)S(1)}, u32[]{:S(2)}, u32[]{:S(2)}) %collective-permute-start.8) | collective-permute-done | bytes 393248 | tf_op jit(solution)/shard_map/ppermute | solution.py:587
  44.8 4.1 %shard_map.325 = (f32[128,768]{1,0:T(8,128)S(1)}, f32[128,768]{1,0:T(8,128)S(1)}, f32[128,768]{1,0:T(8,128)S(1)}, bf16[512,768]{1,0:T(8,128)(2,1)S(1)}, f32[512,...) custom-call(bf16[512,768]{1,0:T(8,128)(2,1)S(1)} %get-tuple-element., ...), custom_call_target="tpu_custom_call" | custom-call | flops 1358954496 | bytes 8257536 | tf_op jit(solution)/shard_map/pallas_call | solution.py:65
  49.5 4.2 %collective-permute-done.13 = f32[128,768]{1,0:T(8,128)S(1)} collective-permute-done((f32[128,768]{1,0:T(8,128)S(1)}, f32[128,768]{1,0:T(8,128)S(1)}, u32[]{:S(2)}, u32[]{:S(2)}) %collective-permute-start.13) | collective-permute-done | bytes 393248 | tf_op jit(solution)/shard_map/ppermute | solution.py:587
  55.4 14.2 %collective-permute-done.15 = f32[128,768]{1,0:T(8,128)S(1)} collective-permute-done((f32[128,768]{1,0:T(8,128)S(1)}, f32[128,768]{1,0:T(8,128)S(1)}, u32[]{:S(2)}, u32[]{:S(2)}) %collective-permute-start.15) | collective-permute-done | bytes 393248 | tf_op jit(solution)/shard_map/ppermute | solution.py:587
  71.6 14.5 %collective-permute-done.17.r1 = f32[128,768]{1,0:T(8,128)S(1)} collective-permute-done((f32[128,768]{1,0:T(8,128)S(1)}, f32[128,768]{1,0:T(8,128)S(1)}, u32[]{:S(2)}, u32[]{:S(2)}) %collective-permute-start.17) | collective-permute-done | bytes 393248 | tf_op jit(solution)/shard_map/ppermute | solution.py:587
  90.8 6.7 %collective-permute-done.18.r3 = f32[128,768]{1,0:T(8,128)S(1)} collective-permute-done((f32[128,768]{1,0:T(8,128)S(1)}, f32[128,768]{1,0:T(8,128)S(1)}, u32[]{:S(2)}, u32[]{:S(2)}) %collective-permute-start.18) | collective-permute-done | bytes 393248 | tf_op jit(solution)/shard_map/ppermute | solution.py:587
  97.5 3.6 %shard_map.328 = (f32[128,768]{1,0:T(8,128)S(1)}, bf16[512,768]{1,0:T(8,128)(2,1)}, f32[48,768]{1,0:T(8,128)S(1)}, f32[16,768]{1,0:T(8,128)S(1)}, bf16[128,768]{...) custom-call(s32[2]{0:T(128)S(1)} %pad_add_fusion.ids.me, s32[1,16]{1,0:T(1,128)S(1)} %copy-done.6, ...), custom_call_target="tpu_custom_call" | custom-call | flops 301989888 | bytes 9437184 | tf_op jit(solution)/shard_map/pallas_call | solution.py:65
  101.1 5.6 %shard_map.329 = (f32[128,768]{1,0:T(8,128)S(1)}, f32[128,768]{1,0:T(8,128)S(1)}, f32[128,768]{1,0:T(8,128)S(1)}, f32[128,768]{1,0:T(8,128)S(1)}, f32[8,768]{1,0...) custom-call(s32[2]{0:T(128)S(1)} %pad_add_fusion.ids.me, s32[1,16]{1,0:T(1,128)S(1)} %copy-done.6, ...), custom_call_target="tpu_custom_call" | custom-call | flops 2415919104 | bytes 14155776 | tf_op jit(solution)/shard_map/pallas_call | solution.py:65
  117.0 12.2 %collective-permute-done.21.near = f32[128,768]{1,0:T(8,128)S(1)} collective-permute-done((f32[128,768]{1,0:T(8,128)S(1)}, f32[128,768]{1,0:T(8,128)S(1)}, u32[]{:S(2)}, u32[]{:S(2)}) %collective-permute-start.21) | collective-permute-done | bytes 393248 | tf_op jit(solution)/shard_map/ppermute | solution.py:587
  129.2 4.3 %collective-permute-done.22.across = f32[128,768]{1,0:T(8,128)S(1)} collective-permute-done((f32[128,768]{1,0:T(8,128)S(1)}, f32[128,768]{1,0:T(8,128)S(1)}, u32[]{:S(2)}, u32[]{:S(2)}) %collective-permute-start.22) | collective-permute-done | bytes 393248 | tf_op jit(solution)/shard_map/ppermute | solution.py:587
  134.9 4.1 %collective-permute-start.27 = (f32[224,128]{1,0:T(8,128)S(1)}, f32[224,128]{1,0:T(8,128)S(1)}, u32[]{:S(2)}, u32[]{:S(2)}) collective-permute-start(f32[224,128]{1,0:T(8,128)S(1)} %get-tuple-element.243), channel_id=1, source_target_pairs={{0,3},{1,2},{2,1},{3,0},{4,7},{5,6},{6,5},{7,4},{8,11},{9,10},{10,... | collective-permute-start | bytes 344072 | tf_op jit(solution)/shard_map/ppermute | solution.py:587
  142.6 3.2 %collective-permute-done.26.e2 = f32[224,128]{1,0:T(8,128)S(1)} collective-permute-done((f32[224,128]{1,0:T(8,128)S(1)}, f32[224,128]{1,0:T(8,128)S(1)}, u32[]{:S(2)}, u32[]{:S(2)}) %collective-permute-start.26) | collective-permute-done | bytes 114720 | tf_op jit(solution)/shard_map/ppermute | solution.py:587
  145.8 3.3 %shard_map.333 = (f32[128,768]{1,0:T(8,128)S(1)}, f32[128,768]{1,0:T(8,128)S(1)}, f32[128,768]{1,0:T(8,128)S(1)}, f32[128,768]{1,0:T(8,128)S(1)}, bf16[512,576]{...) custom-call(f32[224,128]{1,0:T(8,128)S(1)} %get-tuple-element.244.e0, ...), custom_call_target="tpu_custom_call" | custom-call | flops 10000000000 | bytes 4718592 | tf_op jit(solution)/shard_map/pallas_call | solution.py:65
  157.4 5.0 %collective-permute-done.34.o3 = f32[24,768]{1,0:T(8,128)S(1)} collective-permute-done((f32[24,768]{1,0:T(8,128)S(1)}, f32[24,768]{1,0:T(8,128)S(1)}, u32[]{:S(2)}, u32[]{:S(2)}) %collective-permute-start.34) | collective-permute-done | bytes 73760 | tf_op jit(solution)/shard_map/ppermute | solution.py:591
  168.5 5.2 %collective-permute-done.38.o3 = f32[72,768]{1,0:T(8,128)S(1)} collective-permute-done((f32[72,768]{1,0:T(8,128)S(1)}, f32[72,768]{1,0:T(8,128)S(1)}, u32[]{:S(2)}, u32[]{:S(2)}) %collective-permute-start.38) | collective-permute-done | bytes 221216 | tf_op jit(solution)/shard_map/ppermute | solution.py:591
  173.8 10.3 %collective-permute-done.37.across = f32[128,768]{1,0:T(8,128)S(1)} collective-permute-done((f32[128,768]{1,0:T(8,128)S(1)}, f32[128,768]{1,0:T(8,128)S(1)}, u32[]{:S(2)}, u32[]{:S(2)}) %collective-permute-start.37) | collective-permute-done | bytes 393248 | tf_op jit(solution)/shard_map/ppermute | solution.py:587
  188.3 17.6 %collective-permute-done.41.across.r2 = f32[152,768]{1,0:T(8,128)S(1)} collective-permute-done((f32[152,768]{1,0:T(8,128)S(1)}, f32[152,768]{1,0:T(8,128)S(1)}, u32[]{:S(2)}, u32[]{:S(2)}) %collective-permute-start.41) | collective-permute-done | bytes 466976 | tf_op jit(solution)/shard_map/ppermute | solution.py:587
  210.4 5.7 %collective-permute-done.46.r3 = f32[128,768]{1,0:T(8,128)S(1)} collective-permute-done((f32[128,768]{1,0:T(8,128)S(1)}, f32[128,768]{1,0:T(8,128)S(1)}, u32[]{:S(2)}, u32[]{:S(2)}) %collective-permute-start.46) | collective-permute-done | bytes 393248 | tf_op jit(solution)/shard_map/ppermute | solution.py:587
  217.9 3.5 %shard_map.342 = (f32[768,768]{1,0:T(8,128)}, f32[768,768]{1,0:T(8,128)}, f32[1728,128]{1,0:T(8,128)}) custom-call(s32[2]{0:T(128)S(1)} %pad_add_fusion.ids.me, f32[960,768]{1,0:T(8,128)S(1)} %get-tuple-element.309.mine, f32[960,768]{1,0:T(8,128)S(1)} %collective-permute-done.45.theirs), custom_call_target="tpu_custom_call" | custom-call | bytes 9437184 | tf_op jit(solution)/shard_map/pallas_call | solution.py:65
  221.4 3.2 %collective-permute-done.48.refs_4_ = f32[104,768]{1,0:T(8,128)S(1)} collective-permute-done((f32[104,768]{1,0:T(8,128)S(1)}, f32[104,768]{1,0:T(8,128)S(1)}, u32[]{:S(2)}, u32[]{:S(2)}) %collective-permute-start.48) | collective-permute-done | bytes 319520 | tf_op jit(solution)/shard_map/ppermute | solution.py:591
  (166 shorter events, 71.2 us)
Async XLA Ops:
  12.8 19.0 %collective-permute-start.4 = (f32[768,128]{1,0:T(8,128)S(1)}, f32[768,128]{1,0:T(8,128)S(1)}, u32[]{:S(2)}, u32[]{:S(2)}) collective-permute-start(f32[768,128]{1,0:T(8,128)S(1)} %get-tuple-element.180.m0), channel_id=1, source_target_pairs={{0,1},{1,0},{2,3},{3,2},{4,5},{5,4},{6,7},{7,6},{8,9},{9,8},{10,11... | collective-permute-start | bytes 1179656 | tf_op jit(solution)/shard_map/ppermute | solution.py:587
  14.1 19.4 %collective-permute-start.3 = (f32[768,128]{1,0:T(8,128)S(1)}, f32[768,128]{1,0:T(8,128)S(1)}, u32[]{:S(2)}, u32[]{:S(2)}) collective-permute-start(f32[768,128]{1,0:T(8,128)S(1)} %get-tuple-element.180.m0), channel_id=1, source_target_pairs={{0,2},{1,3},{2,0},{3,1},{4,6},{5,7},{6,4},{7,5},{8,10},{9,11},{10,... | collective-permute-start | bytes 1179656 | tf_op jit(solution)/shard_map/ppermute | solution.py:587
  19.6 12.1 %collective-permute-start.6 = (f32[4,24,768]{2,1,0:T(8,128)S(1)}, f32[4,24,768]{2,1,0:T(8,128)S(1)}, u32[]{:S(2)}, u32[]{:S(2)}) collective-permute-start(f32[4,24,768]{2,1,0:T(8,128)S(1)} %pad_maximum_fusion.3.refs_0_), channel_id=1, source_target_pairs={{0,16},{4,20},{8,24},{12,28},{16,0},{20,4},{24,8},{28,12},{1,17},{... | collective-permute-start | bytes 884744 | tf_op jit(solution)/shard_map/ppermute | solution.py:591
  20.1 11.7 %collective-permute-start.5 = (f32[4,24,768]{2,1,0:T(8,128)S(1)}, f32[4,24,768]{2,1,0:T(8,128)S(1)}, u32[]{:S(2)}, u32[]{:S(2)}) collective-permute-start(f32[4,24,768]{2,1,0:T(8,128)S(1)} %pad_maximum_fusion.3.refs_0_), channel_id=1, source_target_pairs={{0,8},{4,12},{8,0},{12,4},{16,24},{20,28},{24,16},{28,20},{1,9},{5... | collective-permute-start | bytes 884744 | tf_op jit(solution)/shard_map/ppermute | solution.py:591
  53.8 15.8 %collective-permute-start.15 = (f32[128,768]{1,0:T(8,128)S(1)}, f32[128,768]{1,0:T(8,128)S(1)}, u32[]{:S(2)}, u32[]{:S(2)}) collective-permute-start(f32[128,768]{1,0:T(8,128)S(1)} %add.47), channel_id=1, source_target_pairs={{0,2},{1,3},{2,0},{3,1},{4,6},{5,7},{6,4},{7,5},{8,10},{9,11},{10,... | collective-permute-start | bytes 1179656 | tf_op jit(solution)/shard_map/ppermute | solution.py:587
  53.9 15.8 %collective-permute-start.14 = (f32[128,768]{1,0:T(8,128)S(1)}, f32[128,768]{1,0:T(8,128)S(1)}, u32[]{:S(2)}, u32[]{:S(2)}) collective-permute-start(f32[128,768]{1,0:T(8,128)S(1)} %get-tuple-element.200), channel_id=1, source_target_pairs={{0,1},{1,0},{2,3},{3,2},{4,5},{5,4},{6,7},{7,6},{8,9},{9,8},{10,11... | collective-permute-start | bytes 1179656 | tf_op jit(solution)/shard_map/ppermute | solution.py:587
  69.7 16.4 %collective-permute-start.17 = (f32[128,768]{1,0:T(8,128)S(1)}, f32[128,768]{1,0:T(8,128)S(1)}, u32[]{:S(2)}, u32[]{:S(2)}) collective-permute-start(f32[128,768]{1,0:T(8,128)S(1)} %add_add_fusion.r0), channel_id=1, source_target_pairs={{0,1},{1,0},{2,3},{3,2},{4,5},{5,4},{6,7},{7,6},{8,9},{9,8},{10,11... | collective-permute-start | bytes 1179656 | tf_op jit(solution)/shard_map/ppermute | solution.py:587
  70.4 18.8 %collective-permute-start.16 = (f32[128,768]{1,0:T(8,128)S(1)}, f32[128,768]{1,0:T(8,128)S(1)}, u32[]{:S(2)}, u32[]{:S(2)}) collective-permute-start(f32[128,768]{1,0:T(8,128)S(1)} %add_add_fusion.r0), channel_id=1, source_target_pairs={{0,2},{1,3},{2,0},{3,1},{4,6},{5,7},{6,4},{7,5},{8,10},{9,11},{10,... | collective-permute-start | bytes 1179656 | tf_op jit(solution)/shard_map/ppermute | solution.py:587
  111.3 17.9 %collective-permute-start.21 = (f32[128,768]{1,0:T(8,128)S(1)}, f32[128,768]{1,0:T(8,128)S(1)}, u32[]{:S(2)}, u32[]{:S(2)}) collective-permute-start(f32[128,768]{1,0:T(8,128)S(1)} %get-tuple-element.223), channel_id=1, source_target_pairs={{0,1},{1,0},{2,3},{3,2},{4,5},{5,4},{6,7},{7,6},{8,9},{9,8},{10,11... | collective-permute-start | bytes 1179656 | tf_op jit(solution)/shard_map/ppermute | solution.py:587
  113.3 20.2 %collective-permute-start.22 = (f32[128,768]{1,0:T(8,128)S(1)}, f32[128,768]{1,0:T(8,128)S(1)}, u32[]{:S(2)}, u32[]{:S(2)}) collective-permute-start(f32[128,768]{1,0:T(8,128)S(1)} %shard_map.330), channel_id=1, source_target_pairs={{0,2},{1,3},{2,0},{3,1},{4,6},{5,7},{6,4},{7,5},{8,10},{9,11},{10,... | collective-permute-start | bytes 1179656 | tf_op jit(solution)/shard_map/ppermute | solution.py:587
  114.1 20.3 %collective-permute-start.23 = (f32[192,768]{1,0:T(8,128)S(1)}, f32[192,768]{1,0:T(8,128)S(1)}, u32[]{:S(2)}, u32[]{:S(2)}) collective-permute-start(f32[192,768]{1,0:T(8,128)S(1)} %get-tuple-element.236), channel_id=1, source_target_pairs={{0,8},{4,12},{8,0},{12,4},{16,24},{20,28},{24,16},{28,20},{1,9},{5... | collective-permute-start | bytes 1769480 | tf_op jit(solution)/shard_map/ppermute | solution.py:591
  117.0 17.4 %collective-permute-start.24 = (f32[192,768]{1,0:T(8,128)S(1)}, f32[192,768]{1,0:T(8,128)S(1)}, u32[]{:S(2)}, u32[]{:S(2)}) collective-permute-start(f32[192,768]{1,0:T(8,128)S(1)} %get-tuple-element.237), channel_id=1, source_target_pairs={{0,16},{4,20},{8,24},{12,28},{16,0},{20,4},{24,8},{28,12},{1,17},{... | collective-permute-start | bytes 1769480 | tf_op jit(solution)/shard_map/ppermute | solution.py:591
  134.5 11.3 %collective-permute-start.26 = (f32[224,128]{1,0:T(8,128)S(1)}, f32[224,128]{1,0:T(8,128)S(1)}, u32[]{:S(2)}, u32[]{:S(2)}) collective-permute-start(f32[224,128]{1,0:T(8,128)S(1)} %get-tuple-element.242), channel_id=1, source_target_pairs={{0,2},{1,3},{2,0},{3,1},{4,6},{5,7},{6,4},{7,5},{8,10},{9,11},{10,... | collective-permute-start | bytes 344072 | tf_op jit(solution)/shard_map/ppermute | solution.py:587
  162.8 21.3 %collective-permute-start.36 = (f32[152,768]{1,0:T(8,128)S(1)}, f32[152,768]{1,0:T(8,128)S(1)}, u32[]{:S(2)}, u32[]{:S(2)}) collective-permute-start(f32[152,768]{1,0:T(8,128)S(1)} %get-tuple-element.285), channel_id=1, source_target_pairs={{0,1},{1,0},{2,3},{3,2},{4,5},{5,4},{6,7},{7,6},{8,9},{9,8},{10,11... | collective-permute-start | bytes 1400840 | tf_op jit(solution)/shard_map/ppermute | solution.py:587
  166.1 18.0 %collective-permute-start.37 = (f32[128,768]{1,0:T(8,128)S(1)}, f32[128,768]{1,0:T(8,128)S(1)}, u32[]{:S(2)}, u32[]{:S(2)}) collective-permute-start(f32[128,768]{1,0:T(8,128)S(1)} %get-tuple-element.286), channel_id=1, source_target_pairs={{0,2},{1,3},{2,0},{3,1},{4,6},{5,7},{6,4},{7,5},{8,10},{9,11},{10,... | collective-permute-start | bytes 1179656 | tf_op jit(solution)/shard_map/ppermute | solution.py:587
  166.4 17.8 %collective-permute-start.39 = (f32[200,768]{1,0:T(8,128)S(1)}, f32[200,768]{1,0:T(8,128)S(1)}, u32[]{:S(2)}, u32[]{:S(2)}) collective-permute-start(f32[200,768]{1,0:T(8,128)S(1)} %get-tuple-element.293), channel_id=1, source_target_pairs={{0,8},{4,12},{8,0},{12,4},{16,24},{20,28},{24,16},{28,20},{1,9},{5... | collective-permute-start | bytes 1843208 | tf_op jit(solution)/shard_map/ppermute | solution.py:591
  168.0 16.3 %collective-permute-start.40 = (f32[200,768]{1,0:T(8,128)S(1)}, f32[200,768]{1,0:T(8,128)S(1)}, u32[]{:S(2)}, u32[]{:S(2)}) collective-permute-start(f32[200,768]{1,0:T(8,128)S(1)} %get-tuple-element.294), channel_id=1, source_target_pairs={{0,16},{4,20},{8,24},{12,28},{16,0},{20,4},{24,8},{28,12},{1,17},{... | collective-permute-start | bytes 1843208 | tf_op jit(solution)/shard_map/ppermute | solution.py:591
  184.3 21.5 %collective-permute-start.41 = (f32[152,768]{1,0:T(8,128)S(1)}, f32[152,768]{1,0:T(8,128)S(1)}, u32[]{:S(2)}, u32[]{:S(2)}) collective-permute-start(f32[152,768]{1,0:T(8,128)S(1)} %get-tuple-element.299), channel_id=1, source_target_pairs={{0,2},{1,3},{2,0},{3,1},{4,6},{5,7},{6,4},{7,5},{8,10},{9,11},{10,... | collective-permute-start | bytes 1400840 | tf_op jit(solution)/shard_map/ppermute | solution.py:587
  185.0 20.8 %collective-permute-start.42 = (f32[152,768]{1,0:T(8,128)S(1)}, f32[152,768]{1,0:T(8,128)S(1)}, u32[]{:S(2)}, u32[]{:S(2)}) collective-permute-start(f32[152,768]{1,0:T(8,128)S(1)} %get-tuple-element.300.r0), channel_id=1, source_target_pairs={{0,1},{1,0},{2,3},{3,2},{4,5},{5,4},{6,7},{7,6},{8,9},{9,8},{10,11... | collective-permute-start | bytes 1400840 | tf_op jit(solution)/shard_map/ppermute | solution.py:587
  186.3 19.6 %collective-permute-start.44 = (f32[280,768]{1,0:T(8,128)S(1)}, f32[280,768]{1,0:T(8,128)S(1)}, u32[]{:S(2)}, u32[]{:S(2)}) collective-permute-start(f32[280,768]{1,0:T(8,128)S(1)} %pad_maximum_fusion.1), channel_id=1, source_target_pairs={{0,8},{4,12},{8,0},{12,4},{16,24},{20,28},{24,16},{28,20},{1,9},{5... | collective-permute-start | bytes 2580488 | tf_op jit(solution)/shard_map/ppermute | solution.py:591
  187.1 18.8 %collective-permute-start.43 = (f32[280,768]{1,0:T(8,128)S(1)}, f32[280,768]{1,0:T(8,128)S(1)}, u32[]{:S(2)}, u32[]{:S(2)}) collective-permute-start(f32[280,768]{1,0:T(8,128)S(1)} %pad_maximum_fusion), channel_id=1, source_target_pairs={{0,16},{4,20},{8,24},{12,28},{16,0},{20,4},{24,8},{28,12},{1,17},{... | collective-permute-start | bytes 2580488 | tf_op jit(solution)/shard_map/ppermute | solution.py:591
  206.9 14.5 %collective-permute-start.49 = (f32[104,768]{1,0:T(8,128)S(1)}, f32[104,768]{1,0:T(8,128)S(1)}, u32[]{:S(2)}, u32[]{:S(2)}) collective-permute-start(f32[104,768]{1,0:T(8,128)S(1)} %get-tuple-element.319.refs_0_), channel_id=1, source_target_pairs={{0,24},{4,28},{8,16},{12,20},{16,8},{20,12},{24,0},{28,4},{1,25},{... | collective-permute-start | bytes 958472 | tf_op jit(solution)/shard_map/ppermute | solution.py:591
  208.3 16.2 %collective-permute-start.48 = (f32[104,768]{1,0:T(8,128)S(1)}, f32[104,768]{1,0:T(8,128)S(1)}, u32[]{:S(2)}, u32[]{:S(2)}) collective-permute-start(f32[104,768]{1,0:T(8,128)S(1)} %get-tuple-element.319.refs_0_), channel_id=1, source_target_pairs={{0,16},{4,20},{8,24},{12,28},{16,0},{20,4},{24,8},{28,12},{1,17},{... | collective-permute-start | bytes 958472 | tf_op jit(solution)/shard_map/ppermute | solution.py:591
  209.1 15.5 %collective-permute-start.47 = (f32[104,768]{1,0:T(8,128)S(1)}, f32[104,768]{1,0:T(8,128)S(1)}, u32[]{:S(2)}, u32[]{:S(2)}) collective-permute-start(f32[104,768]{1,0:T(8,128)S(1)} %get-tuple-element.319.refs_0_), channel_id=1, source_target_pairs={{0,8},{4,12},{8,0},{12,4},{16,24},{20,28},{24,16},{28,20},{1,9},{5... | collective-permute-start | bytes 958472 | tf_op jit(solution)/shard_map/ppermute | solution.py:591
  (47 other events, 601.8 us)

commit v7 on v6

--- a/solution.py
+++ b/solution.py
@@ -817,7 +817,7 @@
             [shape(rows, width)] * 4
             + [shape(slots, 3 * cols, kind=bf16), shape(8, cols), shape(16, cols)],
             [*d_mixed, probs, q, k, v, wq, wk, wv],
-            flops=10 * order,
+            flops=20 * order,
             moved=heads * slots * slots * 2 + 2 * slots * width * 4,
             scratch=[
                 pltpu.VMEM((slots, cols), bf16),

time: 230 us -> 229 us (level)
  waiting for transfers between devices: 139 us -> 133 us
  starting transfers between devices: 49.2 us -> 53.6 us
    ppermute x30, waiting for transfers between devices: 33.7 us -> 29.2 us  [swap_dp(): return lax.ppermute(block, 'dp', [(i, i ^ k) for i in range(n_dp)])]
    ppermute x24, starting transfers between devices: 25.4 us -> 29.3 us  [swap(): return lax.ppermute(block, 'tensor', swaps[k])]
  transfers between devices with their start and end apart: 54 -> 54, of which waited for: 33 -> 35; matrix products, arithmetic and copies ran while one was open for 0% -> 0% of each run, Pallas kernels for 14% -> 14%
where the time goes in v7:
time: 229 us
  waiting for transfers between devices  133 us (58%)
  starting transfers between devices  53.6 us (23%)
  Pallas kernels  38.6 us (17%)
    ppermute x24, waiting for transfers between devices, swap(): return lax.ppermute(block, 'tensor', swaps[k])  104 us
    pallas_call x23, Pallas kernels, call(): pl.pallas_call(body, out_shape=outs, in_specs=specs, out_specs=jax.tree.m...  38.6 us
    ppermute x24, starting transfers between devices, swap(): return lax.ppermute(block, 'tensor', swaps[k])  29.3 us
    ppermute x30, waiting for transfers between devices, swap_dp(): return lax.ppermute(block, 'dp', [(i, i ^ k) for i in range(n_dp)])  29.2 us
    ppermute x30, starting transfers between devices, swap_dp(): return lax.ppermute(block, 'dp', [(i, i ^ k) for i in range(n_dp)])  24.3 us
  transfers between devices with their start and end apart: 54, of which 35 were waited for; matrix products, arithmetic and copies ran while one was open for 0% of the time, Pallas kernels for 14%

profile of v7, /device:TPU:0, one launch (start us, length us, event | category | flops | bytes accessed | tf_op | source)
XLA Modules:
  0.0 228.6 jit_solution(16219153612226415014)
XLA Ops:
  1.5 5.1 %collective-permute-start.2 = (f32[24,768]{1,0:T(8,128)S(1)}, f32[24,768]{1,0:T(8,128)S(1)}, u32[]{:S(2)}, u32[]{:S(2)}) collective-permute-start(f32[24,768]{1,0:T(8,128)S(1)} %dynamic-slice_convert_fusion), channel_id=1, source_target_pairs={{0,3},{1,2},{2,1},{3,0},{4,7},{5,6},{6,5},{7,4},{8,11},{9,10},{10,... | collective-permute-start | bytes 221192 | tf_op jit(solution)/shard_map/ppermute | solution.py:587
  7.3 5.3 %shard_map.322 = (bf16[512,768]{1,0:T(8,128)(2,1)S(1)}, bf16[512,192]{1,0:T(8,128)(2,1)S(1)}, bf16[512,192]{1,0:T(8,128)(2,1)S(1)}, bf16[512,192]{1,0:T(8,128)(2...) custom-call(s32[2]{0:T(128)S(1)} %pad_add_fusion.ids.me, s32[1,16]{1,0:T(1,128)} %lens.5, ...), custom_call_target="tpu_custom_call" | custom-call | flops 654311424 | bytes 4030464 | tf_op jit(solution)/shard_map/pallas_call | solution.py:65
  20.6 7.3 %collective-permute-done.7.refs_6_ = f32[4,24,768]{2,1,0:T(8,128)S(1)} collective-permute-done((f32[4,24,768]{2,1,0:T(8,128)S(1)}, f32[4,24,768]{2,1,0:T(8,128)S(1)}, u32[]{:S(2)}, u32[]{:S(2)}) %collective-permute-start.7) | collective-permute-done | bytes 294944 | tf_op jit(solution)/shard_map/ppermute | solution.py:591
  27.9 3.7 %collective-permute-done.6.refs_4_ = f32[4,24,768]{2,1,0:T(8,128)S(1)} collective-permute-done((f32[4,24,768]{2,1,0:T(8,128)S(1)}, f32[4,24,768]{2,1,0:T(8,128)S(1)}, u32[]{:S(2)}, u32[]{:S(2)}) %collective-permute-start.6) | collective-permute-done | bytes 294944 | tf_op jit(solution)/shard_map/ppermute | solution.py:591
  37.5 5.2 %collective-permute-done.8.m3 = f32[768,128]{1,0:T(8,128)S(1)} collective-permute-done((f32[768,128]{1,0:T(8,128)S(1)}, f32[768,128]{1,0:T(8,128)S(1)}, u32[]{:S(2)}, u32[]{:S(2)}) %collective-permute-start.8) | collective-permute-done | bytes 393248 | tf_op jit(solution)/shard_map/ppermute | solution.py:587
  44.8 4.1 %shard_map.325 = (f32[128,768]{1,0:T(8,128)S(1)}, f32[128,768]{1,0:T(8,128)S(1)}, f32[128,768]{1,0:T(8,128)S(1)}, bf16[512,768]{1,0:T(8,128)(2,1)S(1)}, f32[512,...) custom-call(bf16[512,768]{1,0:T(8,128)(2,1)S(1)} %get-tuple-element., ...), custom_call_target="tpu_custom_call" | custom-call | flops 1358954496 | bytes 8257536 | tf_op jit(solution)/shard_map/pallas_call | solution.py:65
  49.5 4.2 %collective-permute-done.13 = f32[128,768]{1,0:T(8,128)S(1)} collective-permute-done((f32[128,768]{1,0:T(8,128)S(1)}, f32[128,768]{1,0:T(8,128)S(1)}, u32[]{:S(2)}, u32[]{:S(2)}) %collective-permute-start.13) | collective-permute-done | bytes 393248 | tf_op jit(solution)/shard_map/ppermute | solution.py:587
  55.3 14.3 %collective-permute-done.15 = f32[128,768]{1,0:T(8,128)S(1)} collective-permute-done((f32[128,768]{1,0:T(8,128)S(1)}, f32[128,768]{1,0:T(8,128)S(1)}, u32[]{:S(2)}, u32[]{:S(2)}) %collective-permute-start.15) | collective-permute-done | bytes 393248 | tf_op jit(solution)/shard_map/ppermute | solution.py:587
  71.6 14.5 %collective-permute-done.17.r1 = f32[128,768]{1,0:T(8,128)S(1)} collective-permute-done((f32[128,768]{1,0:T(8,128)S(1)}, f32[128,768]{1,0:T(8,128)S(1)}, u32[]{:S(2)}, u32[]{:S(2)}) %collective-permute-start.17) | collective-permute-done | bytes 393248 | tf_op jit(solution)/shard_map/ppermute | solution.py:587
  86.1 3.1 %collective-permute-done.16.r2 = f32[128,768]{1,0:T(8,128)S(1)} collective-permute-done((f32[128,768]{1,0:T(8,128)S(1)}, f32[128,768]{1,0:T(8,128)S(1)}, u32[]{:S(2)}, u32[]{:S(2)}) %collective-permute-start.16) | collective-permute-done | bytes 393248 | tf_op jit(solution)/shard_map/ppermute | solution.py:587
  90.8 6.7 %collective-permute-done.18.r3 = f32[128,768]{1,0:T(8,128)S(1)} collective-permute-done((f32[128,768]{1,0:T(8,128)S(1)}, f32[128,768]{1,0:T(8,128)S(1)}, u32[]{:S(2)}, u32[]{:S(2)}) %collective-permute-start.18) | collective-permute-done | bytes 393248 | tf_op jit(solution)/shard_map/ppermute | solution.py:587
  97.5 3.6 %shard_map.328 = (f32[128,768]{1,0:T(8,128)S(1)}, bf16[512,768]{1,0:T(8,128)(2,1)}, f32[48,768]{1,0:T(8,128)S(1)}, f32[16,768]{1,0:T(8,128)S(1)}, bf16[128,768]{...) custom-call(s32[2]{0:T(128)S(1)} %pad_add_fusion.ids.me, s32[1,16]{1,0:T(1,128)S(1)} %copy-done.6, ...), custom_call_target="tpu_custom_call" | custom-call | flops 301989888 | bytes 9437184 | tf_op jit(solution)/shard_map/pallas_call | solution.py:65
  101.1 5.6 %shard_map.329 = (f32[128,768]{1,0:T(8,128)S(1)}, f32[128,768]{1,0:T(8,128)S(1)}, f32[128,768]{1,0:T(8,128)S(1)}, f32[128,768]{1,0:T(8,128)S(1)}, f32[8,768]{1,0...) custom-call(s32[2]{0:T(128)S(1)} %pad_add_fusion.ids.me, s32[1,16]{1,0:T(1,128)S(1)} %copy-done.6, ...), custom_call_target="tpu_custom_call" | custom-call | flops 2415919104 | bytes 14155776 | tf_op jit(solution)/shard_map/pallas_call | solution.py:65
  114.0 3.0 %collective-permute-start.23 = (f32[192,768]{1,0:T(8,128)S(1)}, f32[192,768]{1,0:T(8,128)S(1)}, u32[]{:S(2)}, u32[]{:S(2)}) collective-permute-start(f32[192,768]{1,0:T(8,128)S(1)} %get-tuple-element.236), channel_id=1, source_target_pairs={{0,8},{4,12},{8,0},{12,4},{16,24},{20,28},{24,16},{28,20},{1,9},{5... | collective-permute-start | bytes 1769480 | tf_op jit(solution)/shard_map/ppermute | solution.py:591
  117.0 12.2 %collective-permute-done.21.near = f32[128,768]{1,0:T(8,128)S(1)} collective-permute-done((f32[128,768]{1,0:T(8,128)S(1)}, f32[128,768]{1,0:T(8,128)S(1)}, u32[]{:S(2)}, u32[]{:S(2)}) %collective-permute-start.21) | collective-permute-done | bytes 393248 | tf_op jit(solution)/shard_map/ppermute | solution.py:587
  129.2 4.3 %collective-permute-done.22.across = f32[128,768]{1,0:T(8,128)S(1)} collective-permute-done((f32[128,768]{1,0:T(8,128)S(1)}, f32[128,768]{1,0:T(8,128)S(1)}, u32[]{:S(2)}, u32[]{:S(2)}) %collective-permute-start.22) | collective-permute-done | bytes 393248 | tf_op jit(solution)/shard_map/ppermute | solution.py:587
  134.8 4.1 %collective-permute-start.27 = (f32[224,128]{1,0:T(8,128)S(1)}, f32[224,128]{1,0:T(8,128)S(1)}, u32[]{:S(2)}, u32[]{:S(2)}) collective-permute-start(f32[224,128]{1,0:T(8,128)S(1)} %get-tuple-element.243), channel_id=1, source_target_pairs={{0,3},{1,2},{2,1},{3,0},{4,7},{5,6},{6,5},{7,4},{8,11},{9,10},{10,... | collective-permute-start | bytes 344072 | tf_op jit(solution)/shard_map/ppermute | solution.py:587
  142.6 3.2 %collective-permute-done.26.e2 = f32[224,128]{1,0:T(8,128)S(1)} collective-permute-done((f32[224,128]{1,0:T(8,128)S(1)}, f32[224,128]{1,0:T(8,128)S(1)}, u32[]{:S(2)}, u32[]{:S(2)}) %collective-permute-start.26) | collective-permute-done | bytes 114720 | tf_op jit(solution)/shard_map/ppermute | solution.py:587
  145.8 3.3 %shard_map.333 = (f32[128,768]{1,0:T(8,128)S(1)}, f32[128,768]{1,0:T(8,128)S(1)}, f32[128,768]{1,0:T(8,128)S(1)}, f32[128,768]{1,0:T(8,128)S(1)}, bf16[512,576]{...) custom-call(f32[224,128]{1,0:T(8,128)S(1)} %get-tuple-element.244.e0, ...), custom_call_target="tpu_custom_call" | custom-call | flops 20000000000 | bytes 4718592 | tf_op jit(solution)/shard_map/pallas_call | solution.py:65
  156.6 4.8 %collective-permute-done.34.o3 = f32[24,768]{1,0:T(8,128)S(1)} collective-permute-done((f32[24,768]{1,0:T(8,128)S(1)}, f32[24,768]{1,0:T(8,128)S(1)}, u32[]{:S(2)}, u32[]{:S(2)}) %collective-permute-start.34) | collective-permute-done | bytes 73760 | tf_op jit(solution)/shard_map/ppermute | solution.py:591
  171.4 9.5 %collective-permute-done.37.across = f32[128,768]{1,0:T(8,128)S(1)} collective-permute-done((f32[128,768]{1,0:T(8,128)S(1)}, f32[128,768]{1,0:T(8,128)S(1)}, u32[]{:S(2)}, u32[]{:S(2)}) %collective-permute-start.37) | collective-permute-done | bytes 393248 | tf_op jit(solution)/shard_map/ppermute | solution.py:587
  187.5 16.7 %collective-permute-done.41.across.r2 = f32[152,768]{1,0:T(8,128)S(1)} collective-permute-done((f32[152,768]{1,0:T(8,128)S(1)}, f32[152,768]{1,0:T(8,128)S(1)}, u32[]{:S(2)}, u32[]{:S(2)}) %collective-permute-start.41) | collective-permute-done | bytes 466976 | tf_op jit(solution)/shard_map/ppermute | solution.py:587
  209.2 6.1 %collective-permute-done.46.r3 = f32[128,768]{1,0:T(8,128)S(1)} collective-permute-done((f32[128,768]{1,0:T(8,128)S(1)}, f32[128,768]{1,0:T(8,128)S(1)}, u32[]{:S(2)}, u32[]{:S(2)}) %collective-permute-start.46) | collective-permute-done | bytes 393248 | tf_op jit(solution)/shard_map/ppermute | solution.py:587
  217.1 3.5 %shard_map.342 = (f32[768,768]{1,0:T(8,128)}, f32[768,768]{1,0:T(8,128)}, f32[1728,128]{1,0:T(8,128)}) custom-call(s32[2]{0:T(128)S(1)} %pad_add_fusion.ids.me, f32[960,768]{1,0:T(8,128)S(1)} %get-tuple-element.309.mine, f32[960,768]{1,0:T(8,128)S(1)} %collective-permute-done.45.theirs), custom_call_target="tpu_custom_call" | custom-call | bytes 9437184 | tf_op jit(solution)/shard_map/pallas_call | solution.py:65
  (166 shorter events, 73.9 us)
Async XLA Ops:
  12.8 19.0 %collective-permute-start.4 = (f32[768,128]{1,0:T(8,128)S(1)}, f32[768,128]{1,0:T(8,128)S(1)}, u32[]{:S(2)}, u32[]{:S(2)}) collective-permute-start(f32[768,128]{1,0:T(8,128)S(1)} %get-tuple-element.180.m0), channel_id=1, source_target_pairs={{0,1},{1,0},{2,3},{3,2},{4,5},{5,4},{6,7},{7,6},{8,9},{9,8},{10,11... | collective-permute-start | bytes 1179656 | tf_op jit(solution)/shard_map/ppermute | solution.py:587
  14.1 19.4 %collective-permute-start.3 = (f32[768,128]{1,0:T(8,128)S(1)}, f32[768,128]{1,0:T(8,128)S(1)}, u32[]{:S(2)}, u32[]{:S(2)}) collective-permute-start(f32[768,128]{1,0:T(8,128)S(1)} %get-tuple-element.180.m0), channel_id=1, source_target_pairs={{0,2},{1,3},{2,0},{3,1},{4,6},{5,7},{6,4},{7,5},{8,10},{9,11},{10,... | collective-permute-start | bytes 1179656 | tf_op jit(solution)/shard_map/ppermute | solution.py:587
  19.6 12.1 %collective-permute-start.6 = (f32[4,24,768]{2,1,0:T(8,128)S(1)}, f32[4,24,768]{2,1,0:T(8,128)S(1)}, u32[]{:S(2)}, u32[]{:S(2)}) collective-permute-start(f32[4,24,768]{2,1,0:T(8,128)S(1)} %pad_maximum_fusion.3.refs_0_), channel_id=1, source_target_pairs={{0,16},{4,20},{8,24},{12,28},{16,0},{20,4},{24,8},{28,12},{1,17},{... | collective-permute-start | bytes 884744 | tf_op jit(solution)/shard_map/ppermute | solution.py:591
  20.1 11.7 %collective-permute-start.5 = (f32[4,24,768]{2,1,0:T(8,128)S(1)}, f32[4,24,768]{2,1,0:T(8,128)S(1)}, u32[]{:S(2)}, u32[]{:S(2)}) collective-permute-start(f32[4,24,768]{2,1,0:T(8,128)S(1)} %pad_maximum_fusion.3.refs_0_), channel_id=1, source_target_pairs={{0,8},{4,12},{8,0},{12,4},{16,24},{20,28},{24,16},{28,20},{1,9},{5... | collective-permute-start | bytes 884744 | tf_op jit(solution)/shard_map/ppermute | solution.py:591
  53.8 15.8 %collective-permute-start.15 = (f32[128,768]{1,0:T(8,128)S(1)}, f32[128,768]{1,0:T(8,128)S(1)}, u32[]{:S(2)}, u32[]{:S(2)}) collective-permute-start(f32[128,768]{1,0:T(8,128)S(1)} %add.47), channel_id=1, source_target_pairs={{0,2},{1,3},{2,0},{3,1},{4,6},{5,7},{6,4},{7,5},{8,10},{9,11},{10,... | collective-permute-start | bytes 1179656 | tf_op jit(solution)/shard_map/ppermute | solution.py:587
  53.9 15.7 %collective-permute-start.14 = (f32[128,768]{1,0:T(8,128)S(1)}, f32[128,768]{1,0:T(8,128)S(1)}, u32[]{:S(2)}, u32[]{:S(2)}) collective-permute-start(f32[128,768]{1,0:T(8,128)S(1)} %get-tuple-element.200), channel_id=1, source_target_pairs={{0,1},{1,0},{2,3},{3,2},{4,5},{5,4},{6,7},{7,6},{8,9},{9,8},{10,11... | collective-permute-start | bytes 1179656 | tf_op jit(solution)/shard_map/ppermute | solution.py:587
  69.7 16.3 %collective-permute-start.17 = (f32[128,768]{1,0:T(8,128)S(1)}, f32[128,768]{1,0:T(8,128)S(1)}, u32[]{:S(2)}, u32[]{:S(2)}) collective-permute-start(f32[128,768]{1,0:T(8,128)S(1)} %add_add_fusion.r0), channel_id=1, source_target_pairs={{0,1},{1,0},{2,3},{3,2},{4,5},{5,4},{6,7},{7,6},{8,9},{9,8},{10,11... | collective-permute-start | bytes 1179656 | tf_op jit(solution)/shard_map/ppermute | solution.py:587
  70.4 18.7 %collective-permute-start.16 = (f32[128,768]{1,0:T(8,128)S(1)}, f32[128,768]{1,0:T(8,128)S(1)}, u32[]{:S(2)}, u32[]{:S(2)}) collective-permute-start(f32[128,768]{1,0:T(8,128)S(1)} %add_add_fusion.r0), channel_id=1, source_target_pairs={{0,2},{1,3},{2,0},{3,1},{4,6},{5,7},{6,4},{7,5},{8,10},{9,11},{10,... | collective-permute-start | bytes 1179656 | tf_op jit(solution)/shard_map/ppermute | solution.py:587
  111.3 17.9 %collective-permute-start.21 = (f32[128,768]{1,0:T(8,128)S(1)}, f32[128,768]{1,0:T(8,128)S(1)}, u32[]{:S(2)}, u32[]{:S(2)}) collective-permute-start(f32[128,768]{1,0:T(8,128)S(1)} %get-tuple-element.223), channel_id=1, source_target_pairs={{0,1},{1,0},{2,3},{3,2},{4,5},{5,4},{6,7},{7,6},{8,9},{9,8},{10,11... | collective-permute-start | bytes 1179656 | tf_op jit(solution)/shard_map/ppermute | solution.py:587
  113.3 20.2 %collective-permute-start.22 = (f32[128,768]{1,0:T(8,128)S(1)}, f32[128,768]{1,0:T(8,128)S(1)}, u32[]{:S(2)}, u32[]{:S(2)}) collective-permute-start(f32[128,768]{1,0:T(8,128)S(1)} %shard_map.330), channel_id=1, source_target_pairs={{0,2},{1,3},{2,0},{3,1},{4,6},{5,7},{6,4},{7,5},{8,10},{9,11},{10,... | collective-permute-start | bytes 1179656 | tf_op jit(solution)/shard_map/ppermute | solution.py:587
  114.0 20.4 %collective-permute-start.23 = (f32[192,768]{1,0:T(8,128)S(1)}, f32[192,768]{1,0:T(8,128)S(1)}, u32[]{:S(2)}, u32[]{:S(2)}) collective-permute-start(f32[192,768]{1,0:T(8,128)S(1)} %get-tuple-element.236), channel_id=1, source_target_pairs={{0,8},{4,12},{8,0},{12,4},{16,24},{20,28},{24,16},{28,20},{1,9},{5... | collective-permute-start | bytes 1769480 | tf_op jit(solution)/shard_map/ppermute | solution.py:591
  117.0 17.4 %collective-permute-start.24 = (f32[192,768]{1,0:T(8,128)S(1)}, f32[192,768]{1,0:T(8,128)S(1)}, u32[]{:S(2)}, u32[]{:S(2)}) collective-permute-start(f32[192,768]{1,0:T(8,128)S(1)} %get-tuple-element.237), channel_id=1, source_target_pairs={{0,16},{4,20},{8,24},{12,28},{16,0},{20,4},{24,8},{28,12},{1,17},{... | collective-permute-start | bytes 1769480 | tf_op jit(solution)/shard_map/ppermute | solution.py:591
  149.2 12.5 %collective-permute-start.31 = (f32[128,768]{1,0:T(8,128)S(1)}, f32[128,768]{1,0:T(8,128)S(1)}, u32[]{:S(2)}, u32[]{:S(2)}) collective-permute-start(f32[128,768]{1,0:T(8,128)S(1)} %get-tuple-element.262), channel_id=1, source_target_pairs={{0,1},{1,0},{2,3},{3,2},{4,5},{5,4},{6,7},{7,6},{8,9},{9,8},{10,11... | collective-permute-start | bytes 1179656 | tf_op jit(solution)/shard_map/ppermute | solution.py:587
  161.8 19.2 %collective-permute-start.36 = (f32[152,768]{1,0:T(8,128)S(1)}, f32[152,768]{1,0:T(8,128)S(1)}, u32[]{:S(2)}, u32[]{:S(2)}) collective-permute-start(f32[152,768]{1,0:T(8,128)S(1)} %get-tuple-element.285), channel_id=1, source_target_pairs={{0,1},{1,0},{2,3},{3,2},{4,5},{5,4},{6,7},{7,6},{8,9},{9,8},{10,11... | collective-permute-start | bytes 1400840 | tf_op jit(solution)/shard_map/ppermute | solution.py:587
  163.7 17.3 %collective-permute-start.37 = (f32[128,768]{1,0:T(8,128)S(1)}, f32[128,768]{1,0:T(8,128)S(1)}, u32[]{:S(2)}, u32[]{:S(2)}) collective-permute-start(f32[128,768]{1,0:T(8,128)S(1)} %get-tuple-element.286), channel_id=1, source_target_pairs={{0,2},{1,3},{2,0},{3,1},{4,6},{5,7},{6,4},{7,5},{8,10},{9,11},{10,... | collective-permute-start | bytes 1179656 | tf_op jit(solution)/shard_map/ppermute | solution.py:587
  166.4 14.8 %collective-permute-start.39 = (f32[200,768]{1,0:T(8,128)S(1)}, f32[200,768]{1,0:T(8,128)S(1)}, u32[]{:S(2)}, u32[]{:S(2)}) collective-permute-start(f32[200,768]{1,0:T(8,128)S(1)} %get-tuple-element.293), channel_id=1, source_target_pairs={{0,8},{4,12},{8,0},{12,4},{16,24},{20,28},{24,16},{28,20},{1,9},{5... | collective-permute-start | bytes 1843208 | tf_op jit(solution)/shard_map/ppermute | solution.py:591
  166.9 15.4 %collective-permute-start.40 = (f32[200,768]{1,0:T(8,128)S(1)}, f32[200,768]{1,0:T(8,128)S(1)}, u32[]{:S(2)}, u32[]{:S(2)}) collective-permute-start(f32[200,768]{1,0:T(8,128)S(1)} %get-tuple-element.294), channel_id=1, source_target_pairs={{0,16},{4,20},{8,24},{12,28},{16,0},{20,4},{24,8},{28,12},{1,17},{... | collective-permute-start | bytes 1843208 | tf_op jit(solution)/shard_map/ppermute | solution.py:591
  182.4 21.8 %collective-permute-start.41 = (f32[152,768]{1,0:T(8,128)S(1)}, f32[152,768]{1,0:T(8,128)S(1)}, u32[]{:S(2)}, u32[]{:S(2)}) collective-permute-start(f32[152,768]{1,0:T(8,128)S(1)} %get-tuple-element.299), channel_id=1, source_target_pairs={{0,2},{1,3},{2,0},{3,1},{4,6},{5,7},{6,4},{7,5},{8,10},{9,11},{10,... | collective-permute-start | bytes 1400840 | tf_op jit(solution)/shard_map/ppermute | solution.py:587
  183.6 20.8 %collective-permute-start.42 = (f32[152,768]{1,0:T(8,128)S(1)}, f32[152,768]{1,0:T(8,128)S(1)}, u32[]{:S(2)}, u32[]{:S(2)}) collective-permute-start(f32[152,768]{1,0:T(8,128)S(1)} %get-tuple-element.300.r0), channel_id=1, source_target_pairs={{0,1},{1,0},{2,3},{3,2},{4,5},{5,4},{6,7},{7,6},{8,9},{9,8},{10,11... | collective-permute-start | bytes 1400840 | tf_op jit(solution)/shard_map/ppermute | solution.py:587
  185.3 19.1 %collective-permute-start.44 = (f32[280,768]{1,0:T(8,128)S(1)}, f32[280,768]{1,0:T(8,128)S(1)}, u32[]{:S(2)}, u32[]{:S(2)}) collective-permute-start(f32[280,768]{1,0:T(8,128)S(1)} %pad_maximum_fusion.1), channel_id=1, source_target_pairs={{0,8},{4,12},{8,0},{12,4},{16,24},{20,28},{24,16},{28,20},{1,9},{5... | collective-permute-start | bytes 2580488 | tf_op jit(solution)/shard_map/ppermute | solution.py:591
  185.9 18.7 %collective-permute-start.43 = (f32[280,768]{1,0:T(8,128)S(1)}, f32[280,768]{1,0:T(8,128)S(1)}, u32[]{:S(2)}, u32[]{:S(2)}) collective-permute-start(f32[280,768]{1,0:T(8,128)S(1)} %pad_maximum_fusion), channel_id=1, source_target_pairs={{0,16},{4,20},{8,24},{12,28},{16,0},{20,4},{24,8},{28,12},{1,17},{... | collective-permute-start | bytes 2580488 | tf_op jit(solution)/shard_map/ppermute | solution.py:591
  205.6 14.9 %collective-permute-start.49 = (f32[104,768]{1,0:T(8,128)S(1)}, f32[104,768]{1,0:T(8,128)S(1)}, u32[]{:S(2)}, u32[]{:S(2)}) collective-permute-start(f32[104,768]{1,0:T(8,128)S(1)} %get-tuple-element.319.refs_0_), channel_id=1, source_target_pairs={{0,24},{4,28},{8,16},{12,20},{16,8},{20,12},{24,0},{28,4},{1,25},{... | collective-permute-start | bytes 958472 | tf_op jit(solution)/shard_map/ppermute | solution.py:591
  207.1 16.2 %collective-permute-start.48 = (f32[104,768]{1,0:T(8,128)S(1)}, f32[104,768]{1,0:T(8,128)S(1)}, u32[]{:S(2)}, u32[]{:S(2)}) collective-permute-start(f32[104,768]{1,0:T(8,128)S(1)} %get-tuple-element.319.refs_0_), channel_id=1, source_target_pairs={{0,16},{4,20},{8,24},{12,28},{16,0},{20,4},{24,8},{28,12},{1,17},{... | collective-permute-start | bytes 958472 | tf_op jit(solution)/shard_map/ppermute | solution.py:591
  208.4 14.9 %collective-permute-start.47 = (f32[104,768]{1,0:T(8,128)S(1)}, f32[104,768]{1,0:T(8,128)S(1)}, u32[]{:S(2)}, u32[]{:S(2)}) collective-permute-start(f32[104,768]{1,0:T(8,128)S(1)} %get-tuple-element.319.refs_0_), channel_id=1, source_target_pairs={{0,8},{4,12},{8,0},{12,4},{16,24},{20,28},{24,16},{28,20},{1,9},{5... | collective-permute-start | bytes 958472 | tf_op jit(solution)/shard_map/ppermute | solution.py:591
  (47 other events, 596.7 us)
